TPU v7x, 512 devices: a whole 4x8x8 slice. The times are simulated.
512 devices in a mesh: gx: 16 (over z, core), gy: 8 (over y), gz: 4 (over x).
Axes of the slice: x: 4, y: 8, z: 8, core: 2. Of those that a mesh axis runs over, the one named last changes fastest.
Arguments:
- right_side: float32 [64, 16, 64, 512], P(None, 'gx', 'gy', 'gz'), may hold values from -180 to 180
- velocity: float32 [3, 16, 64, 512], P(None, 'gx', 'gy', 'gz'), may hold values from 0.1 to 1
- decay_rate: float32 [16, 64, 512], P('gx', 'gy', 'gz'), may hold values from 0.3 to 3
- perm_class: int32 [16, 64, 512], P('gx', 'gy', 'gz'), may hold values from 0 to 15
- conductivity: float32 [16], replicated, may hold values from 0.25 to 2.5
- well_cells: int32 [32], replicated, may hold values from 0 to 524287
- well_rate: float32 [32], replicated, may hold values from 4 to 16
Outputs:
- solution_field: float32 [64, 16, 64, 512], P(None, 'gx', 'gy', 'gz')
- residual: float32 [64, 16, 64, 512], P(None, 'gx', 'gy', 'gz')
Inputs may be any that keep to these rules, and one draw needn't show every extreme that they name: `well_cells`: flat index (x * 64 + y) * 512 + z of a cell; two wells may share a cell.
All inputs are finite; a program needn't handle non-finite values.
Results may differ from a plain program's by a relative error of at most 0.0015.
Values sent between devices are 32-bit elements; how exact they have to be, the bound alone decides.
No kernel may reach another device: no remote copies, remote signals or barrier semaphores. Data moves between devices by JAX's collectives and lax.ppermute only.
A program may use at most 64 MiB of HBM per device.

v0:
```python
import jax
import jax.numpy as jnp
from jax import lax
from jax.sharding import PartitionSpec as P

ITERS = 2


def padded_2(cells, sides, width):
    for axis, dim in sides:
        count = lax.axis_size(axis)
        ends = count - 1
        head = lax.slice_in_dim(cells, 0, width, axis=dim)
        tail = lax.slice_in_dim(cells, cells.shape[dim] - width, cells.shape[dim], axis=dim)
        cells = jnp.concatenate(
            [
                lax.ppermute(tail, axis, [(i, (i + 1) % count) for i in range(ends)]),
                cells,
                lax.ppermute(head, axis, [((i + 1) % count, i) for i in range(ends)]),
            ],
            axis=dim,
        )
    return cells


def gram_matrix(first_block, second_block):
    return jnp.einsum("aijk,bijk->ab", first_block, second_block, precision=lax.Precision.HIGHEST)


def combine(field, coefs):
    return jnp.einsum("ab,aijk->bijk", coefs, field, precision=lax.Precision.HIGHEST)


def solve_block(matrix, wanted):
    normal = jnp.dot(matrix.T, matrix, precision=lax.Precision.HIGHEST)
    target = jnp.dot(matrix.T, wanted, precision=lax.Precision.HIGHEST)
    factor = jnp.linalg.cholesky(normal)
    return jax.scipy.linalg.cho_solve((factor, True), target)


def face_terms(conduct, conduct_rim, velocity, decay_rate, well_sum):
    plus_faces = [
        0.5 * (conduct + conduct_rim[2:, 1:-1, 1:-1]),
        0.5 * (conduct + conduct_rim[1:-1, 2:, 1:-1]),
        0.5 * (conduct + conduct_rim[1:-1, 1:-1, 2:]),
    ]
    minus_faces = [
        0.5 * (conduct + conduct_rim[:-2, 1:-1, 1:-1]),
        0.5 * (conduct + conduct_rim[1:-1, :-2, 1:-1]),
        0.5 * (conduct + conduct_rim[1:-1, 1:-1, :-2]),
    ]
    diagonal_sum = decay_rate + well_sum
    for index in range(3):
        diagonal_sum = diagonal_sum + (velocity[index] + plus_faces[index] + minus_faces[index])
    return (diagonal_sum, plus_faces, minus_faces)


def apply_operator(field, padded, diagonal_sum, upper_coefs, lower_coefs):
    result = diagonal_sum * field
    result = result - (
        upper_coefs[0] * padded[:, 2:, 1:-1, 1:-1] + lower_coefs[0] * padded[:, :-2, 1:-1, 1:-1]
    )
    result = result - (
        upper_coefs[1] * padded[:, 1:-1, 2:, 1:-1] + lower_coefs[1] * padded[:, 1:-1, :-2, 1:-1]
    )
    result = result - (
        upper_coefs[2] * padded[:, 1:-1, 1:-1, 2:] + lower_coefs[2] * padded[:, 1:-1, 1:-1, :-2]
    )
    return result


def per_device(right_side, velocity, decay_rate, perm_class, conductivity, well_cells, well_rate):
    size_x, size_y, size_z = perm_class.shape
    classes = jnp.arange(conductivity.shape[0], dtype=jnp.int32)
    conduct = jnp.sum(
        jnp.where(
            perm_class[None] == classes[:, None, None, None], conductivity[:, None, None, None], 0.0
        ),
        axis=0,
    )
    whole_y = size_y * lax.axis_size("gy")
    whole_z = size_z * lax.axis_size("gz")
    x_index = lax.axis_index("gx") * size_x + jnp.arange(size_x, dtype=jnp.int32)
    y_index = lax.axis_index("gy") * size_y + jnp.arange(size_y, dtype=jnp.int32)
    z_index = lax.axis_index("gz") * size_z + jnp.arange(size_z, dtype=jnp.int32)
    flat_index = (x_index[:, None, None] * whole_y + y_index[None, :, None]) * whole_z + z_index[
        None, None, :
    ]
    matches = flat_index[None] == well_cells[:, None, None, None]
    well_sum = jnp.sum(jnp.where(matches, well_rate[:, None, None, None], 0.0), axis=0)
    conduct_rim = padded_2(conduct, (("gx", 0), ("gy", 1), ("gz", 2)), 1)
    diagonal_sum, plus_faces, minus_faces = face_terms(
        conduct, conduct_rim, velocity, decay_rate, well_sum
    )
    upper_coefs = [velocity[index] + plus_faces[index] for index in range(3)]

    def apply_block(field):
        padded = padded_2(field, (("gx", 1), ("gy", 2), ("gz", 3)), 1)
        return apply_operator(field, padded, diagonal_sum, upper_coefs, minus_faces)

    solution_field = jnp.zeros_like(right_side)
    residual = right_side
    direction = right_side
    for turn_index in range(ITERS):
        image_block = apply_block(direction)
        resid_gram, image_gram = lax.psum(
            (gram_matrix(right_side, residual), gram_matrix(right_side, image_block)),
            ("gx", "gy", "gz"),
        )
        alpha_coef = solve_block(image_gram, resid_gram)
        half_step = residual - combine(image_block, alpha_coef)
        second = apply_block(half_step)
        cross_sum, square, second_gram = lax.psum(
            (
                jnp.sum(second * half_step),
                jnp.sum(second * second),
                gram_matrix(right_side, second),
            ),
            ("gx", "gy", "gz"),
        )
        omega_scale = cross_sum / square
        solution_field = solution_field + combine(direction, alpha_coef) + omega_scale * half_step
        residual = half_step - omega_scale * second
        if turn_index + 1 < ITERS:
            beta_coef = solve_block(image_gram, -second_gram)
            direction = residual + combine(direction - omega_scale * image_block, beta_coef)
    return (solution_field, residual)


def solution(mesh):
    placed = (
        P(None, "gx", "gy", "gz"),
        P(None, "gx", "gy", "gz"),
        P("gx", "gy", "gz"),
        P("gx", "gy", "gz"),
        P(),
        P(),
        P(),
    )
    return jax.shard_map(
        per_device,
        mesh=mesh,
        in_specs=placed,
        out_specs=(P(None, "gx", "gy", "gz"), P(None, "gx", "gy", "gz")),
        check_vma=False,
    )
```

profile of v0, /device:TPU:1, one launch (start us, length us, event | category | flops | bytes accessed | tf_op | source)
XLA Modules:
  0.0 585.4 jit_solution(8652481037299657742)
XLA Ops:
  1.7 5.4 collective-permute-start.7
  7.1 4.7 collective-permute-start.6
  22.6 2.9 collective-permute-done.2
  27.4 4.6 collective-permute-start.5
  33.4 4.0 collective-permute-start.9
  51.0 108.8 %all-reduce.3 = (f32[64,64]{0,1:T(8,128)S(1)}, f32[64,64]{1,0:T(8,128)S(1)}) all-reduce(f32[64,64]{0,1:T(8,128)S(1)} %convolution_bitcast_fusion.12, f32[64,64]{1,0:T(8,128)S(1)} %copy-done.17), channel_id=1, replica_groups=mesh['gx'=16,'gy'=8,'gz'=4] {'gx','gy','gz'}, use_global_device_ids=true, to_apply=%region_2.3 | all-reduce | flops 8192 | bytes 65536 | tf_op jit(solution)/shard_map/psum | solution.py:106
  160.7 5.8 cholesky.44
  167.9 4.9 custom-call.9
  177.2 3.0 collective-permute-start.13
  184.8 4.0 collective-permute-start.15
  191.9 3.3 collective-permute-start.17
  197.2 2.8 collective-permute-done.16
  202.4 101.1 %all-reduce.2 = (f32[]{:T(128)}, f32[]{:T(128)}, f32[64,64]{0,1:T(8,128)S(1)}) all-reduce(f32[]{:T(128)} %get-tuple-element.13, f32[]{:T(128)} %get-tuple-element.12, f32[64,64]{0,1:T(8,128)S(1)} %convolution_bitcast_fusion.10), channel_id=1, replica_groups=mesh['gx'=16,'gy'=8,'gz'=4] {'gx','gy','gz'}, use_global_device_ids=true, to_apply=%region_7.10 | all-reduce | flops 4098 | bytes 32784 | tf_op jit(solution)/shard_map/psum | solution.py:113
  307.2 2.6 collective-permute-start.18
  309.8 3.2 collective-permute-start.19
  317.7 4.0 collective-permute-start.21
  324.7 3.7 collective-permute-start.23
  335.7 101.1 %all-reduce.1 = (f32[64,64]{0,1:T(8,128)S(1)}, f32[64,64]{0,1:T(8,128)S(1)}) all-reduce(f32[64,64]{0,1:T(8,128)S(1)} %convolution_bitcast_fusion.9, f32[64,64]{0,1:T(8,128)S(1)} %copy-done.18), channel_id=1, replica_groups=mesh['gx'=16,'gy'=8,'gz'=4] {'gx','gy','gz'}, use_global_device_ids=true, to_apply=%region_11.14 | all-reduce | flops 8192 | bytes 65536 | tf_op jit(solution)/shard_map/psum | solution.py:106
  437.2 5.8 cholesky.55
  444.4 4.9 custom-call.11
  453.0 3.2 collective-permute-start.25
  460.9 4.0 collective-permute-start.27
  469.4 3.7 collective-permute-start.29
  480.0 101.0 %all-reduce = (f32[]{:T(128)}, f32[]{:T(128)}) all-reduce(f32[]{:T(128)} %get-tuple-element.11, f32[]{:T(128)} %get-tuple-element.10), channel_id=1, replica_groups=mesh['gx'=16,'gy'=8,'gz'=4] {'gx','gy','gz'}, use_global_device_ids=true, to_apply=%region_14.17 | all-reduce | flops 2 | bytes 16 | tf_op jit(solution)/shard_map/psum | solution.py:113
  (181 shorter events, 88.9 us)
Async XLA Ops:
  1.7 30.3 %collective-permute-start.7 = (f32[64,1,8,128]{3,0,2,1:T(8,128)S(1)}, f32[64,1,8,128]{3,0,2,1:T(8,128)S(1)}, u32[]{:S(2)}, u32[]{:S(2)}) collective-permute-start(f32[64,1,8,128]{3,0,2,1:T(8,128)S(1)} %copy.59), channel_id=1, source_target_pairs={{0,32},{32,64},{64,96},{96,128},{128,160},{160,192},{192,224},{224... | collective-permute-start | bytes 786440 | tf_op jit(solution)/shard_map/ppermute | solution.py:17
  7.1 24.9 %collective-permute-start.6 = (f32[64,1,8,128]{3,0,2,1:T(8,128)S(1)}, f32[64,1,8,128]{3,0,2,1:T(8,128)S(1)}, u32[]{:S(2)}, u32[]{:S(2)}) collective-permute-start(f32[64,1,8,128]{3,0,2,1:T(8,128)S(1)} %copy.59), channel_id=1, source_target_pairs={{32,0},{64,32},{96,64},{128,96},{160,128},{192,160},{224,192},{256... | collective-permute-start | bytes 786440 | tf_op jit(solution)/shard_map/ppermute | solution.py:19
  11.9 5.4 collective-permute-start.1
  13.9 4.9 collective-permute-start
  26.1 18.6 %collective-permute-start.4 = (f32[3,10,1]{2,1,0:T(8,128)}, f32[3,10,1]{2,1,0:T(8,128)S(1)}, u32[]{:S(2)}, u32[]{:S(2)}) collective-permute-start(f32[3,10,1]{2,1,0:T(8,128)} %get-tuple-element.45), channel_id=1, source_target_pairs={{1,0},{2,1},{3,2},{5,4},{6,5},{7,6},{9,8},{10,9},{11,10},{13,12},{... | collective-permute-start | bytes 368 | tf_op jit(solution)/shard_map/ppermute | solution.py:19
  27.4 17.3 %collective-permute-start.5 = (f32[3,10,1]{2,1,0:T(8,128)}, f32[3,10,1]{2,1,0:T(8,128)}, u32[]{:S(2)}, u32[]{:S(2)}) collective-permute-start(f32[3,10,1]{2,1,0:T(8,128)} %get-tuple-element.44), channel_id=1, source_target_pairs={{0,1},{1,2},{2,3},{4,5},{5,6},{6,7},{8,9},{9,10},{10,11},{12,13},{... | collective-permute-start | bytes 368 | tf_op jit(solution)/shard_map/ppermute | solution.py:17
  32.1 6.1 %collective-permute-start.8 = (f32[64,3,1,128]{3,0,2,1:T(8,128)S(1)}, f32[64,3,1,128]{3,0,2,1:T(8,128)S(1)}, u32[]{:S(2)}, u32[]{:S(2)}) collective-permute-start(f32[64,3,1,128]{3,0,2,1:T(8,128)S(1)} %get-tuple-element.43), channel_id=1, source_target_pairs={{4,0},{8,4},{12,8},{16,12},{20,16},{24,20},{28,24},{5,1},{9,5},{13... | collective-permute-start | bytes 294920 | tf_op jit(solution)/shard_map/ppermute | solution.py:19
  33.4 5.6 collective-permute-start.9
  40.5 5.0 collective-permute-start.11
  174.6 7.7 %collective-permute-start.12 = (f32[64,1,8,128]{3,0,2,1:T(8,128)S(1)}, f32[64,1,8,128]{3,0,2,1:T(8,128)S(1)}, u32[]{:S(2)}, u32[]{:S(2)}) collective-permute-start(f32[64,1,8,128]{3,0,2,1:T(8,128)S(1)} %fusion.3), channel_id=1, source_target_pairs={{32,0},{64,32},{96,64},{128,96},{160,128},{192,160},{224,192},{256... | collective-permute-start | bytes 786440 | tf_op jit(solution)/shard_map/ppermute | solution.py:19
  177.2 6.3 %collective-permute-start.13 = (f32[64,1,8,128]{3,0,2,1:T(8,128)S(1)}, f32[64,1,8,128]{3,0,2,1:T(8,128)S(1)}, u32[]{:S(2)}, u32[]{:S(2)}) collective-permute-start(f32[64,1,8,128]{3,0,2,1:T(8,128)S(1)} %fusion.3), channel_id=1, source_target_pairs={{0,32},{32,64},{64,96},{96,128},{128,160},{160,192},{192,224},{224... | collective-permute-start | bytes 786440 | tf_op jit(solution)/shard_map/ppermute | solution.py:17
  183.5 5.4 collective-permute-start.14
  184.8 5.6 collective-permute-start.15
  191.9 5.0 collective-permute-start.17
  307.2 7.9 %collective-permute-start.18 = (f32[64,1,8,128]{3,0,2,1:T(8,128)S(1)}, f32[64,1,8,128]{3,0,2,1:T(8,128)S(1)}, u32[]{:S(2)}, u32[]{:S(2)}) collective-permute-start(f32[64,1,8,128]{3,0,2,1:T(8,128)S(1)} %fusion.4), channel_id=1, source_target_pairs={{32,0},{64,32},{96,64},{128,96},{160,128},{192,160},{224,192},{256... | collective-permute-start | bytes 786440 | tf_op jit(solution)/shard_map/ppermute | solution.py:19
  309.8 6.5 %collective-permute-start.19 = (f32[64,1,8,128]{3,0,2,1:T(8,128)S(1)}, f32[64,1,8,128]{3,0,2,1:T(8,128)S(1)}, u32[]{:S(2)}, u32[]{:S(2)}) collective-permute-start(f32[64,1,8,128]{3,0,2,1:T(8,128)S(1)} %fusion.4), channel_id=1, source_target_pairs={{0,32},{32,64},{64,96},{96,128},{128,160},{160,192},{192,224},{224... | collective-permute-start | bytes 786440 | tf_op jit(solution)/shard_map/ppermute | solution.py:17
  316.4 5.4 collective-permute-start.20
  317.7 5.6 collective-permute-start.21
  324.7 6.5 %collective-permute-start.23 = (f32[64,3,10,1]{0,3,2,1:T(1,128)S(1)}, f32[64,3,10,1]{0,3,2,1:T(1,128)S(1)}, u32[]{:S(2)}, u32[]{:S(2)}) collective-permute-start(f32[64,3,10,1]{0,3,2,1:T(1,128)S(1)} %copy.84), channel_id=1, source_target_pairs={{0,1},{1,2},{2,3},{4,5},{5,6},{6,7},{8,9},{9,10},{10,11},{12,13},{... | collective-permute-start | bytes 23048 | tf_op jit(solution)/shard_map/ppermute | solution.py:17
  450.4 7.9 %collective-permute-start.24 = (f32[64,1,8,128]{3,0,2,1:T(8,128)S(1)}, f32[64,1,8,128]{3,0,2,1:T(8,128)S(1)}, u32[]{:S(2)}, u32[]{:S(2)}) collective-permute-start(f32[64,1,8,128]{3,0,2,1:T(8,128)S(1)} %fusion.5), channel_id=1, source_target_pairs={{32,0},{64,32},{96,64},{128,96},{160,128},{192,160},{224,192},{256... | collective-permute-start | bytes 786440 | tf_op jit(solution)/shard_map/ppermute | solution.py:19
  453.0 6.5 %collective-permute-start.25 = (f32[64,1,8,128]{3,0,2,1:T(8,128)S(1)}, f32[64,1,8,128]{3,0,2,1:T(8,128)S(1)}, u32[]{:S(2)}, u32[]{:S(2)}) collective-permute-start(f32[64,1,8,128]{3,0,2,1:T(8,128)S(1)} %fusion.5), channel_id=1, source_target_pairs={{0,32},{32,64},{64,96},{96,128},{128,160},{160,192},{192,224},{224... | collective-permute-start | bytes 786440 | tf_op jit(solution)/shard_map/ppermute | solution.py:17
  459.6 5.5 collective-permute-start.26
  460.9 5.6 collective-permute-start.27
  469.4 6.4 %collective-permute-start.29 = (f32[64,3,10,1]{0,3,2,1:T(1,128)}, f32[64,3,10,1]{0,3,2,1:T(1,128)S(1)}, u32[]{:S(2)}, u32[]{:S(2)}) collective-permute-start(f32[64,3,10,1]{0,3,2,1:T(1,128)} %copy.93), channel_id=1, source_target_pairs={{0,1},{1,2},{2,3},{4,5},{5,6},{6,7},{8,9},{9,10},{10,11},{12,13},{... | collective-permute-start | bytes 23048 | tf_op jit(solution)/shard_map/ppermute | solution.py:17
  (34 other events, 107.6 us)
where the time goes:
time: 587 us; the launch traced here: 585 us
  blocking collectives  412 us (70%)
  starting transfers between devices  80.7 us (14%)
  other arithmetic  33.1 us (6%)
  waiting for transfers between devices  28.1 us (5%)
  local copies, waits for them, and re-layouts  18.5 us (3%)
  matrix products  8.9 us (2%)
    psum x2, blocking collectives, per_device(): lax.psum((gram_matrix(right_side, residual), gram_matrix(right_side, imag...  210 us
    psum x2, blocking collectives, per_device(): lax.psum((jnp.sum(second * half_step), jnp.sum(second * second), gram_mat...  202 us
    ppermute x15, starting transfers between devices, padded_2(): lax.ppermute(tail, axis, [(i, (i + 1) % count) for i in range(ends)])  52.8 us
    ppermute x15, starting transfers between devices, padded_2(): lax.ppermute(head, axis, [((i + 1) % count, i) for i in range(ends)])  27.9 us
    ppermute x15, waiting for transfers between devices, padded_2(): lax.ppermute(head, axis, [((i + 1) % count, i) for i in range(ends)])  19.2 us
    another operation x6, other arithmetic, solve_block(): factor = jnp.linalg.cholesky(normal)  13 us
  transfers between devices with their start and end apart: 30, of which 20 were waited for; matrix products, arithmetic and copies ran while one was open for 2% of the time, Pallas kernels for 0%

commit v1 on v0

v1 whole, which is shorter than its diff:
```python
import functools

import jax
import jax.numpy as jnp
from jax import lax
from jax.experimental import pallas as pl
from jax.experimental.pallas import tpu as pltpu
from jax.sharding import PartitionSpec as P

SHIFT = 7.5
SCALE = 3.0
LEVELS = 5
M = 64
NEXTRA = 5
NF = M + NEXTRA
GROUPS = 16
NE = 5
HI = lax.Precision.HIGHEST


def iota_row():
    return lax.broadcasted_iota(jnp.int32, (8, 128), 0)


def iota_lane():
    return lax.broadcasted_iota(jnp.int32, (8, 128), 1)


def roll_lane(tile, shift):
    shift = shift % 128
    return tile if shift == 0 else pltpu.roll(tile, shift, 1)


def roll_row(tile, shift):
    shift = shift % 8
    return tile if shift == 0 else pltpu.roll(tile, shift, 0)


def swap_shift(first, second, roll, shift, mask):
    first, second = roll(first, shift), roll(second, shift)
    return jnp.where(mask, second, first), jnp.where(mask, first, second)


def tile(ref, index):
    if isinstance(index, int):
        return ref[8 * index : 8 * index + 8, :]
    return ref[pl.ds(pl.multiple_of(index * 8, 8), 8), :]


def put(ref, index, value):
    if isinstance(index, int):
        ref[8 * index : 8 * index + 8, :] = value
    else:
        ref[pl.ds(pl.multiple_of(index * 8, 8), 8), :] = value


def group_mask(lane, q):
    at = (lane + (4 - 8 * q)) & 127
    return at < 8


def pack_kernel(right_ref, vel_ref, decay_ref, class_ref, table_ref, zmsg_ref, conduct_ref):
    lane = iota_lane()
    classes = class_ref[...]
    conduct = jnp.zeros((8, 128), jnp.float32)
    for index in range(table_ref.shape[0]):
        conduct = jnp.where(classes == index, table_ref[index], conduct)
    conduct_ref[...] = conduct

    def packed(get):
        total = jnp.zeros((8, 128), jnp.float32)
        for q in range(GROUPS):
            value = get(q)
            if value is None:
                break
            total = jnp.where(group_mask(lane, q), roll_lane(value, 8 * q), total)
        return total

    for t in range(M // GROUPS):
        put(zmsg_ref, t, packed(lambda q, t=t: tile(right_ref, t * GROUPS + q)))
    extra = [tile(vel_ref, 0), tile(vel_ref, 1), tile(vel_ref, 2), decay_ref[...], conduct]
    put(zmsg_ref, NE - 1, packed(lambda q: extra[q] if q < NEXTRA else None))


def ymsg_kernel(
    right_ref, vel_ref, decay_ref, conduct_ref, low_ref, high_ref, up_ref, down_ref, edge_ref
):
    row, lane = iota_row(), iota_lane()
    edges = []
    for t in range(NE):
        edge = jnp.where((lane & 7) >= 4, tile(low_ref, t), tile(high_ref, t))
        put(edge_ref, t, edge)
        edges.append(edge)

    def source(index):
        if index < M:
            return tile(right_ref, index)
        if index < M + 3:
            return tile(vel_ref, index - M)
        if index == M + 3:
            return decay_ref[...]
        if index == M + 4:
            return conduct_ref[...]
        return edges[index - NF]

    lower = row < 4
    for g in range((NF + NE) // 2):
        first, second = source(2 * g), roll_row(source(2 * g + 1), 4)
        put(up_ref, g, jnp.where(lower, second, first))
        put(down_ref, g, jnp.where(lower, first, second))


X1 = 2 * M + 2 * NE + 2


def xmsg_kernel(right_ref, conduct_ref, edge_ref, below_ref, above_ref, msg_ref, extra_ref):
    row = iota_row()
    lower = row < 4
    for f in range(M):
        put(msg_ref, f, tile(right_ref, f))
    for t in range(NE):
        put(msg_ref, 2 * M + t, tile(edge_ref, t))
    put(msg_ref, 2 * M + 2 * NE, conduct_ref[...])
    for g in range((NF + NE) // 2):
        below, above = tile(below_ref, g), tile(above_ref, g)
        pair = (jnp.where(lower, above, below), roll_row(jnp.where(lower, below, above), 4))
        for half in range(2):
            index = 2 * g + half
            if index < M:
                put(msg_ref, M + index, pair[half])
            elif index < M + 4:
                put(extra_ref, index - M, pair[half])
            elif index == M + 4:
                put(msg_ref, 2 * M + 2 * NE + 1, pair[half])
            else:
                put(msg_ref, 2 * M + NE + index - NF, pair[half])


def coefficients(sizes, cells_ref, rate_ref, vel_ref, decay_ref, extra_ref, own_ref, left_ref, right_ref, coef_ref):
    row, lane = iota_row(), iota_lane()
    size_y, size_z = sizes
    at_x, at_y, at_z = lax.axis_index("gx"), lax.axis_index("gy"), lax.axis_index("gz")

    def parts(ref):
        base = 2 * M
        return [
            tile(ref, base + 2 * NE),
            tile(ref, base + 2 * NE + 1),
            roll_lane(tile(ref, base + NE - 1), -8 * 4),
            roll_lane(tile(ref, base + 2 * NE - 1), -8 * 4),
        ]

    edge_m, edge_y = tile(own_ref, 2 * M + NE - 1), tile(own_ref, 2 * M + 2 * NE - 1)

    def given(main, index):
        return [main, tile(extra_ref, index), roll_lane(edge_m, -8 * index), roll_lane(edge_y, -8 * index)]

    velocity = [given(tile(vel_ref, d), d) for d in range(3)]
    decay = given(decay_ref[...], 3)
    center, before, after = parts(own_ref), parts(left_ref), parts(right_ref)

    def shift_y(four, shift, mask):
        main, my = swap_shift(four[0], four[1], roll_row, shift, mask)
        edge, ey = swap_shift(four[2], four[3], roll_row, shift, mask)
        return [main, my, edge, ey]

    def shift_z(four, shift, mask):
        main, edge = swap_shift(four[0], four[2], roll_lane, shift, mask)
        my, ey = swap_shift(four[1], four[3], roll_lane, shift, mask)
        return [main, my, edge, ey]

    plus = [after, shift_y(center, -1, row == 7), shift_z(center, -1, lane == 127)]
    minus = [before, shift_y(center, 1, row == 0), shift_z(center, 1, lane == 0)]

    y_main = at_y * 8 + row
    y_my = at_y * 8 + jnp.where(row < 4, row + 8, row - 8)
    z_main = at_z * 128 + lane
    z_edge = at_z * 128 + jnp.where(lane < 64, lane + 128, lane - 128)
    for part, (y_at, z_at) in enumerate(((y_main, z_main), (y_my, z_main), (y_main, z_edge), (y_my, z_edge))):
        flat = (at_x * size_y + y_at) * size_z + z_at
        wells = jnp.zeros((8, 128), jnp.float32)
        for w in range(cells_ref.shape[0]):
            wells = wells + jnp.where(flat == cells_ref[w], rate_ref[w], 0.0)
        inside = (y_at >= 0) & (y_at < size_y) & (z_at >= 0) & (z_at < size_z)
        if part >= 2:
            inside = inside & ((lane < 4) | (lane >= 124))
        diagonal = decay[part] + wells
        upper, lower = [], []
        for d in range(3):
            plus_face = 0.5 * (center[part] + plus[d][part])
            minus_face = 0.5 * (center[part] + minus[d][part])
            diagonal = diagonal + (velocity[d][part] + plus_face + minus_face)
            upper.append(velocity[d][part] + plus_face)
            lower.append(minus_face)
        values = [(diagonal - SHIFT) * (1.0 / SCALE)]
        for d in range(3):
            values += [upper[d] * (-1.0 / SCALE), lower[d] * (-1.0 / SCALE)]
        for index, value in enumerate(values):
            value = jnp.where(inside, value, 0.0)
            if part >= 2:
                for shift in (8, 16, 32, 64):
                    value = value + roll_lane(value, shift)
            put(coef_ref, index * 4 + part, value)


def unpack_my(level, ref, t, q, base):
    if level == 1:
        return tile(ref, base + t * GROUPS + q)
    if level == 2:
        return roll_row(tile(ref, base + t * (GROUPS // 2) + q // 2), -4 * (q % 2))
    return roll_row(tile(ref, base + t * (GROUPS // 4) + q // 4), -2 * (q % 4))


def edge_base(level):
    return {1: 2 * M, 2: M + M // 2, 3: M + M // 4}[level]


def message_tiles(level):
    return {1: X1, 2: M + M // 2 + 8, 3: M + M // 4 + 4, 4: M}[level]


def step_body(level, coef_ref, main_ref, my_ref, my_base, em_ref, em_base, ey_ref, ey_base, left_ref, right_ref, out_ref, out_my_ref, out_e_ref):
    row, lane = iota_row(), iota_lane()
    row_0, row_7 = row == 0, row == 7
    lane_0, lane_127 = lane == 0, lane == 127
    with_my = level < 4
    with_ey = level < 3
    keep_2 = (row < 2) | (row >= 6)

    def coef(index, part):
        return tile(coef_ref, index * 4 + part)

    def apply(part, center, after, before, y_plus, y_minus, z_plus, z_minus):
        total = coef(0, part) * center
        if after is not None:
            total = total + (coef(1, part) * after + coef(2, part) * before)
        total = total + (coef(3, part) * y_plus + coef(4, part) * y_minus)
        return total + (coef(5, part) * z_plus + coef(6, part) * z_minus)

    def group(t, carry):
        em = tile(em_ref, em_base + t)
        ey = tile(ey_ref, ey_base + t) if with_my else None
        near_m = jnp.zeros((8, 128), jnp.float32)
        near_y = jnp.zeros((8, 128), jnp.float32)
        packed = None
        for q in range(GROUPS):
            f = t * GROUPS + q
            main, my = tile(main_ref, f), tile(my_ref, my_base + f)
            beside = roll_lane(em, -8 * q)
            z_plus = roll_lane(jnp.where(lane_0, beside, main), -1)
            z_minus = roll_lane(jnp.where(lane_127, beside, main), 1)
            y_plus, my_plus = swap_shift(main, my, roll_row, -1, row_7)
            y_minus, my_minus = swap_shift(main, my, roll_row, 1, row_0)
            result = apply(0, main, tile(right_ref, f), tile(left_ref, f), y_plus, y_minus, z_plus, z_minus)
            put(out_ref, f, result)
            if not with_my:
                continue
            at = ((lane + (1 - 8 * q)) & 127) < 2
            near_m = jnp.where(at, roll_lane(main, 8 * q), near_m)
            beside = roll_lane(ey, -8 * q)
            z_plus = roll_lane(jnp.where(lane_0, beside, my), -1)
            z_minus = roll_lane(jnp.where(lane_127, beside, my), 1)
            result = apply(
                1,
                my,
                unpack_my(level, right_ref, t, q, M),
                unpack_my(level, left_ref, t, q, M),
                my_plus,
                my_minus,
                z_plus,
                z_minus,
            )
            put(out_my_ref, f, result)
            if with_ey:
                near_y = jnp.where(at, roll_lane(my, 8 * q), near_y)
            if level == 1:
                packed = result if q % 2 == 0 else jnp.where(keep_2, packed, roll_row(result, 4))
                if q % 2 == 1:
                    put(out_ref, M + t * (GROUPS // 2) + q // 2, packed)
            elif level == 2:
                s = q % 4
                at_row = ((row + (1 - 2 * s)) & 7) < 2
                packed = result if s == 0 else jnp.where(at_row, roll_row(result, 2 * s), packed)
                if s == 3:
                    put(out_ref, M + t * (GROUPS // 4) + q // 4, packed)
        if with_my:
            seven, zero = (lane & 7) == 7, (lane & 7) == 0
            base = edge_base(level)
            em_plus, ey_plus = swap_shift(em, ey, roll_row, -1, row_7)
            em_minus, ey_minus = swap_shift(em, ey, roll_row, 1, row_0)
            z_plus = jnp.where(seven, roll_lane(near_m, -1), roll_lane(em, -1))
            z_minus = jnp.where(zero, roll_lane(near_m, 1), roll_lane(em, 1))
            result = apply(2, em, tile(right_ref, base + t), tile(left_ref, base + t), em_plus, em_minus, z_plus, z_minus)
            put(out_e_ref, t, result)
            if level < 3:
                put(out_ref, edge_base(level + 1) + t, result)
            if with_ey:
                z_plus = jnp.where(seven, roll_lane(near_y, -1), roll_lane(ey, -1))
                z_minus = jnp.where(zero, roll_lane(near_y, 1), roll_lane(ey, 1))
                base = base + (NE if level == 1 else 4)
                result = apply(3, ey, tile(right_ref, base + t), tile(left_ref, base + t), ey_plus, ey_minus, z_plus, z_minus)
                put(out_e_ref, 4 + t, result)
                if level == 1:
                    put(out_ref, edge_base(2) + 4 + t, result)
        return carry

    lax.fori_loop(0, M // GROUPS, group, 0)


def first_kernel(sizes, cells_ref, rate_ref, vel_ref, decay_ref, extra_ref, own_ref, left_ref, right_ref, coef_ref, out_ref, out_my_ref, out_e_ref):
    coefficients(sizes, cells_ref, rate_ref, vel_ref, decay_ref, extra_ref, own_ref, left_ref, right_ref, coef_ref)
    step_body(1, coef_ref, own_ref, own_ref, M, own_ref, 2 * M, own_ref, 2 * M + NE, left_ref, right_ref, out_ref, out_my_ref, out_e_ref)


def middle_kernel(level, coef_ref, own_ref, my_ref, e_ref, left_ref, right_ref, out_ref, out_my_ref, out_e_ref):
    step_body(level, coef_ref, own_ref, my_ref, 0, e_ref, 0, e_ref, 4, left_ref, right_ref, out_ref, out_my_ref, out_e_ref)


PAIRS = (
    ((0, 0), (0, 1)),
    ((0, 2), (0, 3)),
    ((1, 1), (1, 2)),
    ((1, 3), (1, 4)),
    ((2, 2), (2, 3)),
    ((3, 3), (3, 4)),
    ((4, 4), (2, 4)),
    ((0, 4), None),
)


def dot_nt(first, second):
    return lax.dot_general(first, second, (((1,), (1,)), ((), ())), precision=HI, preferred_element_type=jnp.float32)


def dot_tn(first, second):
    return lax.dot_general(first, second, (((0,), (0,)), ((), ())), precision=HI, preferred_element_type=jnp.float32)


def dot_nn(first, second):
    return lax.dot_general(first, second, (((1,), (0,)), ((), ())), precision=HI, preferred_element_type=jnp.float32)


def gram_kernel(coef_ref, own_ref, my_ref, e_ref, left_ref, right_ref, block_0, block_1, block_2, basis_ref, gram_ref, last_ref):
    step_body(4, coef_ref, own_ref, my_ref, 0, e_ref, 0, None, 0, left_ref, right_ref, last_ref, None, None)
    for level, ref in enumerate((block_0, block_1, block_2, own_ref, last_ref)):
        for y in range(8):
            basis_ref[M * level : M * (level + 1), 128 * y : 128 * (y + 1)] = ref[pl.ds(y, M, stride=8), :]
    full = dot_nt(basis_ref[...], basis_ref[...])
    for index, pair in enumerate(PAIRS):
        for half, at in enumerate(pair):
            if at is None:
                value = jnp.zeros((M, M), jnp.float32)
            else:
                value = full[M * at[0] : M * at[0] + M, M * at[1] : M * at[1] + M]
            gram_ref[M * index : M * (index + 1), M * half : M * (half + 1)] = value


def eliminate(matrix, wanted):
    both = jnp.concatenate([matrix, wanted], axis=1)
    rows = lax.broadcasted_iota(jnp.int32, both.shape, 0)
    for k in range(M):
        pivot_row = both[k : k + 1, :]
        scaled = pivot_row / pivot_row[:, k : k + 1]
        column = both[:, k : k + 1]
        both = jnp.where(rows == k, scaled, both - column * scaled)
    return both[:, M:]


def apply_levels(blocks):
    out = [SHIFT * b for b in blocks] + [None]
    for j, b in enumerate(blocks):
        out[j + 1] = SCALE * b if out[j + 1] is None else out[j + 1] + SCALE * b
    return out


def pad_levels(blocks, count):
    return list(blocks) + [jnp.zeros((M, M), jnp.float32)] * (count - len(blocks))


def final_kernel(gram_ref, basis_ref, field_ref, resid_ref, full_ref):
    for index, pair in enumerate(PAIRS):
        for half, at in enumerate(pair):
            if at is None:
                continue
            value = gram_ref[M * index : M * (index + 1), M * half : M * (half + 1)]
            full_ref[M * at[0] : M * at[0] + M, M * at[1] : M * at[1] + M] = value
            if at[0] != at[1]:
                full_ref[M * at[1] : M * at[1] + M, M * at[0] : M * at[0] + M] = value.T
    eye = jnp.where(
        lax.broadcasted_iota(jnp.int32, (M, M), 0) == lax.broadcasted_iota(jnp.int32, (M, M), 1), 1.0, 0.0
    ).astype(jnp.float32)

    def gram(levels, blocks):
        count = M * levels
        return dot_nn(full_ref[0:count, 0 : M * len(blocks)], jnp.concatenate(blocks, axis=0))

    def minimal(half, second):
        levels = len(second)
        product = gram(levels, second)
        cross = sum(product[M * j : M * j + M] * b for j, b in enumerate(half))
        square = sum(product[M * j : M * j + M] * b for j, b in enumerate(second))
        return jnp.sum(cross) / jnp.sum(square), product[0:M]

    image_gram = SHIFT * full_ref[0:M, 0:M] + SCALE * full_ref[0:M, M : 2 * M]
    inverse = eliminate(dot_tn(image_gram, image_gram), image_gram.T)
    alpha = dot_nn(inverse, full_ref[0:M, 0:M])
    half = [eye - SHIFT * alpha, -SCALE * alpha]
    second = apply_levels(half)
    omega, second_gram = minimal(half, second)
    field = [alpha + omega * half[0], omega * half[1]]
    resid = [half[0] - omega * second[0], half[1] - omega * second[1], -omega * second[2]]
    beta = -dot_nn(inverse, second_gram)
    direct = [
        resid[0] + (1.0 - omega * SHIFT) * beta,
        resid[1] - (omega * SCALE) * beta,
        resid[2],
    ]
    image = apply_levels(direct)
    stacked = jnp.concatenate(
        [jnp.concatenate(image, axis=0), jnp.concatenate(pad_levels(resid, 4), axis=0)], axis=1
    )
    both = dot_nn(full_ref[0:M, 0 : 4 * M], stacked)
    image_gram, resid_gram = both[:, 0:M], both[:, M:]
    inverse = eliminate(dot_tn(image_gram, image_gram), image_gram.T)
    alpha = dot_nn(inverse, resid_gram)
    product = dot_nn(jnp.concatenate(image + direct, axis=0), alpha)
    half = [r - product[M * j : M * j + M] for j, r in enumerate(pad_levels(resid, 4))]
    second = apply_levels(half)
    omega, _ = minimal(half, second)
    field = pad_levels(field, 4)
    moved = [product[M * (4 + j) : M * (5 + j)] for j in range(3)] + [None]
    field = [
        f + omega * h + (0.0 if m is None else m) for f, h, m in zip(field, half, moved)
    ]
    field = pad_levels(field, 5)
    resid = [h - omega * s for h, s in zip(pad_levels(half, 5), second)]
    coefs = jnp.concatenate([jnp.concatenate(field, axis=0), jnp.concatenate(resid, axis=0)], axis=1)
    for y in range(8):
        result = dot_tn(coefs, basis_ref[:, 128 * y : 128 * (y + 1)])
        field_ref[pl.ds(y, M, stride=8), :] = result[0:M]
        resid_ref[pl.ds(y, M, stride=8), :] = result[M:]


VMEM = pl.BlockSpec(memory_space=pltpu.VMEM)
SMEM = pl.BlockSpec(memory_space=pltpu.SMEM)


def f32(*shape):
    return jax.ShapeDtypeStruct(shape, jnp.float32)


def call(kernel, name, outs, specs, scratch=()):
    return pl.pallas_call(
        kernel,
        name=name,
        out_shape=outs,
        in_specs=specs,
        out_specs=tuple(VMEM for _ in outs) if isinstance(outs, tuple) else VMEM,
        scratch_shapes=list(scratch),
        compiler_params=pltpu.CompilerParams(vmem_limit_bytes=32 * 1024 * 1024),
    )


def from_sides(axis, up, down):
    count = lax.axis_size(axis)
    lower = lax.ppermute(up, axis, [(i, i + 1) for i in range(count - 1)])
    upper = lax.ppermute(down, axis, [(i + 1, i) for i in range(count - 1)])
    return lower, upper


def spread(values, axes):
    count = lax.axis_size(axes)
    return lax.all_to_all(jnp.broadcast_to(values, (count, *values.shape)), axes, 0, 0)


def per_device(right_side, velocity, decay_rate, perm_class, conductivity, well_cells, well_rate):
    sizes = (8 * lax.axis_size("gy"), 128 * lax.axis_size("gz"))
    block_0 = right_side.reshape(8 * M, 128)
    vel = velocity.reshape(24, 128)
    decay = decay_rate.reshape(8, 128)
    classes = perm_class.reshape(8, 128)

    zmsg, conduct = call(
        pack_kernel, "pack", (f32(8 * NE, 128), f32(8, 128)), [VMEM, VMEM, VMEM, VMEM, SMEM]
    )(block_0, vel, decay, classes, conductivity)
    low, high = from_sides("gz", zmsg, zmsg)
    tiles = 8 * ((NF + NE) // 2)
    up, down, edge = call(
        ymsg_kernel, "ymsg", (f32(tiles, 128), f32(tiles, 128), f32(8 * NE, 128)), [VMEM] * 6
    )(block_0, vel, decay, conduct, low, high)
    below, above = from_sides("gy", up, down)
    own, extra = call(xmsg_kernel, "xmsg", (f32(8 * X1, 128), f32(32, 128)), [VMEM] * 5)(
        block_0, conduct, edge, below, above
    )
    left, right = from_sides("gx", own, own)

    def outs(level):
        return (f32(8 * message_tiles(level + 1), 128), f32(8 * M, 128), f32(64, 128))

    coef, block_1, my, edges = call(
        functools.partial(first_kernel, sizes),
        "first",
        (f32(8 * 28, 128), *outs(1)),
        [SMEM, SMEM] + [VMEM] * 6,
    )(well_cells, well_rate, vel, decay, extra, own, left, right)
    left, right = from_sides("gx", block_1, block_1)
    block_2, my, edges = call(functools.partial(middle_kernel, 2), "second", outs(2), [VMEM] * 6)(
        coef, block_1, my, edges, left, right
    )
    left, right = from_sides("gx", block_2, block_2)
    block_3, my, edges = call(functools.partial(middle_kernel, 3), "third", outs(3), [VMEM] * 6)(
        coef, block_2, my, edges, left, right
    )
    left, right = from_sides("gx", block_3, block_3)
    basis, gram = call(
        gram_kernel,
        "gram",
        (f32(LEVELS * M, 1024), f32(8 * M, 128)),
        [VMEM] * 9,
        [pltpu.VMEM((8 * M, 128), jnp.float32)],
    )(coef, block_3, my, edges, left, right, block_0, block_1, block_2)

    plane = ("gy", "gz")
    count = lax.axis_size(plane)
    gram = lax.all_to_all(gram.reshape(count, -1, 128), plane, 0, 0)
    gram = jnp.sum(gram, axis=0)
    gram = jnp.sum(spread(gram, "gx"), axis=0)
    gram = spread(gram, plane).reshape(8 * M, 128)
    field, resid = call(
        final_kernel,
        "final",
        (f32(8 * M, 128), f32(8 * M, 128)),
        [VMEM, VMEM],
        [pltpu.VMEM((LEVELS * M, LEVELS * M), jnp.float32)],
    )(gram, basis)
    return field.reshape(right_side.shape), resid.reshape(right_side.shape)


def solution(mesh):
    placed = (
        P(None, "gx", "gy", "gz"),
        P(None, "gx", "gy", "gz"),
        P("gx", "gy", "gz"),
        P("gx", "gy", "gz"),
        P(),
        P(),
        P(),
    )
    return jax.shard_map(
        per_device,
        mesh=mesh,
        in_specs=placed,
        out_specs=(P(None, "gx", "gy", "gz"), P(None, "gx", "gy", "gz")),
        check_vma=False,
    )
```

time: 587 us -> 158 us (0.27)
  blocking collectives: 412 us -> 61.4 us
  starting transfers between devices: 80.7 us -> 39.8 us
  other arithmetic: 33.1 us -> 0.05 us
  Pallas kernels: 0 us -> 24.4 us
  local copies, waits for them, and re-layouts: 18.5 us -> 6.41 us
  matrix products: 8.9 us -> 0 us
    psum x4 -> x0, blocking collectives: 412 us -> none  [the longest x2 210 us: per_device(): lax.psum((gram_matrix(right_side, residual), gram_matrix(right_side, imag...]
    all_to_all x0 -> x3, blocking collectives: none -> 61.4 us  [the longest x2 41.6 us: spread(): lax.all_to_all(jnp.broadcast_to(values, (count, *values.shape)), axes, 0, 0)]
    ppermute x30 -> x12, starting transfers between devices: 80.7 us -> 39.8 us  [the longest x6 23.1 us: from_sides(): lower = lax.ppermute(up, axis, [(i, i + 1) for i in range(count - 1)])]
    another operation x11 -> x0, other arithmetic: 25.4 us -> none  [the longest x6 13 us: solve_block(): factor = jnp.linalg.cholesky(normal)]
    pallas_call x0 -> x8, Pallas kernels: none -> 24.4 us  [the longest x1 16.4 us: per_device(): call(final_kernel, 'final', (f32(8 * M, 128), f32(8 * M, 128)), [VMEM, VM...]
    dot_general x15 -> x0, matrix products: 7.48 us -> none  [the longest x5 3.55 us: combine(): jnp.einsum('ab,aijk->bijk', coefs, field, precision=lax.Precision.HIGHEST)]
    ppermute x30 -> x12, waiting for transfers between devices: 28.1 us -> 24.7 us  [the longest x6 17 us: from_sides(): upper = lax.ppermute(down, axis, [(i + 1, i) for i in range(count - 1)])]
  transfers between devices with their start and end apart: 30 -> 12, of which waited for: 20 -> 11; matrix products, arithmetic and copies ran while one was open for 2% -> 0% of each run, Pallas kernels for 0% -> 0%
where the time goes in v1:
time: 158 us; the launch traced here: 157 us
  blocking collectives  61.4 us (39%)
  starting transfers between devices  39.8 us (25%)
  waiting for transfers between devices  24.7 us (16%)
  Pallas kernels  24.4 us (15%)
  local copies, waits for them, and re-layouts  6.41 us (4%)
    all_to_all x2, blocking collectives, spread(): lax.all_to_all(jnp.broadcast_to(values, (count, *values.shape)), axes, 0, 0)  41.6 us
    ppermute x6, starting transfers between devices, from_sides(): lower = lax.ppermute(up, axis, [(i, i + 1) for i in range(count - 1)])  23.1 us
    all_to_all x1, blocking collectives, per_device(): gram = lax.all_to_all(gram.reshape(count, -1, 128), plane, 0, 0)  19.7 us
    ppermute x6, waiting for transfers between devices, from_sides(): upper = lax.ppermute(down, axis, [(i + 1, i) for i in range(count - 1)])  17 us
    ppermute x6, starting transfers between devices, from_sides(): upper = lax.ppermute(down, axis, [(i + 1, i) for i in range(count - 1)])  16.7 us
    pallas_call x1, Pallas kernels, per_device(): call(final_kernel, 'final', (f32(8 * M, 128), f32(8 * M, 128)), [VMEM, VM...  16.4 us
    ppermute x6, waiting for transfers between devices, from_sides(): lower = lax.ppermute(up, axis, [(i, i + 1) for i in range(count - 1)])  7.62 us
    unnamed x20, local copies, waits for them, and re-layouts  6.38 us
  transfers between devices with their start and end apart: 12, of which 11 were waited for; matrix products, arithmetic and copies ran while one was open for 0% of the time, Pallas kernels for 0%

profile of v1, /device:TPU:1, one launch (start us, length us, event | category | flops | bytes accessed | tf_op | source)
XLA Modules:
  0.0 157.5 jit_solution(13997961898158407549)
XLA Ops:
  5.0 1.3 collective-permute-start.1
  6.3 4.6 %collective-permute-start = (f32[40,128]{1,0:T(8,128)S(1)}, f32[40,128]{1,0:T(8,128)S(1)}, u32[]{:S(2)}, u32[]{:S(2)}) collective-permute-start(f32[40,128]{1,0:T(8,128)S(1)} %get-tuple-element.24), channel_id=1, source_target_pairs={{0,1},{1,2},{2,3},{4,5},{5,6},{6,7},{8,9},{9,10},{10,11},{12,13},{... | collective-permute-start | bytes 61448 | tf_op jit(solution)/shard_map/ppermute | solution.py:466
  11.8 3.5 %collective-permute-start.2 = (f32[296,128]{1,0:T(8,128)S(1)}, f32[296,128]{1,0:T(8,128)S(1)}, u32[]{:S(2)}, u32[]{:S(2)}) collective-permute-start(f32[296,128]{1,0:T(8,128)S(1)} %get-tuple-element.26), channel_id=1, source_target_pairs={{0,4},{4,8},{8,12},{12,16},{16,20},{20,24},{24,28},{1,5},{5,9},{9,... | collective-permute-start | bytes 454664 | tf_op jit(solution)/shard_map/ppermute | solution.py:466
  15.3 1.3 collective-permute-start.3
  17.4 3.8 %collective-permute-done.3.above_ref = f32[296,128]{1,0:T(8,128)S(1)} collective-permute-done((f32[296,128]{1,0:T(8,128)S(1)}, f32[296,128]{1,0:T(8,128)S(1)}, u32[]{:S(2)}, u32[]{:S(2)}) %collective-permute-start.3) | collective-permute-done | bytes 151584 | tf_op jit(solution)/shard_map/ppermute | solution.py:467
  21.2 8.3 %collective-permute-start.5 = (f32[1120,128]{1,0:T(8,128)S(1)}, f32[1120,128]{1,0:T(8,128)S(1)}, u32[]{:S(2)}, u32[]{:S(2)}) collective-permute-start(f32[1120,128]{1,0:T(8,128)S(1)} %get-tuple-element.29.own_ref), channel_id=1, source_target_pairs={{32,0},{64,32},{96,64},{128,96},{160,128},{192,160},{224,192},{256... | collective-permute-start | bytes 1720328 | tf_op jit(solution)/shard_map/ppermute | solution.py:467
  29.6 1.9 %collective-permute-start.4 = (f32[1120,128]{1,0:T(8,128)S(1)}, f32[1120,128]{1,0:T(8,128)S(1)}, u32[]{:S(2)}, u32[]{:S(2)}) collective-permute-start(f32[1120,128]{1,0:T(8,128)S(1)} %get-tuple-element.29.own_ref), channel_id=1, source_target_pairs={{0,32},{32,64},{64,96},{96,128},{128,160},{160,192},{192,224},{224... | collective-permute-start | bytes 1720328 | tf_op jit(solution)/shard_map/ppermute | solution.py:466
  31.5 4.2 %collective-permute-done.5.right_ref = f32[1120,128]{1,0:T(8,128)S(1)} collective-permute-done((f32[1120,128]{1,0:T(8,128)S(1)}, f32[1120,128]{1,0:T(8,128)S(1)}, u32[]{:S(2)}, u32[]{:S(2)}) %collective-permute-start.5) | collective-permute-done | bytes 573472 | tf_op jit(solution)/shard_map/ppermute | solution.py:467
  35.7 2.4 %collective-permute-done.4.left_ref = f32[1120,128]{1,0:T(8,128)S(1)} collective-permute-done((f32[1120,128]{1,0:T(8,128)S(1)}, f32[1120,128]{1,0:T(8,128)S(1)}, u32[]{:S(2)}, u32[]{:S(2)}) %collective-permute-start.4) | collective-permute-done | bytes 573472 | tf_op jit(solution)/shard_map/ppermute | solution.py:466
  40.8 2.1 %first.1 = (f32[224,128]{1,0:T(8,128)S(1)}, f32[832,128]{1,0:T(8,128)S(1)}, f32[512,128]{1,0:T(8,128)S(1)}, f32[64,128]{1,0:T(8,128)S(1)}) custom-call(s32[32]{0:T(128)S(1)} %copy-done.8, f32[32]{0:T(128)S(1)} %copy-done.9, f32[24,128]{1,0:T(8,128)S(1)} %bitcast.20, f32[8,128]{1,0:T(8,128)S(1)} %bitcast.23, f32[32,128]{1,0:T(8,128)S(1)} %get-tuple-element.28.extra_ref, ...), custom_call_target="tpu_custom_call" | custom-call | tf_op jit(solution)/shard_map/first/pallas_call | solution.py:500
  42.9 1.9 %collective-permute-start.7 = (f32[832,128]{1,0:T(8,128)S(1)}, f32[832,128]{1,0:T(8,128)S(1)}, u32[]{:S(2)}, u32[]{:S(2)}) collective-permute-start(f32[832,128]{1,0:T(8,128)S(1)} %get-tuple-element.31.own_ref.block_1), channel_id=1, source_target_pairs={{32,0},{64,32},{96,64},{128,96},{160,128},{192,160},{224,192},{256... | collective-permute-start | bytes 1277960 | tf_op jit(solution)/shard_map/ppermute | solution.py:467
  44.8 4.4 %collective-permute-start.6 = (f32[832,128]{1,0:T(8,128)S(1)}, f32[832,128]{1,0:T(8,128)S(1)}, u32[]{:S(2)}, u32[]{:S(2)}) collective-permute-start(f32[832,128]{1,0:T(8,128)S(1)} %get-tuple-element.31.own_ref.block_1), channel_id=1, source_target_pairs={{0,32},{32,64},{64,96},{96,128},{128,160},{160,192},{192,224},{224... | collective-permute-start | bytes 1277960 | tf_op jit(solution)/shard_map/ppermute | solution.py:466
  49.2 3.9 %collective-permute-done.7.right_ref = f32[832,128]{1,0:T(8,128)S(1)} collective-permute-done((f32[832,128]{1,0:T(8,128)S(1)}, f32[832,128]{1,0:T(8,128)S(1)}, u32[]{:S(2)}, u32[]{:S(2)}) %collective-permute-start.7) | collective-permute-done | bytes 426016 | tf_op jit(solution)/shard_map/ppermute | solution.py:467
  55.5 1.9 %collective-permute-start.9 = (f32[672,128]{1,0:T(8,128)S(1)}, f32[672,128]{1,0:T(8,128)S(1)}, u32[]{:S(2)}, u32[]{:S(2)}) collective-permute-start(f32[672,128]{1,0:T(8,128)S(1)} %get-tuple-element.34.own_ref.block_2), channel_id=1, source_target_pairs={{32,0},{64,32},{96,64},{128,96},{160,128},{192,160},{224,192},{256... | collective-permute-start | bytes 1032200 | tf_op jit(solution)/shard_map/ppermute | solution.py:467
  57.4 4.4 %collective-permute-start.8 = (f32[672,128]{1,0:T(8,128)S(1)}, f32[672,128]{1,0:T(8,128)S(1)}, u32[]{:S(2)}, u32[]{:S(2)}) collective-permute-start(f32[672,128]{1,0:T(8,128)S(1)} %get-tuple-element.34.own_ref.block_2), channel_id=1, source_target_pairs={{0,32},{32,64},{64,96},{96,128},{128,160},{160,192},{192,224},{224... | collective-permute-start | bytes 1032200 | tf_op jit(solution)/shard_map/ppermute | solution.py:466
  61.8 3.0 %collective-permute-done.9.right_ref = f32[672,128]{1,0:T(8,128)S(1)} collective-permute-done((f32[672,128]{1,0:T(8,128)S(1)}, f32[672,128]{1,0:T(8,128)S(1)}, u32[]{:S(2)}, u32[]{:S(2)}) %collective-permute-start.9) | collective-permute-done | bytes 344096 | tf_op jit(solution)/shard_map/ppermute | solution.py:467
  66.9 1.9 %collective-permute-start.11 = (f32[512,128]{1,0:T(8,128)S(1)}, f32[512,128]{1,0:T(8,128)S(1)}, u32[]{:S(2)}, u32[]{:S(2)}) collective-permute-start(f32[512,128]{1,0:T(8,128)S(1)} %get-tuple-element.37.own_ref), channel_id=1, source_target_pairs={{32,0},{64,32},{96,64},{128,96},{160,128},{192,160},{224,192},{256... | collective-permute-start | bytes 786440 | tf_op jit(solution)/shard_map/ppermute | solution.py:467
  68.9 4.4 %collective-permute-start.10 = (f32[512,128]{1,0:T(8,128)S(1)}, f32[512,128]{1,0:T(8,128)S(1)}, u32[]{:S(2)}, u32[]{:S(2)}) collective-permute-start(f32[512,128]{1,0:T(8,128)S(1)} %get-tuple-element.37.own_ref), channel_id=1, source_target_pairs={{0,32},{32,64},{64,96},{96,128},{128,160},{160,192},{192,224},{224... | collective-permute-start | bytes 786440 | tf_op jit(solution)/shard_map/ppermute | solution.py:466
  73.3 2.1 %collective-permute-done.11.right_ref = f32[512,128]{1,0:T(8,128)S(1)} collective-permute-done((f32[512,128]{1,0:T(8,128)S(1)}, f32[512,128]{1,0:T(8,128)S(1)}, u32[]{:S(2)}, u32[]{:S(2)}) %collective-permute-start.11) | collective-permute-done | bytes 262176 | tf_op jit(solution)/shard_map/ppermute | solution.py:467
  76.5 3.0 %gram.1 = (f32[320,1024]{1,0:T(8,128)S(1)}, f32[512,128]{1,0:T(8,128)S(1)}) custom-call(f32[224,128]{1,0:T(8,128)S(1)} %get-tuple-element.30.coef_ref, f32[512,128]{1,0:T(8,128)S(1)} %get-tuple-element.37.own_ref, f32[512,128]{1,0:T(8,128)S(1)} %get-tuple-element.38.my_ref, f32[64,128]{1,0:T(8,128)S(1)} %get-tuple-element.39.e_ref, ...), custom_call_target="tpu_custom_call" | custom-call | tf_op jit(solution)/shard_map/gram/pallas_call | solution.py:515
  79.6 19.7 %all_to_all.15 = f32[32,16,128]{2,1,0:T(8,128)S(1)} all-to-all(f32[32,16,128]{2,1,0:T(8,128)S(1)} %bitcast.17), channel_id=1, replica_groups=mesh['gx'=16,'gy'=8,'gz'=4] {'gy','gz'}, dimensions={0} | all-to-all | bytes 524288 | tf_op jit(solution)/shard_map/all_to_all | solution.py:525
  99.4 25.9 %all_to_all.16 = f32[16,16,128]{2,1,0:T(8,128)S(1)} all-to-all(f32[16,16,128]{2,1,0:T(8,128)S(1)} %broadcast_in_dim.6), channel_id=1, replica_groups=mesh['gx'=16,'gy'=8,'gz'=4] {'gx'}, dimensions={0} | all-to-all | bytes 262144 | tf_op jit(solution)/shard_map/all_to_all | solution.py:473
  125.3 15.7 %all_to_all.17 = f32[32,16,128]{2,1,0:T(8,128)S(1)} all-to-all(f32[32,16,128]{2,1,0:T(8,128)S(1)} %broadcast_in_dim.7), channel_id=1, replica_groups=mesh['gx'=16,'gy'=8,'gz'=4] {'gy','gz'}, dimensions={0} | all-to-all | bytes 524288 | tf_op jit(solution)/shard_map/all_to_all | solution.py:473
  141.0 16.4 %final.1 = (f32[512,128]{1,0:T(8,128)}, f32[512,128]{1,0:T(8,128)}) custom-call(f32[512,128]{1,0:T(8,128)S(1)} %bitcast.16, f32[320,1024]{1,0:T(8,128)S(1)} %get-tuple-element.41.basis_ref), custom_call_target="tpu_custom_call" | custom-call | tf_op jit(solution)/shard_map/final/pallas_call | solution.py:529
  (35 shorter events, 14.6 us)
Async XLA Ops:
  0.6 1.0 copy-start
  1.6 0.7 copy-start.2
  2.3 0.7 copy-start.4
  3.0 0.7 copy-start.6
  3.7 0.7 copy-start.7
  5.0 5.9 %collective-permute-start.1 = (f32[40,128]{1,0:T(8,128)S(1)}, f32[40,128]{1,0:T(8,128)S(1)}, u32[]{:S(2)}, u32[]{:S(2)}) collective-permute-start(f32[40,128]{1,0:T(8,128)S(1)} %get-tuple-element.24), channel_id=1, source_target_pairs={{1,0},{2,1},{3,2},{5,4},{6,5},{7,6},{9,8},{10,9},{11,10},{13,12},{... | collective-permute-start | bytes 61448 | tf_op jit(solution)/shard_map/ppermute | solution.py:467
  6.3 5.5 %collective-permute-start = (f32[40,128]{1,0:T(8,128)S(1)}, f32[40,128]{1,0:T(8,128)S(1)}, u32[]{:S(2)}, u32[]{:S(2)}) collective-permute-start(f32[40,128]{1,0:T(8,128)S(1)} %get-tuple-element.24), channel_id=1, source_target_pairs={{0,1},{1,2},{2,3},{4,5},{5,6},{6,7},{8,9},{9,10},{10,11},{12,13},{... | collective-permute-start | bytes 61448 | tf_op jit(solution)/shard_map/ppermute | solution.py:466
  11.8 5.6 %collective-permute-start.2 = (f32[296,128]{1,0:T(8,128)S(1)}, f32[296,128]{1,0:T(8,128)S(1)}, u32[]{:S(2)}, u32[]{:S(2)}) collective-permute-start(f32[296,128]{1,0:T(8,128)S(1)} %get-tuple-element.26), channel_id=1, source_target_pairs={{0,4},{4,8},{8,12},{12,16},{16,20},{20,24},{24,28},{1,5},{5,9},{9,... | collective-permute-start | bytes 454664 | tf_op jit(solution)/shard_map/ppermute | solution.py:466
  15.3 5.9 %collective-permute-start.3 = (f32[296,128]{1,0:T(8,128)S(1)}, f32[296,128]{1,0:T(8,128)S(1)}, u32[]{:S(2)}, u32[]{:S(2)}) collective-permute-start(f32[296,128]{1,0:T(8,128)S(1)} %get-tuple-element.27), channel_id=1, source_target_pairs={{4,0},{8,4},{12,8},{16,12},{20,16},{24,20},{28,24},{5,1},{9,5},{13... | collective-permute-start | bytes 454664 | tf_op jit(solution)/shard_map/ppermute | solution.py:467
  21.2 14.5 %collective-permute-start.5 = (f32[1120,128]{1,0:T(8,128)S(1)}, f32[1120,128]{1,0:T(8,128)S(1)}, u32[]{:S(2)}, u32[]{:S(2)}) collective-permute-start(f32[1120,128]{1,0:T(8,128)S(1)} %get-tuple-element.29.own_ref), channel_id=1, source_target_pairs={{32,0},{64,32},{96,64},{128,96},{160,128},{192,160},{224,192},{256... | collective-permute-start | bytes 1720328 | tf_op jit(solution)/shard_map/ppermute | solution.py:467
  29.6 8.6 %collective-permute-start.4 = (f32[1120,128]{1,0:T(8,128)S(1)}, f32[1120,128]{1,0:T(8,128)S(1)}, u32[]{:S(2)}, u32[]{:S(2)}) collective-permute-start(f32[1120,128]{1,0:T(8,128)S(1)} %get-tuple-element.29.own_ref), channel_id=1, source_target_pairs={{0,32},{32,64},{64,96},{96,128},{128,160},{160,192},{192,224},{224... | collective-permute-start | bytes 1720328 | tf_op jit(solution)/shard_map/ppermute | solution.py:466
  38.1 0.7 copy-start.3
  38.8 0.7 copy-start.5
  39.5 0.7 copy-start.8
  40.2 0.7 copy-start.9
  42.9 10.2 %collective-permute-start.7 = (f32[832,128]{1,0:T(8,128)S(1)}, f32[832,128]{1,0:T(8,128)S(1)}, u32[]{:S(2)}, u32[]{:S(2)}) collective-permute-start(f32[832,128]{1,0:T(8,128)S(1)} %get-tuple-element.31.own_ref.block_1), channel_id=1, source_target_pairs={{32,0},{64,32},{96,64},{128,96},{160,128},{192,160},{224,192},{256... | collective-permute-start | bytes 1277960 | tf_op jit(solution)/shard_map/ppermute | solution.py:467
  44.8 9.4 %collective-permute-start.6 = (f32[832,128]{1,0:T(8,128)S(1)}, f32[832,128]{1,0:T(8,128)S(1)}, u32[]{:S(2)}, u32[]{:S(2)}) collective-permute-start(f32[832,128]{1,0:T(8,128)S(1)} %get-tuple-element.31.own_ref.block_1), channel_id=1, source_target_pairs={{0,32},{32,64},{64,96},{96,128},{128,160},{160,192},{192,224},{224... | collective-permute-start | bytes 1277960 | tf_op jit(solution)/shard_map/ppermute | solution.py:466
  54.3 22.3 %copy-start.1 = (f32[64,1,8,128]{3,2,1,0:T(8,128)S(1)}, f32[64,1,8,128]{3,2,1,0:T(8,128)}, u32[]{:S(2)}) copy-start(f32[64,1,8,128]{3,2,1,0:T(8,128)} %param.7) | copy-start | bytes 786436
  55.5 9.3 %collective-permute-start.9 = (f32[672,128]{1,0:T(8,128)S(1)}, f32[672,128]{1,0:T(8,128)S(1)}, u32[]{:S(2)}, u32[]{:S(2)}) collective-permute-start(f32[672,128]{1,0:T(8,128)S(1)} %get-tuple-element.34.own_ref.block_2), channel_id=1, source_target_pairs={{32,0},{64,32},{96,64},{128,96},{160,128},{192,160},{224,192},{256... | collective-permute-start | bytes 1032200 | tf_op jit(solution)/shard_map/ppermute | solution.py:467
  57.4 8.6 %collective-permute-start.8 = (f32[672,128]{1,0:T(8,128)S(1)}, f32[672,128]{1,0:T(8,128)S(1)}, u32[]{:S(2)}, u32[]{:S(2)}) collective-permute-start(f32[672,128]{1,0:T(8,128)S(1)} %get-tuple-element.34.own_ref.block_2), channel_id=1, source_target_pairs={{0,32},{32,64},{64,96},{96,128},{128,160},{160,192},{192,224},{224... | collective-permute-start | bytes 1032200 | tf_op jit(solution)/shard_map/ppermute | solution.py:466
  66.9 8.4 %collective-permute-start.11 = (f32[512,128]{1,0:T(8,128)S(1)}, f32[512,128]{1,0:T(8,128)S(1)}, u32[]{:S(2)}, u32[]{:S(2)}) collective-permute-start(f32[512,128]{1,0:T(8,128)S(1)} %get-tuple-element.37.own_ref), channel_id=1, source_target_pairs={{32,0},{64,32},{96,64},{128,96},{160,128},{192,160},{224,192},{256... | collective-permute-start | bytes 786440 | tf_op jit(solution)/shard_map/ppermute | solution.py:467
  68.9 7.7 %collective-permute-start.10 = (f32[512,128]{1,0:T(8,128)S(1)}, f32[512,128]{1,0:T(8,128)S(1)}, u32[]{:S(2)}, u32[]{:S(2)}) collective-permute-start(f32[512,128]{1,0:T(8,128)S(1)} %get-tuple-element.37.own_ref), channel_id=1, source_target_pairs={{0,32},{32,64},{64,96},{96,128},{128,160},{160,192},{192,224},{224... | collective-permute-start | bytes 786440 | tf_op jit(solution)/shard_map/ppermute | solution.py:466

commit v2 on v1

--- a/solution.py
+++ b/solution.py
@@ -357,13 +357,43 @@
 
 def eliminate(matrix, wanted):
     both = jnp.concatenate([matrix, wanted], axis=1)
-    rows = lax.broadcasted_iota(jnp.int32, both.shape, 0)
-    for k in range(M):
-        pivot_row = both[k : k + 1, :]
-        scaled = pivot_row / pivot_row[:, k : k + 1]
-        column = both[:, k : k + 1]
-        both = jnp.where(rows == k, scaled, both - column * scaled)
-    return both[:, M:]
+    tiles = [both[8 * i : 8 * i + 8, :] for i in range(M // 8)]
+    rows = iota_row()
+
+    def column(value, at):
+        return jnp.broadcast_to(value[:, at : at + 1], (8, 128))
+
+    for i in range(M // 8):
+        columns = [[column(t, 8 * i + b) for b in range(8)] for t in tiles]
+        row = [jnp.broadcast_to(tiles[i][a : a + 1, :], (8, 128)) for a in range(8)]
+        small = [
+            [jnp.broadcast_to(columns[i][b][a : a + 1, :], (8, 128)) for b in range(8)]
+            for a in range(8)
+        ]
+        for p in range(8):
+            inverse = 1.0 / small[p][p]
+            for a in range(p + 1, 8):
+                factor = small[a][p] * inverse
+                row[a] = row[a] - factor * row[p]
+                for b in range(p + 1, 8):
+                    small[a][b] = small[a][b] - factor * small[p][b]
+            row[p] = row[p] * inverse
+            for b in range(p + 1, 8):
+                small[p][b] = small[p][b] * inverse
+        for p in range(7, 0, -1):
+            for a in range(p):
+                row[a] = row[a] - small[a][p] * row[p]
+        for j in range(M // 8):
+            if j == i:
+                value = row[0]
+                for b in range(1, 8):
+                    value = jnp.where(rows == b, row[b], value)
+            else:
+                value = tiles[j]
+                for b in range(8):
+                    value = value - columns[j][b] * row[b]
+            tiles[j] = value
+    return jnp.concatenate(tiles, axis=0)[:, M:]
 
 
 def apply_levels(blocks):

time: 158 us -> 154 us (0.975)
  Pallas kernels: 24.4 us -> 20.4 us
    pallas_call x1, Pallas kernels: 16.4 us -> 12.5 us  [per_device(): call(final_kernel, 'final', (f32(8 * M, 128), f32(8 * M, 128)), [VMEM, VM...]
where the time goes in v2:
time: 154 us
  blocking collectives  61.4 us (40%)
  starting transfers between devices  39.8 us (26%)
  waiting for transfers between devices  24.7 us (16%)
  Pallas kernels  20.4 us (13%)
  local copies, waits for them, and re-layouts  6.41 us (4%)
    all_to_all x2, blocking collectives, spread(): lax.all_to_all(jnp.broadcast_to(values, (count, *values.shape)), axes, 0, 0)  41.6 us
    ppermute x6, starting transfers between devices, from_sides(): lower = lax.ppermute(up, axis, [(i, i + 1) for i in range(count - 1)])  23.1 us
    all_to_all x1, blocking collectives, per_device(): gram = lax.all_to_all(gram.reshape(count, -1, 128), plane, 0, 0)  19.7 us
    ppermute x6, waiting for transfers between devices, from_sides(): upper = lax.ppermute(down, axis, [(i + 1, i) for i in range(count - 1)])  17 us
    ppermute x6, starting transfers between devices, from_sides(): upper = lax.ppermute(down, axis, [(i + 1, i) for i in range(count - 1)])  16.7 us
    pallas_call x1, Pallas kernels, per_device(): call(final_kernel, 'final', (f32(8 * M, 128), f32(8 * M, 128)), [VMEM, VM...  12.5 us
    ppermute x6, waiting for transfers between devices, from_sides(): lower = lax.ppermute(up, axis, [(i, i + 1) for i in range(count - 1)])  7.62 us
    unnamed x20, local copies, waits for them, and re-layouts  6.38 us
  transfers between devices with their start and end apart: 12, of which 11 were waited for; matrix products, arithmetic and copies ran while one was open for 0% of the time, Pallas kernels for 0%

profile of v2, /device:TPU:1, one launch (start us, length us, event | category | flops | bytes accessed | tf_op | source)
XLA Modules:
  0.0 153.5 jit_solution(17254092341147521604)
XLA Ops:
  5.0 1.3 collective-permute-start.1
  6.3 4.6 %collective-permute-start = (f32[40,128]{1,0:T(8,128)S(1)}, f32[40,128]{1,0:T(8,128)S(1)}, u32[]{:S(2)}, u32[]{:S(2)}) collective-permute-start(f32[40,128]{1,0:T(8,128)S(1)} %get-tuple-element.24), channel_id=1, source_target_pairs={{0,1},{1,2},{2,3},{4,5},{5,6},{6,7},{8,9},{9,10},{10,11},{12,13},{... | collective-permute-start | bytes 61448 | tf_op jit(solution)/shard_map/ppermute | solution.py:496
  11.8 3.5 %collective-permute-start.2 = (f32[296,128]{1,0:T(8,128)S(1)}, f32[296,128]{1,0:T(8,128)S(1)}, u32[]{:S(2)}, u32[]{:S(2)}) collective-permute-start(f32[296,128]{1,0:T(8,128)S(1)} %get-tuple-element.26), channel_id=1, source_target_pairs={{0,4},{4,8},{8,12},{12,16},{16,20},{20,24},{24,28},{1,5},{5,9},{9,... | collective-permute-start | bytes 454664 | tf_op jit(solution)/shard_map/ppermute | solution.py:496
  15.3 1.3 collective-permute-start.3
  17.4 3.8 %collective-permute-done.3.above_ref = f32[296,128]{1,0:T(8,128)S(1)} collective-permute-done((f32[296,128]{1,0:T(8,128)S(1)}, f32[296,128]{1,0:T(8,128)S(1)}, u32[]{:S(2)}, u32[]{:S(2)}) %collective-permute-start.3) | collective-permute-done | bytes 151584 | tf_op jit(solution)/shard_map/ppermute | solution.py:497
  21.2 8.3 %collective-permute-start.5 = (f32[1120,128]{1,0:T(8,128)S(1)}, f32[1120,128]{1,0:T(8,128)S(1)}, u32[]{:S(2)}, u32[]{:S(2)}) collective-permute-start(f32[1120,128]{1,0:T(8,128)S(1)} %get-tuple-element.29.own_ref), channel_id=1, source_target_pairs={{32,0},{64,32},{96,64},{128,96},{160,128},{192,160},{224,192},{256... | collective-permute-start | bytes 1720328 | tf_op jit(solution)/shard_map/ppermute | solution.py:497
  29.6 1.9 %collective-permute-start.4 = (f32[1120,128]{1,0:T(8,128)S(1)}, f32[1120,128]{1,0:T(8,128)S(1)}, u32[]{:S(2)}, u32[]{:S(2)}) collective-permute-start(f32[1120,128]{1,0:T(8,128)S(1)} %get-tuple-element.29.own_ref), channel_id=1, source_target_pairs={{0,32},{32,64},{64,96},{96,128},{128,160},{160,192},{192,224},{224... | collective-permute-start | bytes 1720328 | tf_op jit(solution)/shard_map/ppermute | solution.py:496
  31.5 4.2 %collective-permute-done.5.right_ref = f32[1120,128]{1,0:T(8,128)S(1)} collective-permute-done((f32[1120,128]{1,0:T(8,128)S(1)}, f32[1120,128]{1,0:T(8,128)S(1)}, u32[]{:S(2)}, u32[]{:S(2)}) %collective-permute-start.5) | collective-permute-done | bytes 573472 | tf_op jit(solution)/shard_map/ppermute | solution.py:497
  35.7 2.4 %collective-permute-done.4.left_ref = f32[1120,128]{1,0:T(8,128)S(1)} collective-permute-done((f32[1120,128]{1,0:T(8,128)S(1)}, f32[1120,128]{1,0:T(8,128)S(1)}, u32[]{:S(2)}, u32[]{:S(2)}) %collective-permute-start.4) | collective-permute-done | bytes 573472 | tf_op jit(solution)/shard_map/ppermute | solution.py:496
  40.8 2.1 %first.1 = (f32[224,128]{1,0:T(8,128)S(1)}, f32[832,128]{1,0:T(8,128)S(1)}, f32[512,128]{1,0:T(8,128)S(1)}, f32[64,128]{1,0:T(8,128)S(1)}) custom-call(s32[32]{0:T(128)S(1)} %copy-done.8, f32[32]{0:T(128)S(1)} %copy-done.9, f32[24,128]{1,0:T(8,128)S(1)} %bitcast.20, f32[8,128]{1,0:T(8,128)S(1)} %bitcast.23, f32[32,128]{1,0:T(8,128)S(1)} %get-tuple-element.28.extra_ref, ...), custom_call_target="tpu_custom_call" | custom-call | tf_op jit(solution)/shard_map/first/pallas_call | solution.py:530
  42.9 1.9 %collective-permute-start.7 = (f32[832,128]{1,0:T(8,128)S(1)}, f32[832,128]{1,0:T(8,128)S(1)}, u32[]{:S(2)}, u32[]{:S(2)}) collective-permute-start(f32[832,128]{1,0:T(8,128)S(1)} %get-tuple-element.31.own_ref.block_1), channel_id=1, source_target_pairs={{32,0},{64,32},{96,64},{128,96},{160,128},{192,160},{224,192},{256... | collective-permute-start | bytes 1277960 | tf_op jit(solution)/shard_map/ppermute | solution.py:497
  44.8 4.4 %collective-permute-start.6 = (f32[832,128]{1,0:T(8,128)S(1)}, f32[832,128]{1,0:T(8,128)S(1)}, u32[]{:S(2)}, u32[]{:S(2)}) collective-permute-start(f32[832,128]{1,0:T(8,128)S(1)} %get-tuple-element.31.own_ref.block_1), channel_id=1, source_target_pairs={{0,32},{32,64},{64,96},{96,128},{128,160},{160,192},{192,224},{224... | collective-permute-start | bytes 1277960 | tf_op jit(solution)/shard_map/ppermute | solution.py:496
  49.2 3.9 %collective-permute-done.7.right_ref = f32[832,128]{1,0:T(8,128)S(1)} collective-permute-done((f32[832,128]{1,0:T(8,128)S(1)}, f32[832,128]{1,0:T(8,128)S(1)}, u32[]{:S(2)}, u32[]{:S(2)}) %collective-permute-start.7) | collective-permute-done | bytes 426016 | tf_op jit(solution)/shard_map/ppermute | solution.py:497
  55.5 1.9 %collective-permute-start.9 = (f32[672,128]{1,0:T(8,128)S(1)}, f32[672,128]{1,0:T(8,128)S(1)}, u32[]{:S(2)}, u32[]{:S(2)}) collective-permute-start(f32[672,128]{1,0:T(8,128)S(1)} %get-tuple-element.34.own_ref.block_2), channel_id=1, source_target_pairs={{32,0},{64,32},{96,64},{128,96},{160,128},{192,160},{224,192},{256... | collective-permute-start | bytes 1032200 | tf_op jit(solution)/shard_map/ppermute | solution.py:497
  57.4 4.4 %collective-permute-start.8 = (f32[672,128]{1,0:T(8,128)S(1)}, f32[672,128]{1,0:T(8,128)S(1)}, u32[]{:S(2)}, u32[]{:S(2)}) collective-permute-start(f32[672,128]{1,0:T(8,128)S(1)} %get-tuple-element.34.own_ref.block_2), channel_id=1, source_target_pairs={{0,32},{32,64},{64,96},{96,128},{128,160},{160,192},{192,224},{224... | collective-permute-start | bytes 1032200 | tf_op jit(solution)/shard_map/ppermute | solution.py:496
  61.8 3.0 %collective-permute-done.9.right_ref = f32[672,128]{1,0:T(8,128)S(1)} collective-permute-done((f32[672,128]{1,0:T(8,128)S(1)}, f32[672,128]{1,0:T(8,128)S(1)}, u32[]{:S(2)}, u32[]{:S(2)}) %collective-permute-start.9) | collective-permute-done | bytes 344096 | tf_op jit(solution)/shard_map/ppermute | solution.py:497
  66.9 1.9 %collective-permute-start.11 = (f32[512,128]{1,0:T(8,128)S(1)}, f32[512,128]{1,0:T(8,128)S(1)}, u32[]{:S(2)}, u32[]{:S(2)}) collective-permute-start(f32[512,128]{1,0:T(8,128)S(1)} %get-tuple-element.37.own_ref), channel_id=1, source_target_pairs={{32,0},{64,32},{96,64},{128,96},{160,128},{192,160},{224,192},{256... | collective-permute-start | bytes 786440 | tf_op jit(solution)/shard_map/ppermute | solution.py:497
  68.9 4.4 %collective-permute-start.10 = (f32[512,128]{1,0:T(8,128)S(1)}, f32[512,128]{1,0:T(8,128)S(1)}, u32[]{:S(2)}, u32[]{:S(2)}) collective-permute-start(f32[512,128]{1,0:T(8,128)S(1)} %get-tuple-element.37.own_ref), channel_id=1, source_target_pairs={{0,32},{32,64},{64,96},{96,128},{128,160},{160,192},{192,224},{224... | collective-permute-start | bytes 786440 | tf_op jit(solution)/shard_map/ppermute | solution.py:496
  73.3 2.1 %collective-permute-done.11.right_ref = f32[512,128]{1,0:T(8,128)S(1)} collective-permute-done((f32[512,128]{1,0:T(8,128)S(1)}, f32[512,128]{1,0:T(8,128)S(1)}, u32[]{:S(2)}, u32[]{:S(2)}) %collective-permute-start.11) | collective-permute-done | bytes 262176 | tf_op jit(solution)/shard_map/ppermute | solution.py:497
  76.5 3.0 %gram.1 = (f32[320,1024]{1,0:T(8,128)S(1)}, f32[512,128]{1,0:T(8,128)S(1)}) custom-call(f32[224,128]{1,0:T(8,128)S(1)} %get-tuple-element.30.coef_ref, f32[512,128]{1,0:T(8,128)S(1)} %get-tuple-element.37.own_ref, f32[512,128]{1,0:T(8,128)S(1)} %get-tuple-element.38.my_ref, f32[64,128]{1,0:T(8,128)S(1)} %get-tuple-element.39.e_ref, ...), custom_call_target="tpu_custom_call" | custom-call | tf_op jit(solution)/shard_map/gram/pallas_call | solution.py:545
  79.6 19.7 %all_to_all.15 = f32[32,16,128]{2,1,0:T(8,128)S(1)} all-to-all(f32[32,16,128]{2,1,0:T(8,128)S(1)} %bitcast.17), channel_id=1, replica_groups=mesh['gx'=16,'gy'=8,'gz'=4] {'gy','gz'}, dimensions={0} | all-to-all | bytes 524288 | tf_op jit(solution)/shard_map/all_to_all | solution.py:555
  99.4 25.9 %all_to_all.16 = f32[16,16,128]{2,1,0:T(8,128)S(1)} all-to-all(f32[16,16,128]{2,1,0:T(8,128)S(1)} %broadcast_in_dim.6), channel_id=1, replica_groups=mesh['gx'=16,'gy'=8,'gz'=4] {'gx'}, dimensions={0} | all-to-all | bytes 262144 | tf_op jit(solution)/shard_map/all_to_all | solution.py:503
  125.3 15.7 %all_to_all.17 = f32[32,16,128]{2,1,0:T(8,128)S(1)} all-to-all(f32[32,16,128]{2,1,0:T(8,128)S(1)} %broadcast_in_dim.7), channel_id=1, replica_groups=mesh['gx'=16,'gy'=8,'gz'=4] {'gy','gz'}, dimensions={0} | all-to-all | bytes 524288 | tf_op jit(solution)/shard_map/all_to_all | solution.py:503
  141.0 12.5 %final.1 = (f32[512,128]{1,0:T(8,128)}, f32[512,128]{1,0:T(8,128)}) custom-call(f32[512,128]{1,0:T(8,128)S(1)} %bitcast.16, f32[320,1024]{1,0:T(8,128)S(1)} %get-tuple-element.41.basis_ref), custom_call_target="tpu_custom_call" | custom-call | tf_op jit(solution)/shard_map/final/pallas_call | solution.py:559
  (35 shorter events, 14.6 us)
Async XLA Ops:
  0.6 1.0 copy-start
  1.6 0.7 copy-start.2
  2.3 0.7 copy-start.4
  3.0 0.7 copy-start.6
  3.7 0.7 copy-start.7
  5.0 5.9 %collective-permute-start.1 = (f32[40,128]{1,0:T(8,128)S(1)}, f32[40,128]{1,0:T(8,128)S(1)}, u32[]{:S(2)}, u32[]{:S(2)}) collective-permute-start(f32[40,128]{1,0:T(8,128)S(1)} %get-tuple-element.24), channel_id=1, source_target_pairs={{1,0},{2,1},{3,2},{5,4},{6,5},{7,6},{9,8},{10,9},{11,10},{13,12},{... | collective-permute-start | bytes 61448 | tf_op jit(solution)/shard_map/ppermute | solution.py:497
  6.3 5.5 %collective-permute-start = (f32[40,128]{1,0:T(8,128)S(1)}, f32[40,128]{1,0:T(8,128)S(1)}, u32[]{:S(2)}, u32[]{:S(2)}) collective-permute-start(f32[40,128]{1,0:T(8,128)S(1)} %get-tuple-element.24), channel_id=1, source_target_pairs={{0,1},{1,2},{2,3},{4,5},{5,6},{6,7},{8,9},{9,10},{10,11},{12,13},{... | collective-permute-start | bytes 61448 | tf_op jit(solution)/shard_map/ppermute | solution.py:496
  11.8 5.6 %collective-permute-start.2 = (f32[296,128]{1,0:T(8,128)S(1)}, f32[296,128]{1,0:T(8,128)S(1)}, u32[]{:S(2)}, u32[]{:S(2)}) collective-permute-start(f32[296,128]{1,0:T(8,128)S(1)} %get-tuple-element.26), channel_id=1, source_target_pairs={{0,4},{4,8},{8,12},{12,16},{16,20},{20,24},{24,28},{1,5},{5,9},{9,... | collective-permute-start | bytes 454664 | tf_op jit(solution)/shard_map/ppermute | solution.py:496
  15.3 5.9 %collective-permute-start.3 = (f32[296,128]{1,0:T(8,128)S(1)}, f32[296,128]{1,0:T(8,128)S(1)}, u32[]{:S(2)}, u32[]{:S(2)}) collective-permute-start(f32[296,128]{1,0:T(8,128)S(1)} %get-tuple-element.27), channel_id=1, source_target_pairs={{4,0},{8,4},{12,8},{16,12},{20,16},{24,20},{28,24},{5,1},{9,5},{13... | collective-permute-start | bytes 454664 | tf_op jit(solution)/shard_map/ppermute | solution.py:497
  21.2 14.5 %collective-permute-start.5 = (f32[1120,128]{1,0:T(8,128)S(1)}, f32[1120,128]{1,0:T(8,128)S(1)}, u32[]{:S(2)}, u32[]{:S(2)}) collective-permute-start(f32[1120,128]{1,0:T(8,128)S(1)} %get-tuple-element.29.own_ref), channel_id=1, source_target_pairs={{32,0},{64,32},{96,64},{128,96},{160,128},{192,160},{224,192},{256... | collective-permute-start | bytes 1720328 | tf_op jit(solution)/shard_map/ppermute | solution.py:497
  29.6 8.6 %collective-permute-start.4 = (f32[1120,128]{1,0:T(8,128)S(1)}, f32[1120,128]{1,0:T(8,128)S(1)}, u32[]{:S(2)}, u32[]{:S(2)}) collective-permute-start(f32[1120,128]{1,0:T(8,128)S(1)} %get-tuple-element.29.own_ref), channel_id=1, source_target_pairs={{0,32},{32,64},{64,96},{96,128},{128,160},{160,192},{192,224},{224... | collective-permute-start | bytes 1720328 | tf_op jit(solution)/shard_map/ppermute | solution.py:496
  38.1 0.7 copy-start.3
  38.8 0.7 copy-start.5
  39.5 0.7 copy-start.8
  40.2 0.7 copy-start.9
  42.9 10.2 %collective-permute-start.7 = (f32[832,128]{1,0:T(8,128)S(1)}, f32[832,128]{1,0:T(8,128)S(1)}, u32[]{:S(2)}, u32[]{:S(2)}) collective-permute-start(f32[832,128]{1,0:T(8,128)S(1)} %get-tuple-element.31.own_ref.block_1), channel_id=1, source_target_pairs={{32,0},{64,32},{96,64},{128,96},{160,128},{192,160},{224,192},{256... | collective-permute-start | bytes 1277960 | tf_op jit(solution)/shard_map/ppermute | solution.py:497
  44.8 9.4 %collective-permute-start.6 = (f32[832,128]{1,0:T(8,128)S(1)}, f32[832,128]{1,0:T(8,128)S(1)}, u32[]{:S(2)}, u32[]{:S(2)}) collective-permute-start(f32[832,128]{1,0:T(8,128)S(1)} %get-tuple-element.31.own_ref.block_1), channel_id=1, source_target_pairs={{0,32},{32,64},{64,96},{96,128},{128,160},{160,192},{192,224},{224... | collective-permute-start | bytes 1277960 | tf_op jit(solution)/shard_map/ppermute | solution.py:496
  54.3 22.3 %copy-start.1 = (f32[64,1,8,128]{3,2,1,0:T(8,128)S(1)}, f32[64,1,8,128]{3,2,1,0:T(8,128)}, u32[]{:S(2)}) copy-start(f32[64,1,8,128]{3,2,1,0:T(8,128)} %param.7) | copy-start | bytes 786436
  55.5 9.3 %collective-permute-start.9 = (f32[672,128]{1,0:T(8,128)S(1)}, f32[672,128]{1,0:T(8,128)S(1)}, u32[]{:S(2)}, u32[]{:S(2)}) collective-permute-start(f32[672,128]{1,0:T(8,128)S(1)} %get-tuple-element.34.own_ref.block_2), channel_id=1, source_target_pairs={{32,0},{64,32},{96,64},{128,96},{160,128},{192,160},{224,192},{256... | collective-permute-start | bytes 1032200 | tf_op jit(solution)/shard_map/ppermute | solution.py:497
  57.4 8.6 %collective-permute-start.8 = (f32[672,128]{1,0:T(8,128)S(1)}, f32[672,128]{1,0:T(8,128)S(1)}, u32[]{:S(2)}, u32[]{:S(2)}) collective-permute-start(f32[672,128]{1,0:T(8,128)S(1)} %get-tuple-element.34.own_ref.block_2), channel_id=1, source_target_pairs={{0,32},{32,64},{64,96},{96,128},{128,160},{160,192},{192,224},{224... | collective-permute-start | bytes 1032200 | tf_op jit(solution)/shard_map/ppermute | solution.py:496
  66.9 8.4 %collective-permute-start.11 = (f32[512,128]{1,0:T(8,128)S(1)}, f32[512,128]{1,0:T(8,128)S(1)}, u32[]{:S(2)}, u32[]{:S(2)}) collective-permute-start(f32[512,128]{1,0:T(8,128)S(1)} %get-tuple-element.37.own_ref), channel_id=1, source_target_pairs={{32,0},{64,32},{96,64},{128,96},{160,128},{192,160},{224,192},{256... | collective-permute-start | bytes 786440 | tf_op jit(solution)/shard_map/ppermute | solution.py:497
  68.9 7.7 %collective-permute-start.10 = (f32[512,128]{1,0:T(8,128)S(1)}, f32[512,128]{1,0:T(8,128)S(1)}, u32[]{:S(2)}, u32[]{:S(2)}) collective-permute-start(f32[512,128]{1,0:T(8,128)S(1)} %get-tuple-element.37.own_ref), channel_id=1, source_target_pairs={{0,32},{32,64},{64,96},{96,128},{128,160},{160,192},{192,224},{224... | collective-permute-start | bytes 786440 | tf_op jit(solution)/shard_map/ppermute | solution.py:496

commit v3 on v2

v3 whole, which is shorter than its diff:
```python
import functools

import jax
import jax.numpy as jnp
from jax import lax
from jax.experimental import pallas as pl
from jax.experimental.pallas import tpu as pltpu
from jax.sharding import PartitionSpec as P

SHIFT = 7.5
SCALE = 3.0
LEVELS = 5
M = 64
HALF = M // 2
NEXTRA = 5
SLOT = HALF + NEXTRA
GROUPS = 16
TG = HALF // GROUPS
NE = 2 * TG + 1
HI = lax.Precision.HIGHEST


def iota_row():
    return lax.broadcasted_iota(jnp.int32, (8, 128), 0)


def iota_lane():
    return lax.broadcasted_iota(jnp.int32, (8, 128), 1)


def roll_lane(tile, shift):
    shift = shift % 128
    return tile if shift == 0 else pltpu.roll(tile, shift, 1)


def roll_row(tile, shift):
    shift = shift % 8
    return tile if shift == 0 else pltpu.roll(tile, shift, 0)


def swap_shift(first, second, roll, shift, mask):
    first, second = roll(first, shift), roll(second, shift)
    return jnp.where(mask, second, first), jnp.where(mask, first, second)


def tile(ref, index):
    if isinstance(index, int):
        return ref[8 * index : 8 * index + 8, :]
    return ref[pl.ds(pl.multiple_of(index * 8, 8), 8), :]


def put(ref, index, value):
    if isinstance(index, int):
        ref[8 * index : 8 * index + 8, :] = value
    else:
        ref[pl.ds(pl.multiple_of(index * 8, 8), 8), :] = value


def group_mask(lane, q):
    at = (lane + (4 - 8 * q)) & 127
    return at < 8


def core():
    return lax.rem(lax.axis_index("gx"), 2)


def pack_kernel(right_hbm, vel_hbm, decay_hbm, class_hbm, table_ref, send_ref, keep_ref, class_ref, sems):
    mine = pl.multiple_of(core() * 8 * HALF, 8)
    other = pl.multiple_of((1 - core()) * 8 * HALF, 8)
    copies = [
        (class_hbm, class_ref),
        (vel_hbm, keep_ref.at[pl.ds(8 * HALF, 24), :]),
        (decay_hbm, keep_ref.at[pl.ds(8 * (HALF + 3), 8), :]),
        (right_hbm.at[pl.ds(mine, 8 * HALF), :], keep_ref.at[pl.ds(0, 8 * HALF), :]),
        (right_hbm.at[pl.ds(other, 8 * HALF), :], send_ref.at[pl.ds(0, 8 * HALF), :]),
    ]
    copies = [pltpu.make_async_copy(src, dst, sems.at[i]) for i, (src, dst) in enumerate(copies)]
    for copy in copies:
        copy.start()
    for copy in copies:
        copy.wait()
    classes = class_ref[...]
    conduct = jnp.zeros((8, 128), jnp.float32)
    for index in range(table_ref.shape[0]):
        conduct = jnp.where(classes == index, table_ref[index], conduct)
    put(keep_ref, HALF + 4, conduct)
    put(send_ref, HALF + 4, conduct)
    for e in range(4):
        put(send_ref, HALF + e, tile(keep_ref, HALF + e))


def zmsg_kernel(keep_ref, got_ref, main_ref, zmsg_ref):
    lane = iota_lane()
    mine, other = core() * SLOT, (1 - core()) * SLOT
    for i in range(SLOT):
        put(main_ref, mine + i, tile(keep_ref, i))
        put(main_ref, other + i, tile(got_ref, i))

    def packed(indices):
        total = jnp.zeros((8, 128), jnp.float32)
        for q, index in enumerate(indices):
            total = jnp.where(group_mask(lane, q), roll_lane(tile(main_ref, index), 8 * q), total)
        return total

    for p in range(2):
        for t in range(TG):
            put(zmsg_ref, TG * p + t, packed([SLOT * p + GROUPS * t + q for q in range(GROUPS)]))
    put(zmsg_ref, NE - 1, packed([SLOT * p + HALF + e for p in range(2) for e in range(NEXTRA)]))


YPAIRS = (2 * SLOT + NE + 1) // 2


def ymsg_kernel(main_ref, low_ref, high_ref, up_ref, down_ref, edge_ref):
    row, lane = iota_row(), iota_lane()
    edges = []
    for t in range(NE):
        edge = jnp.where((lane & 7) >= 4, tile(low_ref, t), tile(high_ref, t))
        put(edge_ref, t, edge)
        edges.append(edge)

    def source(index):
        if index < 2 * SLOT:
            return tile(main_ref, index)
        return edges[min(index - 2 * SLOT, NE - 1)]

    lower = row < 4
    for g in range(YPAIRS):
        first, second = source(2 * g), roll_row(source(2 * g + 1), 4)
        put(up_ref, g, jnp.where(lower, second, first))
        put(down_ref, g, jnp.where(lower, first, second))


A_MY = SLOT
A_SECOND = 2 * SLOT
A_SECOND_MY = A_SECOND + HALF + 1
A_EDGE = A_SECOND_MY + HALF // 2 + 1
A_TILES = A_EDGE + 2 * NE
B_MY = HALF
B_EDGE = B_MY + HALF // 4
B_SECOND = B_EDGE + TG
B_TILES = B_SECOND + HALF


def xmsg_kernel(main_ref, edge_ref, below_ref, above_ref, my_ref, ey_ref, to_left_ref, to_right_ref):
    row = iota_row()
    lower = row < 4
    keep_2 = (row < 2) | (row >= 6)
    for g in range(YPAIRS):
        below, above = tile(below_ref, g), tile(above_ref, g)
        pair = (jnp.where(lower, above, below), roll_row(jnp.where(lower, below, above), 4))
        for half in range(2):
            index = 2 * g + half
            if index < 2 * SLOT:
                put(my_ref, index, pair[half])
                p, i = divmod(index, SLOT)
                put((to_left_ref, to_right_ref)[p], A_MY + i, pair[half])
                if i == SLOT - 1:
                    put((to_right_ref, to_left_ref)[p], A_SECOND_MY + HALF // 2, pair[half])
            elif index < 2 * SLOT + NE:
                put(ey_ref, index - 2 * SLOT, pair[half])
                for ref in (to_left_ref, to_right_ref):
                    put(ref, A_EDGE + NE + index - 2 * SLOT, pair[half])
    for p, (adjacent, second) in enumerate(((to_left_ref, to_right_ref), (to_right_ref, to_left_ref))):
        for i in range(SLOT):
            value = tile(main_ref, SLOT * p + i)
            put(adjacent, i, value)
            if i < HALF:
                put(second, A_SECOND + i, value)
            elif i == SLOT - 1:
                put(second, A_SECOND + HALF, value)
        for i in range(HALF // 2):
            value = jnp.where(
                keep_2,
                tile(my_ref, SLOT * p + 2 * i),
                roll_row(tile(my_ref, SLOT * p + 2 * i + 1), 4),
            )
            put(second, A_SECOND_MY + i, value)
    for t in range(NE):
        value = tile(edge_ref, t)
        put(to_left_ref, A_EDGE + t, value)
        put(to_right_ref, A_EDGE + t, value)


def plane_coefficients(sizes, cells_ref, rate_ref, conduct_ref, given_ref, coef_ref):
    row, lane = iota_row(), iota_lane()
    size_x, size_y, size_z = sizes
    first_x = lax.axis_index("gx") - core() - 1
    at_y, at_z = lax.axis_index("gy"), lax.axis_index("gz")
    y_main = at_y * 8 + row
    y_my = at_y * 8 + jnp.where(row < 4, row + 8, row - 8)
    z_main = at_z * 128 + lane
    z_edge = at_z * 128 + jnp.where(lane < 64, lane + 128, lane - 128)
    where = ((y_main, z_main), (y_my, z_main), (y_main, z_edge), (y_my, z_edge))

    def shift_y(four, shift, mask):
        main, my = swap_shift(four[0], four[1], roll_row, shift, mask)
        edge, ey = swap_shift(four[2], four[3], roll_row, shift, mask)
        return [main, my, edge, ey]

    def shift_z(four, shift, mask):
        main, edge = swap_shift(four[0], four[2], roll_lane, shift, mask)
        my, ey = swap_shift(four[1], four[3], roll_lane, shift, mask)
        return [main, my, edge, ey]

    def plane(s, carry):
        center = [tile(conduct_ref, (s + 1) * 4 + part) for part in range(4)]
        before = [tile(conduct_ref, s * 4 + part) for part in range(4)]
        after = [tile(conduct_ref, (s + 2) * 4 + part) for part in range(4)]
        plus = [after, shift_y(center, -1, row == 7), shift_z(center, -1, lane == 127)]
        minus = [before, shift_y(center, 1, row == 0), shift_z(center, 1, lane == 0)]
        at_x = first_x + s
        x_inside = (at_x >= 0) & (at_x < size_x)
        for part, (y_at, z_at) in enumerate(where):
            flat = (at_x * size_y + y_at) * size_z + z_at
            wells = jnp.zeros((8, 128), jnp.float32)
            for w in range(cells_ref.shape[0]):
                wells = wells + jnp.where(flat == cells_ref[w], rate_ref[w], 0.0)
            inside = (y_at >= 0) & (y_at < size_y) & (z_at >= 0) & (z_at < size_z) & x_inside
            if part >= 2:
                inside = inside & ((lane < 4) | (lane >= 124))
            given = [tile(given_ref, (s * 4 + e) * 4 + part) for e in range(4)]
            diagonal = given[3] + wells
            values = []
            for d in range(3):
                plus_face = 0.5 * (center[part] + plus[d][part])
                minus_face = 0.5 * (center[part] + minus[d][part])
                diagonal = diagonal + (given[d] + plus_face + minus_face)
                values += [(given[d] + plus_face) * (-1.0 / SCALE), minus_face * (-1.0 / SCALE)]
            for index, value in enumerate([(diagonal - SHIFT) * (1.0 / SCALE)] + values):
                value = jnp.where(inside, value, 0.0)
                if part >= 2:
                    for shift in (8, 16, 32, 64):
                        value = value + roll_lane(value, shift)
                put(coef_ref, (s * 7 + index) * 4 + part, value)
        return carry

    lax.fori_loop(0, 4, plane, 0)


def step(source, target, coef_ref, first, count, coef_shift, out_shift, with_my=True, with_em=True, with_ey=True):
    main_ref, my_ref, em_ref, ey_ref = source
    row, lane = iota_row(), iota_lane()
    row_0, row_7 = row == 0, row == 7
    lane_0, lane_127 = lane == 0, lane == 127

    def block(i, carry):
        s, t = first + lax.div(i, TG), lax.rem(i, TG)

        def apply(part, center, after, before, y_plus, y_minus, z_plus, z_minus):
            def coef(index):
                return tile(coef_ref, ((s + coef_shift) * 7 + index) * 4 + part)

            total = coef(0) * center + (coef(1) * after + coef(2) * before)
            total = total + (coef(3) * y_plus + coef(4) * y_minus)
            return total + (coef(5) * z_plus + coef(6) * z_minus)

        at_field, at_edge = s * HALF + t * GROUPS, s * TG + t
        out_field, out_edge = (s + out_shift) * HALF + t * GROUPS, (s + out_shift) * TG + t
        em = tile(em_ref, at_edge)
        ey = tile(ey_ref, at_edge) if with_em or with_my else None
        near_m = jnp.zeros((8, 128), jnp.float32)
        near_y = jnp.zeros((8, 128), jnp.float32)
        for q in range(GROUPS):
            f = at_field + q
            main, my = tile(main_ref, f), tile(my_ref, f)
            beside = roll_lane(em, -8 * q)
            z_plus = roll_lane(jnp.where(lane_0, beside, main), -1)
            z_minus = roll_lane(jnp.where(lane_127, beside, main), 1)
            y_plus, my_plus = swap_shift(main, my, roll_row, -1, row_7)
            y_minus, my_minus = swap_shift(main, my, roll_row, 1, row_0)
            after, before = tile(main_ref, f + HALF), tile(main_ref, f - HALF)
            put(target[0], out_field + q, apply(0, main, after, before, y_plus, y_minus, z_plus, z_minus))
            at = ((lane + (1 - 8 * q)) & 127) < 2
            if with_em:
                near_m = jnp.where(at, roll_lane(main, 8 * q), near_m)
            if with_ey:
                near_y = jnp.where(at, roll_lane(my, 8 * q), near_y)
            if with_my:
                beside = roll_lane(ey, -8 * q)
                z_plus = roll_lane(jnp.where(lane_0, beside, my), -1)
                z_minus = roll_lane(jnp.where(lane_127, beside, my), 1)
                after, before = tile(my_ref, f + HALF), tile(my_ref, f - HALF)
                put(target[1], out_field + q, apply(1, my, after, before, my_plus, my_minus, z_plus, z_minus))
        seven, zero = (lane & 7) == 7, (lane & 7) == 0
        if with_em:
            em_plus, ey_plus = swap_shift(em, ey, roll_row, -1, row_7)
            em_minus, ey_minus = swap_shift(em, ey, roll_row, 1, row_0)
            z_plus = jnp.where(seven, roll_lane(near_m, -1), roll_lane(em, -1))
            z_minus = jnp.where(zero, roll_lane(near_m, 1), roll_lane(em, 1))
            after, before = tile(em_ref, at_edge + TG), tile(em_ref, at_edge - TG)
            put(target[2], out_edge, apply(2, em, after, before, em_plus, em_minus, z_plus, z_minus))
        if with_ey:
            z_plus = jnp.where(seven, roll_lane(near_y, -1), roll_lane(ey, -1))
            z_minus = jnp.where(zero, roll_lane(near_y, 1), roll_lane(ey, 1))
            after, before = tile(ey_ref, at_edge + TG), tile(ey_ref, at_edge - TG)
            put(target[3], out_edge, apply(3, ey, after, before, ey_plus, ey_minus, z_plus, z_minus))
        return carry

    lax.fori_loop(0, count * TG, block, 0)


def copy_tiles(source, at, target, to, count):
    for i in range(count):
        put(target, to + i, tile(source, at + i))


def first_two_kernel(
    sizes,
    cells_ref,
    rate_ref,
    main_ref,
    edge_ref,
    my_ref,
    ey_ref,
    left_ref,
    right_ref,
    coef_ref,
    block_1_ref,
    block_2_ref,
    my_2_ref,
    em_2_ref,
    ey_2_ref,
    to_left_ref,
    to_right_ref,
    conduct_ref,
    given_ref,
    main_0,
    my_0,
    em_0,
    ey_0,
    main_1,
    my_1,
    em_1,
    ey_1,
):
    row = iota_row()
    for p in range(2):
        copy_tiles(main_ref, SLOT * p, main_0, HALF * (2 + p), HALF)
        copy_tiles(my_ref, SLOT * p, my_0, HALF * (2 + p), HALF)
        copy_tiles(edge_ref, TG * p, em_0, TG * (2 + p), TG)
        copy_tiles(ey_ref, TG * p, ey_0, TG * (2 + p), TG)
    extras = {2: (main_ref, HALF, my_ref, HALF, edge_ref, NE - 1, ey_ref, NE - 1, 0)}
    extras[3] = (main_ref, SLOT + HALF, my_ref, SLOT + HALF, edge_ref, NE - 1, ey_ref, NE - 1, NEXTRA)
    for ref, adjacent, second, p in ((left_ref, 1, 0, 1), (right_ref, 4, 5, 0)):
        copy_tiles(ref, 0, main_0, HALF * adjacent, HALF)
        copy_tiles(ref, A_MY, my_0, HALF * adjacent, HALF)
        copy_tiles(ref, A_SECOND, main_0, HALF * second, HALF)
        for i in range(HALF // 2):
            value = tile(ref, A_SECOND_MY + i)
            put(my_0, HALF * second + 2 * i, value)
            put(my_0, HALF * second + 2 * i + 1, roll_row(value, 4))
        for plane, at in ((adjacent, p), (second, 1 - p)):
            copy_tiles(ref, A_EDGE + TG * at, em_0, TG * plane, TG)
            copy_tiles(ref, A_EDGE + NE + TG * at, ey_0, TG * plane, TG)
        em_at, ey_at = A_EDGE + NE - 1, A_EDGE + 2 * NE - 1
        extras[adjacent] = (ref, HALF, ref, A_MY + HALF, ref, em_at, ref, ey_at, NEXTRA * p)
        for part, value in enumerate(
            (
                tile(ref, A_SECOND + HALF),
                tile(ref, A_SECOND_MY + HALF // 2),
                roll_lane(tile(ref, em_at), -8 * (NEXTRA * (1 - p) + 4)),
                roll_lane(tile(ref, ey_at), -8 * (NEXTRA * (1 - p) + 4)),
            )
        ):
            put(conduct_ref, 4 * second + part, value)
    for plane, (a, a_at, b, b_at, c, c_at, d, d_at, q) in extras.items():
        for e in range(NEXTRA):
            values = (
                tile(a, a_at + e),
                tile(b, b_at + e),
                roll_lane(tile(c, c_at), -8 * (q + e)),
                roll_lane(tile(d, d_at), -8 * (q + e)),
            )
            for part, value in enumerate(values):
                if e == NEXTRA - 1:
                    put(conduct_ref, 4 * plane + part, value)
                else:
                    put(given_ref, ((plane - 1) * 4 + e) * 4 + part, value)
    plane_coefficients(sizes, cells_ref, rate_ref, conduct_ref, given_ref, coef_ref)
    step((main_0, my_0, em_0, ey_0), (main_1, my_1, em_1, ey_1), coef_ref, 1, 4, -1, -1)
    copy_tiles(main_1, HALF, block_1_ref, 0, 2 * HALF)
    step((main_1, my_1, em_1, ey_1), (block_2_ref, my_2_ref, em_2_ref, ey_2_ref), coef_ref, 1, 2, 0, -1)
    for p, (adjacent, second) in enumerate(((to_left_ref, to_right_ref), (to_right_ref, to_left_ref))):
        for i in range(HALF):
            value = tile(block_2_ref, HALF * p + i)
            put(adjacent, i, value)
            put(second, B_SECOND + i, value)
        for i in range(HALF // 4):
            value = tile(my_2_ref, HALF * p + 4 * i)
            for k in range(1, 4):
                at_row = ((row + (1 - 2 * k)) & 7) < 2
                value = jnp.where(at_row, roll_row(tile(my_2_ref, HALF * p + 4 * i + k), 2 * k), value)
            put(adjacent, B_MY + i, value)
        copy_tiles(em_2_ref, TG * p, adjacent, B_EDGE, TG)


def last_two_kernel(
    coef_ref,
    block_1_ref,
    block_2_ref,
    my_2_ref,
    em_2_ref,
    ey_2_ref,
    left_ref,
    right_ref,
    keep_ref,
    send_ref,
    main_2,
    my_2,
    em_2,
    ey_2,
    main_3,
    my_3,
    em_3,
    main_4,
):
    copy_tiles(block_2_ref, 0, main_2, 2 * HALF, 2 * HALF)
    copy_tiles(my_2_ref, 0, my_2, 2 * HALF, 2 * HALF)
    copy_tiles(em_2_ref, 0, em_2, 2 * TG, 2 * TG)
    copy_tiles(ey_2_ref, 0, ey_2, 2 * TG, 2 * TG)
    for ref, adjacent, second in ((left_ref, 1, 0), (right_ref, 4, 5)):
        copy_tiles(ref, 0, main_2, HALF * adjacent, HALF)
        for i in range(HALF // 4):
            value = tile(ref, B_MY + i)
            for k in range(4):
                put(my_2, HALF * adjacent + 4 * i + k, roll_row(value, -2 * k))
        copy_tiles(ref, B_EDGE, em_2, TG * adjacent, TG)
        copy_tiles(ref, B_SECOND, main_2, HALF * second, HALF)
    source, target = (main_2, my_2, em_2, ey_2), (main_3, my_3, em_3, None)
    for plane in (1, 4):
        step(source, target, coef_ref, plane, 1, -1, -1, False, False, False)
    step(source, target, coef_ref, 2, 2, -1, -1, True, True, False)
    step((main_3, my_3, em_3, None), (main_4, None, None, None), coef_ref, 1, 2, 0, -1, False, False, False)
    mine, other = core() * HALF, (1 - core()) * HALF
    for level, (ref, base) in enumerate(((block_1_ref, 0), (block_2_ref, 0), (main_3, HALF), (main_4, 0))):
        for i in range(HALF):
            put(keep_ref, HALF * level + i, tile(ref, base + mine + i))
            put(send_ref, HALF * level + i, tile(ref, base + other + i))


PAIRS = (
    ((0, 0), (0, 1)),
    ((0, 2), (0, 3)),
    ((1, 1), (1, 2)),
    ((1, 3), (1, 4)),
    ((2, 2), (2, 3)),
    ((3, 3), (3, 4)),
    ((4, 4), (2, 4)),
    ((0, 4), None),
)


def dot_nt(first, second):
    return lax.dot_general(first, second, (((1,), (1,)), ((), ())), precision=HI, preferred_element_type=jnp.float32)


def dot_tn(first, second):
    return lax.dot_general(first, second, (((0,), (0,)), ((), ())), precision=HI, preferred_element_type=jnp.float32)


def dot_nn(first, second):
    return lax.dot_general(first, second, (((1,), (0,)), ((), ())), precision=HI, preferred_element_type=jnp.float32)


def gram_kernel(block_0, keep_ref, got_ref, basis_ref, gram_ref):
    mine, other = core() * HALF, (1 - core()) * HALF
    for y in range(8):
        lanes = slice(128 * y, 128 * (y + 1))
        basis_ref[0:M, lanes] = block_0[pl.ds(y, M, stride=8), :]
        for level in range(1, LEVELS):
            at = pl.ds(8 * HALF * (level - 1) + y, HALF, stride=8)
            basis_ref[pl.ds(pl.multiple_of(M * level + mine, 8), HALF), lanes] = keep_ref[at, :]
            basis_ref[pl.ds(pl.multiple_of(M * level + other, 8), HALF), lanes] = got_ref[at, :]
    full = dot_nt(basis_ref[...], basis_ref[...])
    for index, pair in enumerate(PAIRS):
        for half, at in enumerate(pair):
            if at is None:
                value = jnp.zeros((M, M), jnp.float32)
            else:
                value = full[M * at[0] : M * at[0] + M, M * at[1] : M * at[1] + M]
            gram_ref[M * index : M * (index + 1), M * half : M * (half + 1)] = value


def eliminate(matrix, wanted):
    both = jnp.concatenate([matrix, wanted], axis=1)
    tiles = [both[8 * i : 8 * i + 8, :] for i in range(M // 8)]
    rows = iota_row()

    def column(value, at):
        return jnp.broadcast_to(value[:, at : at + 1], (8, 128))

    for i in range(M // 8):
        columns = [[column(t, 8 * i + b) for b in range(8)] for t in tiles]
        row = [jnp.broadcast_to(tiles[i][a : a + 1, :], (8, 128)) for a in range(8)]
        small = [
            [jnp.broadcast_to(columns[i][b][a : a + 1, :], (8, 128)) for b in range(8)]
            for a in range(8)
        ]
        for p in range(8):
            inverse = 1.0 / small[p][p]
            for a in range(p + 1, 8):
                factor = small[a][p] * inverse
                row[a] = row[a] - factor * row[p]
                for b in range(p + 1, 8):
                    small[a][b] = small[a][b] - factor * small[p][b]
            row[p] = row[p] * inverse
            for b in range(p + 1, 8):
                small[p][b] = small[p][b] * inverse
        for p in range(7, 0, -1):
            for a in range(p):
                row[a] = row[a] - small[a][p] * row[p]
        for j in range(M // 8):
            if j == i:
                value = row[0]
                for b in range(1, 8):
                    value = jnp.where(rows == b, row[b], value)
            else:
                value = tiles[j]
                for b in range(8):
                    value = value - columns[j][b] * row[b]
            tiles[j] = value
    return jnp.concatenate(tiles, axis=0)[:, M:]


def apply_levels(blocks):
    out = [SHIFT * b for b in blocks] + [None]
    for j, b in enumerate(blocks):
        out[j + 1] = SCALE * b if out[j + 1] is None else out[j + 1] + SCALE * b
    return out


def pad_levels(blocks, count):
    return list(blocks) + [jnp.zeros((M, M), jnp.float32)] * (count - len(blocks))


def final_kernel(gram_ref, basis_ref, field_ref, resid_ref, full_ref):
    for index, pair in enumerate(PAIRS):
        for half, at in enumerate(pair):
            if at is None:
                continue
            value = gram_ref[M * index : M * (index + 1), M * half : M * (half + 1)]
            full_ref[M * at[0] : M * at[0] + M, M * at[1] : M * at[1] + M] = value
            if at[0] != at[1]:
                full_ref[M * at[1] : M * at[1] + M, M * at[0] : M * at[0] + M] = value.T
    eye = jnp.where(
        lax.broadcasted_iota(jnp.int32, (M, M), 0) == lax.broadcasted_iota(jnp.int32, (M, M), 1), 1.0, 0.0
    ).astype(jnp.float32)

    def gram(levels, blocks):
        count = M * levels
        return dot_nn(full_ref[0:count, 0 : M * len(blocks)], jnp.concatenate(blocks, axis=0))

    def minimal(half, second):
        levels = len(second)
        product = gram(levels, second)
        cross = sum(product[M * j : M * j + M] * b for j, b in enumerate(half))
        square = sum(product[M * j : M * j + M] * b for j, b in enumerate(second))
        return jnp.sum(cross) / jnp.sum(square), product[0:M]

    image_gram = SHIFT * full_ref[0:M, 0:M] + SCALE * full_ref[0:M, M : 2 * M]
    inverse = eliminate(dot_tn(image_gram, image_gram), image_gram.T)
    alpha = dot_nn(inverse, full_ref[0:M, 0:M])
    half = [eye - SHIFT * alpha, -SCALE * alpha]
    second = apply_levels(half)
    omega, second_gram = minimal(half, second)
    field = [alpha + omega * half[0], omega * half[1]]
    resid = [half[0] - omega * second[0], half[1] - omega * second[1], -omega * second[2]]
    beta = -dot_nn(inverse, second_gram)
    direct = [
        resid[0] + (1.0 - omega * SHIFT) * beta,
        resid[1] - (omega * SCALE) * beta,
        resid[2],
    ]
    image = apply_levels(direct)
    stacked = jnp.concatenate(
        [jnp.concatenate(image, axis=0), jnp.concatenate(pad_levels(resid, 4), axis=0)], axis=1
    )
    both = dot_nn(full_ref[0:M, 0 : 4 * M], stacked)
    image_gram, resid_gram = both[:, 0:M], both[:, M:]
    inverse = eliminate(dot_tn(image_gram, image_gram), image_gram.T)
    alpha = dot_nn(inverse, resid_gram)
    product = dot_nn(jnp.concatenate(image + direct, axis=0), alpha)
    half = [r - product[M * j : M * j + M] for j, r in enumerate(pad_levels(resid, 4))]
    second = apply_levels(half)
    omega, _ = minimal(half, second)
    field = pad_levels(field, 4)
    moved = [product[M * (4 + j) : M * (5 + j)] for j in range(3)] + [None]
    field = [
        f + omega * h + (0.0 if m is None else m) for f, h, m in zip(field, half, moved)
    ]
    field = pad_levels(field, 5)
    resid = [h - omega * s for h, s in zip(pad_levels(half, 5), second)]
    coefs = jnp.concatenate([jnp.concatenate(field, axis=0), jnp.concatenate(resid, axis=0)], axis=1)
    for y in range(8):
        result = dot_tn(coefs, basis_ref[:, 128 * y : 128 * (y + 1)])
        field_ref[pl.ds(y, M, stride=8), :] = result[0:M]
        resid_ref[pl.ds(y, M, stride=8), :] = result[M:]


VMEM = pl.BlockSpec(memory_space=pltpu.VMEM)
SMEM = pl.BlockSpec(memory_space=pltpu.SMEM)


def f32(*shape):
    return jax.ShapeDtypeStruct(shape, jnp.float32)


def call(kernel, name, outs, specs, scratch=()):
    return pl.pallas_call(
        kernel,
        name=name,
        out_shape=outs,
        in_specs=specs,
        out_specs=tuple(VMEM for _ in outs) if isinstance(outs, tuple) else VMEM,
        scratch_shapes=list(scratch),
        compiler_params=pltpu.CompilerParams(vmem_limit_bytes=32 * 1024 * 1024),
    )


def from_sides(axis, up, down, by=1):
    count = lax.axis_size(axis)
    lower = lax.ppermute(up, axis, [(i, i + by) for i in range(count - by)])
    upper = lax.ppermute(down, axis, [(i + by, i) for i in range(count - by)])
    return lower, upper


def spread(values, axes):
    count = lax.axis_size(axes)
    return lax.all_to_all(jnp.broadcast_to(values, (count, *values.shape)), axes, 0, 0)


def other_core(values):
    count = lax.axis_size("gx")
    return lax.ppermute(values, "gx", [(i, i ^ 1) for i in range(count)])


def tiles(count):
    return f32(8 * count, 128)


def scratch(*counts):
    return [pltpu.VMEM((8 * count, 128), jnp.float32) for count in counts]


def per_device(right_side, velocity, decay_rate, perm_class, conductivity, well_cells, well_rate):
    sizes = (lax.axis_size("gx"), 8 * lax.axis_size("gy"), 128 * lax.axis_size("gz"))
    block_0 = right_side.reshape(8 * M, 128)
    any_space = pl.BlockSpec(memory_space=pl.ANY)

    send, keep = call(
        pack_kernel,
        "pack",
        (tiles(SLOT), tiles(SLOT)),
        [any_space] * 4 + [SMEM],
        [pltpu.VMEM((8, 128), jnp.int32), pltpu.SemaphoreType.DMA((5,))],
    )(block_0, velocity.reshape(24, 128), decay_rate.reshape(8, 128), perm_class.reshape(8, 128), conductivity)
    got = other_core(send)
    main, zmsg = call(zmsg_kernel, "zmsg", (tiles(2 * SLOT), tiles(NE)), [VMEM] * 2)(keep, got)
    low, high = from_sides("gz", zmsg, zmsg)
    up, down, edge = call(ymsg_kernel, "ymsg", (tiles(YPAIRS), tiles(YPAIRS), tiles(NE)), [VMEM] * 3)(
        main, low, high
    )
    below, above = from_sides("gy", up, down)
    my, ey, to_left, to_right = call(
        xmsg_kernel, "xmsg", (tiles(2 * SLOT), tiles(NE), tiles(A_TILES), tiles(A_TILES)), [VMEM] * 4
    )(main, edge, below, above)
    left, right = from_sides("gx", to_right, to_left, 2)
    coef, block_1, block_2, my, em, ey, to_left, to_right = call(
        functools.partial(first_two_kernel, sizes),
        "first_two",
        (
            tiles(4 * 28),
            tiles(M),
            tiles(M),
            tiles(M),
            tiles(2 * TG),
            tiles(2 * TG),
            tiles(B_TILES),
            tiles(B_TILES),
        ),
        [SMEM, SMEM] + [VMEM] * 6,
        scratch(24, 64, 6 * HALF, 6 * HALF, 6 * TG, 6 * TG, 4 * HALF, 4 * HALF, 4 * TG, 4 * TG),
    )(well_cells, well_rate, main, edge, my, ey, left, right)
    left, right = from_sides("gx", to_right, to_left, 2)
    keep, send = call(
        last_two_kernel,
        "last_two",
        (tiles(4 * HALF), tiles(4 * HALF)),
        [VMEM] * 8,
        scratch(6 * HALF, 6 * HALF, 6 * TG, 6 * TG, 4 * HALF, 4 * HALF, 4 * TG, 2 * HALF),
    )(coef, block_1, block_2, my, em, ey, left, right)
    got = other_core(send)
    basis, gram = call(gram_kernel, "gram", (f32(LEVELS * M, 1024), f32(8 * M, 128)), [VMEM] * 3)(
        block_0, keep, got
    )

    plane = ("gy", "gz")
    count = lax.axis_size(plane)
    gram = lax.all_to_all(gram.reshape(count, -1, 128), plane, 0, 0)
    gram = jnp.sum(gram, axis=0)
    gram = jnp.sum(spread(gram, "gx"), axis=0)
    gram = spread(gram, plane).reshape(8 * M, 128)
    field, resid = call(
        final_kernel,
        "final",
        (f32(8 * M, 128), f32(8 * M, 128)),
        [VMEM, VMEM],
        [pltpu.VMEM((LEVELS * M, LEVELS * M), jnp.float32)],
    )(gram, basis)
    return field.reshape(right_side.shape), resid.reshape(right_side.shape)


def solution(mesh):
    placed = (
        P(None, "gx", "gy", "gz"),
        P(None, "gx", "gy", "gz"),
        P("gx", "gy", "gz"),
        P("gx", "gy", "gz"),
        P(),
        P(),
        P(),
    )
    return jax.shard_map(
        per_device,
        mesh=mesh,
        in_specs=placed,
        out_specs=(P(None, "gx", "gy", "gz"), P(None, "gx", "gy", "gz")),
        check_vma=False,
    )
```

time: 154 us -> 144 us (0.935)
  starting transfers between devices: 39.8 us -> 31.3 us
  blocking collectives: 61.4 us -> 55.3 us
  Pallas kernels: 20.4 us -> 24.4 us
  waiting for transfers between devices: 24.7 us -> 28 us
  local copies, waits for them, and re-layouts: 6.41 us -> 3.73 us
    ppermute x12 -> x10, starting transfers between devices: 39.8 us -> 31.3 us  [the longest x2 15.7 us: other_core(): return lax.ppermute(values, 'gx', [(i, i ^ 1) for i in range(count)])]
    all_to_all x2, blocking collectives: 41.6 us -> 33.5 us  [spread(): lax.all_to_all(jnp.broadcast_to(values, (count, *values.shape)), axes, 0, 0)]
    pallas_call x6, Pallas kernels: 4.94 us -> 9.42 us  [the longest x1 5.78 us: per_device(): call(functools.partial(first_two_kernel, sizes), 'first_two', (tiles(4 *...]
    ppermute x12 -> x10, waiting for transfers between devices: 24.7 us -> 28 us  [the longest x4 13.2 us: from_sides(): upper = lax.ppermute(down, axis, [(i + by, i) for i in range(count - by)])]
    unnamed x20 -> x16, local copies, waits for them, and re-layouts: 6.38 us -> 3.7 us
    all_to_all x1, blocking collectives: 19.7 us -> 21.8 us  [per_device(): gram = lax.all_to_all(gram.reshape(count, -1, 128), plane, 0, 0)]
  transfers between devices with their start and end apart: 12 -> 10, of which waited for: 11 -> 9; matrix products, arithmetic and copies ran while one was open for 0% -> 0% of each run, Pallas kernels for 0% -> 0%
where the time goes in v3:
time: 144 us
  blocking collectives  55.3 us (38%)
  starting transfers between devices  31.3 us (22%)
  waiting for transfers between devices  28 us (19%)
  Pallas kernels  24.4 us (17%)
  local copies, waits for them, and re-layouts  3.73 us (3%)
    all_to_all x2, blocking collectives, spread(): lax.all_to_all(jnp.broadcast_to(values, (count, *values.shape)), axes, 0, 0)  33.5 us
    all_to_all x1, blocking collectives, per_device(): gram = lax.all_to_all(gram.reshape(count, -1, 128), plane, 0, 0)  21.8 us
    ppermute x2, starting transfers between devices, other_core(): return lax.ppermute(values, 'gx', [(i, i ^ 1) for i in range(count)])  15.7 us
    ppermute x4, waiting for transfers between devices, from_sides(): upper = lax.ppermute(down, axis, [(i + by, i) for i in range(count - by)])  13.2 us
    pallas_call x1, Pallas kernels, per_device(): call(final_kernel, 'final', (f32(8 * M, 128), f32(8 * M, 128)), [VMEM, VM...  12.5 us
    ppermute x4, waiting for transfers between devices, from_sides(): lower = lax.ppermute(up, axis, [(i, i + by) for i in range(count - by)])  12.3 us
    ppermute x4, starting transfers between devices, from_sides(): lower = lax.ppermute(up, axis, [(i, i + by) for i in range(count - by)])  10.5 us
    pallas_call x1, Pallas kernels, per_device(): call(functools.partial(first_two_kernel, sizes), 'first_two', (tiles(4 *...  5.78 us
  transfers between devices with their start and end apart: 10, of which 9 were waited for; matrix products, arithmetic and copies ran while one was open for 0% of the time, Pallas kernels for 0%

profile of v3, /device:TPU:1, one launch (start us, length us, event | category | flops | bytes accessed | tf_op | source)
XLA Modules:
  0.0 143.6 jit_solution(15828202574633050324)
XLA Ops:
  5.3 8.8 %collective-permute-start = (f32[296,128]{1,0:T(8,128)S(1)}, f32[296,128]{1,0:T(8,128)S(1)}, u32[]{:S(2)}, u32[]{:S(2)}) collective-permute-start(f32[296,128]{1,0:T(8,128)S(1)} %get-tuple-element.28), channel_id=1, source_target_pairs={{0,32},{32,0},{64,96},{96,64},{128,160},{160,128},{192,224},{224,1... | collective-permute-start | bytes 454664 | tf_op jit(solution)/shard_map/ppermute | solution.py:636
  14.1 1.0 collective-permute-done.got_ref
  15.3 1.3 collective-permute-start.2
  16.6 4.0 %collective-permute-start.1 = (f32[40,128]{1,0:T(8,128)S(1)}, f32[40,128]{1,0:T(8,128)S(1)}, u32[]{:S(2)}, u32[]{:S(2)}) collective-permute-start(f32[40,128]{1,0:T(8,128)S(1)} %get-tuple-element.30), channel_id=1, source_target_pairs={{0,1},{1,2},{2,3},{4,5},{5,6},{6,7},{8,9},{9,10},{10,11},{12,13},{... | collective-permute-start | bytes 61448 | tf_op jit(solution)/shard_map/ppermute | solution.py:624
  21.5 1.3 collective-permute-start.3
  22.8 1.3 collective-permute-start.4
  25.1 3.8 %collective-permute-done.4.above_ref = f32[320,128]{1,0:T(8,128)S(1)} collective-permute-done((f32[320,128]{1,0:T(8,128)S(1)}, f32[320,128]{1,0:T(8,128)S(1)}, u32[]{:S(2)}, u32[]{:S(2)}) %collective-permute-start.4) | collective-permute-done | bytes 163872 | tf_op jit(solution)/shard_map/ppermute | solution.py:625
  29.0 1.3 collective-permute-start.5
  30.3 1.3 collective-permute-start.6
  31.6 8.0 %collective-permute-done.5.left_ref = f32[1072,128]{1,0:T(8,128)S(1)} collective-permute-done((f32[1072,128]{1,0:T(8,128)S(1)}, f32[1072,128]{1,0:T(8,128)S(1)}, u32[]{:S(2)}, u32[]{:S(2)}) %collective-permute-start.5) | collective-permute-done | bytes 548896 | tf_op jit(solution)/shard_map/ppermute | solution.py:624
  39.6 3.7 %collective-permute-done.6.right_ref = f32[1072,128]{1,0:T(8,128)S(1)} collective-permute-done((f32[1072,128]{1,0:T(8,128)S(1)}, f32[1072,128]{1,0:T(8,128)S(1)}, u32[]{:S(2)}, u32[]{:S(2)}) %collective-permute-start.6) | collective-permute-done | bytes 548896 | tf_op jit(solution)/shard_map/ppermute | solution.py:625
  43.4 5.8 %first_two.1 = (f32[896,128]{1,0:T(8,128)S(1)}, f32[512,128]{1,0:T(8,128)S(1)}, f32[512,128]{1,0:T(8,128)S(1)}, f32[512,128]{1,0:T(8,128)S(1)}, f32[32,128]{1,0:...) custom-call(s32[32]{0:T(128)S(1)} %copy-done.6, f32[32]{0:T(128)S(1)} %copy-done.7, ...), custom_call_target="tpu_custom_call" | custom-call | tf_op jit(solution)/shard_map/first_two/pallas_call | solution.py:670
  49.2 3.9 %collective-permute-start.7 = (f32[592,128]{1,0:T(8,128)S(1)}, f32[592,128]{1,0:T(8,128)S(1)}, u32[]{:S(2)}, u32[]{:S(2)}) collective-permute-start(f32[592,128]{1,0:T(8,128)S(1)} %get-tuple-element.44), channel_id=1, source_target_pairs={{0,64},{32,96},{64,128},{96,160},{128,192},{160,224},{192,256},{22... | collective-permute-start | bytes 909320 | tf_op jit(solution)/shard_map/ppermute | solution.py:624
  53.0 1.3 collective-permute-start.8
  54.3 2.4 %collective-permute-done.7.left_ref = f32[592,128]{1,0:T(8,128)S(1)} collective-permute-done((f32[592,128]{1,0:T(8,128)S(1)}, f32[592,128]{1,0:T(8,128)S(1)}, u32[]{:S(2)}, u32[]{:S(2)}) %collective-permute-start.7) | collective-permute-done | bytes 303136 | tf_op jit(solution)/shard_map/ppermute | solution.py:624
  56.8 5.7 %collective-permute-done.8.right_ref = f32[592,128]{1,0:T(8,128)S(1)} collective-permute-done((f32[592,128]{1,0:T(8,128)S(1)}, f32[592,128]{1,0:T(8,128)S(1)}, u32[]{:S(2)}, u32[]{:S(2)}) %collective-permute-start.8) | collective-permute-done | bytes 303136 | tf_op jit(solution)/shard_map/ppermute | solution.py:625
  62.4 2.4 %last_two.1 = (f32[1024,128]{1,0:T(8,128)S(1)}, f32[1024,128]{1,0:T(8,128)S(1)}) custom-call(f32[896,128]{1,0:T(8,128)S(1)} %get-tuple-element.38.coef_ref, f32[512,128]{1,0:T(8,128)S(1)} %get-tuple-element.39.block_1_ref, f32[512,128]{1,0:T(8,128)S(1)} %get-tuple-element.40.block_2_ref, f32[512,128]{1,0:T(8,128)S(1)} %get-tuple-element.41.my_2_ref, ...), custom_call_target="tpu_custom_call" | custom-call | tf_op jit(solution)/shard_map/last_two/pallas_call | solution.py:687
  64.8 6.9 %collective-permute-start.9 = (f32[1024,128]{1,0:T(8,128)S(1)}, f32[1024,128]{1,0:T(8,128)S(1)}, u32[]{:S(2)}, u32[]{:S(2)}) collective-permute-start(f32[1024,128]{1,0:T(8,128)S(1)} %get-tuple-element.47), channel_id=1, source_target_pairs={{0,32},{32,0},{64,96},{96,64},{128,160},{160,128},{192,224},{224,1... | collective-permute-start | bytes 1572872 | tf_op jit(solution)/shard_map/ppermute | solution.py:636
  71.7 1.5 %collective-permute-done.9.got_ref = f32[1024,128]{1,0:T(8,128)S(1)} collective-permute-done((f32[1024,128]{1,0:T(8,128)S(1)}, f32[1024,128]{1,0:T(8,128)S(1)}, u32[]{:S(2)}, u32[]{:S(2)}) %collective-permute-start.9) | collective-permute-done | bytes 524320 | tf_op jit(solution)/shard_map/ppermute | solution.py:636
  73.2 2.5 %gram.1 = (f32[320,1024]{1,0:T(8,128)S(1)}, f32[512,128]{1,0:T(8,128)S(1)}) custom-call(f32[512,128]{1,0:T(8,128)S(1)} %bitcast.13, f32[1024,128]{1,0:T(8,128)S(1)} %get-tuple-element.46.keep_ref, f32[1024,128]{1,0:T(8,128)S(1)} %collective-permute-done.9.got_ref), custom_call_target="tpu_custom_call" | custom-call | tf_op jit(solution)/shard_map/gram/pallas_call | solution.py:695
  75.7 21.8 %all_to_all.15 = f32[32,16,128]{2,1,0:T(8,128)S(1)} all-to-all(f32[32,16,128]{2,1,0:T(8,128)S(1)} %bitcast.15), channel_id=1, replica_groups=mesh['gx'=16,'gy'=8,'gz'=4] {'gy','gz'}, dimensions={0} | all-to-all | bytes 524288 | tf_op jit(solution)/shard_map/all_to_all | solution.py:701
  97.6 17.9 %all_to_all.16 = f32[16,16,128]{2,1,0:T(8,128)S(1)} all-to-all(f32[16,16,128]{2,1,0:T(8,128)S(1)} %broadcast_in_dim.6), channel_id=1, replica_groups=mesh['gx'=16,'gy'=8,'gz'=4] {'gx'}, dimensions={0} | all-to-all | bytes 262144 | tf_op jit(solution)/shard_map/all_to_all | solution.py:631
  115.5 15.7 %all_to_all.17 = f32[32,16,128]{2,1,0:T(8,128)S(1)} all-to-all(f32[32,16,128]{2,1,0:T(8,128)S(1)} %broadcast_in_dim.7), channel_id=1, replica_groups=mesh['gx'=16,'gy'=8,'gz'=4] {'gy','gz'}, dimensions={0} | all-to-all | bytes 524288 | tf_op jit(solution)/shard_map/all_to_all | solution.py:631
  131.1 12.5 %final.1 = (f32[512,128]{1,0:T(8,128)}, f32[512,128]{1,0:T(8,128)}) custom-call(f32[512,128]{1,0:T(8,128)S(1)} %bitcast.14, f32[320,1024]{1,0:T(8,128)S(1)} %get-tuple-element.49.basis_ref), custom_call_target="tpu_custom_call" | custom-call | tf_op jit(solution)/shard_map/final/pallas_call | solution.py:705
  (27 shorter events, 6.9 us)
Async XLA Ops:
  0.6 42.8 %copy-start.7 = (f32[32]{0:T(128)S(1)}, f32[32]{0:T(128)}, u32[]{:S(2)}) copy-start(f32[32]{0:T(128)} %rate_ref.1) | copy-start | bytes 388
  0.6 42.7 %copy-start.6 = (s32[32]{0:T(128)S(1)}, s32[32]{0:T(128)}, u32[]{:S(2)}) copy-start(s32[32]{0:T(128)} %cells_ref.1) | copy-start | bytes 388
  0.7 1.0 copy-start
  1.6 0.7 copy-start.2
  2.3 0.7 copy-start.3
  3.0 0.7 copy-start.4
  3.7 0.7 copy-start.5
  5.3 9.8 %collective-permute-start = (f32[296,128]{1,0:T(8,128)S(1)}, f32[296,128]{1,0:T(8,128)S(1)}, u32[]{:S(2)}, u32[]{:S(2)}) collective-permute-start(f32[296,128]{1,0:T(8,128)S(1)} %get-tuple-element.28), channel_id=1, source_target_pairs={{0,32},{32,0},{64,96},{96,64},{128,160},{160,128},{192,224},{224,1... | collective-permute-start | bytes 454664 | tf_op jit(solution)/shard_map/ppermute | solution.py:636
  15.3 5.3 %collective-permute-start.2 = (f32[40,128]{1,0:T(8,128)S(1)}, f32[40,128]{1,0:T(8,128)S(1)}, u32[]{:S(2)}, u32[]{:S(2)}) collective-permute-start(f32[40,128]{1,0:T(8,128)S(1)} %get-tuple-element.30), channel_id=1, source_target_pairs={{1,0},{2,1},{3,2},{5,4},{6,5},{7,6},{9,8},{10,9},{11,10},{13,12},{... | collective-permute-start | bytes 61448 | tf_op jit(solution)/shard_map/ppermute | solution.py:625
  16.6 4.9 %collective-permute-start.1 = (f32[40,128]{1,0:T(8,128)S(1)}, f32[40,128]{1,0:T(8,128)S(1)}, u32[]{:S(2)}, u32[]{:S(2)}) collective-permute-start(f32[40,128]{1,0:T(8,128)S(1)} %get-tuple-element.30), channel_id=1, source_target_pairs={{0,1},{1,2},{2,3},{4,5},{5,6},{6,7},{8,9},{9,10},{10,11},{12,13},{... | collective-permute-start | bytes 61448 | tf_op jit(solution)/shard_map/ppermute | solution.py:624
  21.5 3.5 %collective-permute-start.3 = (f32[320,128]{1,0:T(8,128)S(1)}, f32[320,128]{1,0:T(8,128)S(1)}, u32[]{:S(2)}, u32[]{:S(2)}) collective-permute-start(f32[320,128]{1,0:T(8,128)S(1)} %get-tuple-element.32), channel_id=1, source_target_pairs={{0,4},{4,8},{8,12},{12,16},{16,20},{20,24},{24,28},{1,5},{5,9},{9,... | collective-permute-start | bytes 491528 | tf_op jit(solution)/shard_map/ppermute | solution.py:624
  22.8 6.1 %collective-permute-start.4 = (f32[320,128]{1,0:T(8,128)S(1)}, f32[320,128]{1,0:T(8,128)S(1)}, u32[]{:S(2)}, u32[]{:S(2)}) collective-permute-start(f32[320,128]{1,0:T(8,128)S(1)} %get-tuple-element.33), channel_id=1, source_target_pairs={{4,0},{8,4},{12,8},{16,12},{20,16},{24,20},{28,24},{5,1},{9,5},{13... | collective-permute-start | bytes 491528 | tf_op jit(solution)/shard_map/ppermute | solution.py:625
  29.0 10.7 %collective-permute-start.5 = (f32[1072,128]{1,0:T(8,128)S(1)}, f32[1072,128]{1,0:T(8,128)S(1)}, u32[]{:S(2)}, u32[]{:S(2)}) collective-permute-start(f32[1072,128]{1,0:T(8,128)S(1)} %get-tuple-element.36), channel_id=1, source_target_pairs={{0,64},{32,96},{64,128},{96,160},{128,192},{160,224},{192,256},{22... | collective-permute-start | bytes 1646600 | tf_op jit(solution)/shard_map/ppermute | solution.py:624
  30.3 13.1 %collective-permute-start.6 = (f32[1072,128]{1,0:T(8,128)S(1)}, f32[1072,128]{1,0:T(8,128)S(1)}, u32[]{:S(2)}, u32[]{:S(2)}) collective-permute-start(f32[1072,128]{1,0:T(8,128)S(1)} %get-tuple-element.37), channel_id=1, source_target_pairs={{64,0},{96,32},{128,64},{160,96},{192,128},{224,160},{256,192},{28... | collective-permute-start | bytes 1646600 | tf_op jit(solution)/shard_map/ppermute | solution.py:625
  49.2 24.1 %copy-start.1 = (f32[64,1,8,128]{3,2,1,0:T(8,128)S(1)}, f32[64,1,8,128]{3,2,1,0:T(8,128)}, u32[]{:S(2)}) copy-start(f32[64,1,8,128]{3,2,1,0:T(8,128)} %param.7) | copy-start | bytes 786436
  49.2 7.6 %collective-permute-start.7 = (f32[592,128]{1,0:T(8,128)S(1)}, f32[592,128]{1,0:T(8,128)S(1)}, u32[]{:S(2)}, u32[]{:S(2)}) collective-permute-start(f32[592,128]{1,0:T(8,128)S(1)} %get-tuple-element.44), channel_id=1, source_target_pairs={{0,64},{32,96},{64,128},{96,160},{128,192},{160,224},{192,256},{22... | collective-permute-start | bytes 909320 | tf_op jit(solution)/shard_map/ppermute | solution.py:624
  53.0 9.4 %collective-permute-start.8 = (f32[592,128]{1,0:T(8,128)S(1)}, f32[592,128]{1,0:T(8,128)S(1)}, u32[]{:S(2)}, u32[]{:S(2)}) collective-permute-start(f32[592,128]{1,0:T(8,128)S(1)} %get-tuple-element.45), channel_id=1, source_target_pairs={{64,0},{96,32},{128,64},{160,96},{192,128},{224,160},{256,192},{28... | collective-permute-start | bytes 909320 | tf_op jit(solution)/shard_map/ppermute | solution.py:625
  64.8 8.4 %collective-permute-start.9 = (f32[1024,128]{1,0:T(8,128)S(1)}, f32[1024,128]{1,0:T(8,128)S(1)}, u32[]{:S(2)}, u32[]{:S(2)}) collective-permute-start(f32[1024,128]{1,0:T(8,128)S(1)} %get-tuple-element.47), channel_id=1, source_target_pairs={{0,32},{32,0},{64,96},{96,64},{128,160},{160,128},{192,224},{224,1... | collective-permute-start | bytes 1572872 | tf_op jit(solution)/shard_map/ppermute | solution.py:636

commit v4 on v3

--- a/solution.py
+++ b/solution.py
@@ -65,11 +65,12 @@
     return lax.rem(lax.axis_index("gx"), 2)
 
 
-def pack_kernel(right_hbm, vel_hbm, decay_hbm, class_hbm, table_ref, send_ref, keep_ref, class_ref, sems):
+def pack_kernel(right_hbm, vel_hbm, decay_hbm, class_hbm, table_hbm, send_ref, keep_ref, class_ref, table_ref, sems):
     mine = pl.multiple_of(core() * 8 * HALF, 8)
     other = pl.multiple_of((1 - core()) * 8 * HALF, 8)
     copies = [
         (class_hbm, class_ref),
+        (table_hbm, table_ref),
         (vel_hbm, keep_ref.at[pl.ds(8 * HALF, 24), :]),
         (decay_hbm, keep_ref.at[pl.ds(8 * (HALF + 3), 8), :]),
         (right_hbm.at[pl.ds(mine, 8 * HALF), :], keep_ref.at[pl.ds(0, 8 * HALF), :]),
@@ -132,10 +133,8 @@
         put(down_ref, g, jnp.where(lower, first, second))
 
 
-A_MY = SLOT
-A_SECOND = 2 * SLOT
-A_SECOND_MY = A_SECOND + HALF + 1
-A_EDGE = A_SECOND_MY + HALF // 2 + 1
+A_SECOND = SLOT
+A_EDGE = A_SECOND + HALF // 2 + 1
 A_TILES = A_EDGE + 2 * NE
 B_MY = HALF
 B_EDGE = B_MY + HALF // 4
@@ -143,7 +142,7 @@
 B_TILES = B_SECOND + HALF
 
 
-def xmsg_kernel(main_ref, edge_ref, below_ref, above_ref, my_ref, ey_ref, to_left_ref, to_right_ref):
+def xmsg_kernel(edge_ref, below_ref, above_ref, my_ref, ey_ref, to_left_ref, to_right_ref):
     row = iota_row()
     lower = row < 4
     keep_2 = (row < 2) | (row >= 6)
@@ -155,44 +154,55 @@
             if index < 2 * SLOT:
                 put(my_ref, index, pair[half])
                 p, i = divmod(index, SLOT)
-                put((to_left_ref, to_right_ref)[p], A_MY + i, pair[half])
+                put((to_left_ref, to_right_ref)[p], i, pair[half])
                 if i == SLOT - 1:
-                    put((to_right_ref, to_left_ref)[p], A_SECOND_MY + HALF // 2, pair[half])
+                    put((to_right_ref, to_left_ref)[p], A_SECOND + HALF // 2, pair[half])
             elif index < 2 * SLOT + NE:
                 put(ey_ref, index - 2 * SLOT, pair[half])
                 for ref in (to_left_ref, to_right_ref):
                     put(ref, A_EDGE + NE + index - 2 * SLOT, pair[half])
-    for p, (adjacent, second) in enumerate(((to_left_ref, to_right_ref), (to_right_ref, to_left_ref))):
-        for i in range(SLOT):
-            value = tile(main_ref, SLOT * p + i)
-            put(adjacent, i, value)
-            if i < HALF:
-                put(second, A_SECOND + i, value)
-            elif i == SLOT - 1:
-                put(second, A_SECOND + HALF, value)
+    for p, second in enumerate((to_right_ref, to_left_ref)):
         for i in range(HALF // 2):
             value = jnp.where(
                 keep_2,
                 tile(my_ref, SLOT * p + 2 * i),
                 roll_row(tile(my_ref, SLOT * p + 2 * i + 1), 4),
             )
-            put(second, A_SECOND_MY + i, value)
+            put(second, A_SECOND + i, value)
     for t in range(NE):
         value = tile(edge_ref, t)
         put(to_left_ref, A_EDGE + t, value)
         put(to_right_ref, A_EDGE + t, value)
 
 
-def plane_coefficients(sizes, cells_ref, rate_ref, conduct_ref, given_ref, coef_ref):
+def part_places():
     row, lane = iota_row(), iota_lane()
-    size_x, size_y, size_z = sizes
-    first_x = lax.axis_index("gx") - core() - 1
     at_y, at_z = lax.axis_index("gy"), lax.axis_index("gz")
     y_main = at_y * 8 + row
     y_my = at_y * 8 + jnp.where(row < 4, row + 8, row - 8)
     z_main = at_z * 128 + lane
     z_edge = at_z * 128 + jnp.where(lane < 64, lane + 128, lane - 128)
-    where = ((y_main, z_main), (y_my, z_main), (y_main, z_edge), (y_my, z_edge))
+    return ((y_main, z_main), (y_my, z_main), (y_main, z_edge), (y_my, z_edge))
+
+
+def wells_kernel(sizes, cells_ref, rate_ref, wells_ref):
+    size_x, size_y, size_z = sizes
+    first_x = lax.axis_index("gx") - core() - 1
+    for part, (y_at, z_at) in enumerate(part_places()):
+        flats = [((first_x + s) * size_y + y_at) * size_z + z_at for s in range(4)]
+        wells = [jnp.zeros((8, 128), jnp.float32)] * 4
+        for w in range(cells_ref.shape[0]):
+            for s in range(4):
+                wells[s] = wells[s] + jnp.where(flats[s] == cells_ref[w], rate_ref[w], 0.0)
+        for s in range(4):
+            put(wells_ref, s * 4 + part, wells[s])
+
+
+def plane_coefficients(sizes, wells_ref, conduct_ref, given_ref, coef_ref):
+    row, lane = iota_row(), iota_lane()
+    size_x, size_y, size_z = sizes
+    first_x = lax.axis_index("gx") - core() - 1
+    where = part_places()
 
     def shift_y(four, shift, mask):
         main, my = swap_shift(four[0], four[1], roll_row, shift, mask)
@@ -213,15 +223,11 @@
         at_x = first_x + s
         x_inside = (at_x >= 0) & (at_x < size_x)
         for part, (y_at, z_at) in enumerate(where):
-            flat = (at_x * size_y + y_at) * size_z + z_at
-            wells = jnp.zeros((8, 128), jnp.float32)
-            for w in range(cells_ref.shape[0]):
-                wells = wells + jnp.where(flat == cells_ref[w], rate_ref[w], 0.0)
             inside = (y_at >= 0) & (y_at < size_y) & (z_at >= 0) & (z_at < size_z) & x_inside
             if part >= 2:
                 inside = inside & ((lane < 4) | (lane >= 124))
             given = [tile(given_ref, (s * 4 + e) * 4 + part) for e in range(4)]
-            diagonal = given[3] + wells
+            diagonal = given[3] + tile(wells_ref, s * 4 + part)
             values = []
             for d in range(3):
                 plus_face = 0.5 * (center[part] + plus[d][part])
@@ -308,12 +314,13 @@
 
 def first_two_kernel(
     sizes,
-    cells_ref,
-    rate_ref,
+    wells_ref,
     main_ref,
     edge_ref,
     my_ref,
     ey_ref,
+    left_main_ref,
+    right_main_ref,
     left_ref,
     right_ref,
     coef_ref,
@@ -343,23 +350,23 @@
         copy_tiles(ey_ref, TG * p, ey_0, TG * (2 + p), TG)
     extras = {2: (main_ref, HALF, my_ref, HALF, edge_ref, NE - 1, ey_ref, NE - 1, 0)}
     extras[3] = (main_ref, SLOT + HALF, my_ref, SLOT + HALF, edge_ref, NE - 1, ey_ref, NE - 1, NEXTRA)
-    for ref, adjacent, second, p in ((left_ref, 1, 0, 1), (right_ref, 4, 5, 0)):
-        copy_tiles(ref, 0, main_0, HALF * adjacent, HALF)
-        copy_tiles(ref, A_MY, my_0, HALF * adjacent, HALF)
-        copy_tiles(ref, A_SECOND, main_0, HALF * second, HALF)
+    for whole, ref, adjacent, second, p in ((left_main_ref, left_ref, 1, 0, 1), (right_main_ref, right_ref, 4, 5, 0)):
+        copy_tiles(whole, SLOT * p, main_0, HALF * adjacent, HALF)
+        copy_tiles(whole, SLOT * (1 - p), main_0, HALF * second, HALF)
+        copy_tiles(ref, 0, my_0, HALF * adjacent, HALF)
         for i in range(HALF // 2):
-            value = tile(ref, A_SECOND_MY + i)
+            value = tile(ref, A_SECOND + i)
             put(my_0, HALF * second + 2 * i, value)
             put(my_0, HALF * second + 2 * i + 1, roll_row(value, 4))
         for plane, at in ((adjacent, p), (second, 1 - p)):
             copy_tiles(ref, A_EDGE + TG * at, em_0, TG * plane, TG)
             copy_tiles(ref, A_EDGE + NE + TG * at, ey_0, TG * plane, TG)
         em_at, ey_at = A_EDGE + NE - 1, A_EDGE + 2 * NE - 1
-        extras[adjacent] = (ref, HALF, ref, A_MY + HALF, ref, em_at, ref, ey_at, NEXTRA * p)
+        extras[adjacent] = (whole, SLOT * p + HALF, ref, HALF, ref, em_at, ref, ey_at, NEXTRA * p)
         for part, value in enumerate(
             (
-                tile(ref, A_SECOND + HALF),
-                tile(ref, A_SECOND_MY + HALF // 2),
+                tile(whole, SLOT * (1 - p) + SLOT - 1),
+                tile(ref, A_SECOND + HALF // 2),
                 roll_lane(tile(ref, em_at), -8 * (NEXTRA * (1 - p) + 4)),
                 roll_lane(tile(ref, ey_at), -8 * (NEXTRA * (1 - p) + 4)),
             )
@@ -378,7 +385,7 @@
                     put(conduct_ref, 4 * plane + part, value)
                 else:
                     put(given_ref, ((plane - 1) * 4 + e) * 4 + part, value)
-    plane_coefficients(sizes, cells_ref, rate_ref, conduct_ref, given_ref, coef_ref)
+    plane_coefficients(sizes, wells_ref, conduct_ref, given_ref, coef_ref)
     step((main_0, my_0, em_0, ey_0), (main_1, my_1, em_1, ey_1), coef_ref, 1, 4, -1, -1)
     copy_tiles(main_1, HALF, block_1_ref, 0, 2 * HALF)
     step((main_1, my_1, em_1, ey_1), (block_2_ref, my_2_ref, em_2_ref, ey_2_ref), coef_ref, 1, 2, 0, -1)
@@ -452,8 +459,16 @@
 )
 
 
-def dot_nt(first, second):
-    return lax.dot_general(first, second, (((1,), (1,)), ((), ())), precision=HI, preferred_element_type=jnp.float32)
+def two_parts(values):
+    high = values.astype(jnp.bfloat16)
+    return high, (values - high.astype(jnp.float32)).astype(jnp.bfloat16)
+
+
+def three_products(first, second, dims):
+    def dot(a, b):
+        return lax.dot_general(a, b, (dims, ((), ())), preferred_element_type=jnp.float32)
+
+    return dot(first[0], second[0]) + (dot(first[0], second[1]) + dot(first[1], second[0]))
 
 
 def dot_tn(first, second):
@@ -464,7 +479,7 @@
     return lax.dot_general(first, second, (((1,), (0,)), ((), ())), precision=HI, preferred_element_type=jnp.float32)
 
 
-def gram_kernel(block_0, keep_ref, got_ref, basis_ref, gram_ref):
+def gram_kernel(block_0, keep_ref, got_ref, high_ref, low_ref, gram_ref, basis_ref):
     mine, other = core() * HALF, (1 - core()) * HALF
     for y in range(8):
         lanes = slice(128 * y, 128 * (y + 1))
@@ -473,7 +488,9 @@
             at = pl.ds(8 * HALF * (level - 1) + y, HALF, stride=8)
             basis_ref[pl.ds(pl.multiple_of(M * level + mine, 8), HALF), lanes] = keep_ref[at, :]
             basis_ref[pl.ds(pl.multiple_of(M * level + other, 8), HALF), lanes] = got_ref[at, :]
-    full = dot_nt(basis_ref[...], basis_ref[...])
+    parts = two_parts(basis_ref[...])
+    high_ref[...], low_ref[...] = parts
+    full = three_products(parts, parts, ((1,), (1,)))
     for index, pair in enumerate(PAIRS):
         for half, at in enumerate(pair):
             if at is None:
@@ -535,7 +552,7 @@
     return list(blocks) + [jnp.zeros((M, M), jnp.float32)] * (count - len(blocks))
 
 
-def final_kernel(gram_ref, basis_ref, field_ref, resid_ref, full_ref):
+def final_kernel(gram_ref, high_ref, low_ref, field_ref, resid_ref, full_ref):
     for index, pair in enumerate(PAIRS):
         for half, at in enumerate(pair):
             if at is None:
@@ -557,7 +574,10 @@
         product = gram(levels, second)
         cross = sum(product[M * j : M * j + M] * b for j, b in enumerate(half))
         square = sum(product[M * j : M * j + M] * b for j, b in enumerate(second))
-        return jnp.sum(cross) / jnp.sum(square), product[0:M]
+        def total(values):
+            return jnp.sum(jnp.sum(values, axis=0, keepdims=True), axis=1, keepdims=True)
+
+        return total(cross) / total(square), product[0:M]
 
     image_gram = SHIFT * full_ref[0:M, 0:M] + SCALE * full_ref[0:M, M : 2 * M]
     inverse = eliminate(dot_tn(image_gram, image_gram), image_gram.T)
@@ -593,10 +613,10 @@
     field = pad_levels(field, 5)
     resid = [h - omega * s for h, s in zip(pad_levels(half, 5), second)]
     coefs = jnp.concatenate([jnp.concatenate(field, axis=0), jnp.concatenate(resid, axis=0)], axis=1)
+    result = three_products(two_parts(coefs.T), (high_ref[...], low_ref[...]), ((1,), (0,)))
     for y in range(8):
-        result = dot_tn(coefs, basis_ref[:, 128 * y : 128 * (y + 1)])
-        field_ref[pl.ds(y, M, stride=8), :] = result[0:M]
-        resid_ref[pl.ds(y, M, stride=8), :] = result[M:]
+        field_ref[pl.ds(y, M, stride=8), :] = result[0:M, 128 * y : 128 * (y + 1)]
+        resid_ref[pl.ds(y, M, stride=8), :] = result[M:, 128 * y : 128 * (y + 1)]
 
 
 VMEM = pl.BlockSpec(memory_space=pltpu.VMEM)
@@ -631,6 +651,10 @@
     return lax.all_to_all(jnp.broadcast_to(values, (count, *values.shape)), axes, 0, 0)
 
 
+def in_hbm(values):
+    return pltpu.with_memory_space_constraint(values, pltpu.HBM)
+
+
 def other_core(values):
     count = lax.axis_size("gx")
     return lax.ppermute(values, "gx", [(i, i ^ 1) for i in range(count)])
@@ -647,25 +671,37 @@
 def per_device(right_side, velocity, decay_rate, perm_class, conductivity, well_cells, well_rate):
     sizes = (lax.axis_size("gx"), 8 * lax.axis_size("gy"), 128 * lax.axis_size("gz"))
     block_0 = right_side.reshape(8 * M, 128)
-    any_space = pl.BlockSpec(memory_space=pl.ANY)
+    any_space = pl.BlockSpec(memory_space=pltpu.HBM)
 
     send, keep = call(
         pack_kernel,
         "pack",
         (tiles(SLOT), tiles(SLOT)),
-        [any_space] * 4 + [SMEM],
-        [pltpu.VMEM((8, 128), jnp.int32), pltpu.SemaphoreType.DMA((5,))],
-    )(block_0, velocity.reshape(24, 128), decay_rate.reshape(8, 128), perm_class.reshape(8, 128), conductivity)
+        [any_space] * 5,
+        [
+            pltpu.VMEM((8, 128), jnp.int32),
+            pltpu.SMEM(conductivity.shape, jnp.float32),
+            pltpu.SemaphoreType.DMA((6,)),
+        ],
+    )(
+        in_hbm(block_0),
+        in_hbm(velocity.reshape(24, 128)),
+        in_hbm(decay_rate.reshape(8, 128)),
+        in_hbm(perm_class.reshape(8, 128)),
+        in_hbm(conductivity),
+    )
     got = other_core(send)
+    wells = call(functools.partial(wells_kernel, sizes), "wells", tiles(16), [SMEM, SMEM])(well_cells, well_rate)
     main, zmsg = call(zmsg_kernel, "zmsg", (tiles(2 * SLOT), tiles(NE)), [VMEM] * 2)(keep, got)
+    left_main, right_main = from_sides("gx", main, main, 2)
     low, high = from_sides("gz", zmsg, zmsg)
     up, down, edge = call(ymsg_kernel, "ymsg", (tiles(YPAIRS), tiles(YPAIRS), tiles(NE)), [VMEM] * 3)(
         main, low, high
     )
     below, above = from_sides("gy", up, down)
     my, ey, to_left, to_right = call(
-        xmsg_kernel, "xmsg", (tiles(2 * SLOT), tiles(NE), tiles(A_TILES), tiles(A_TILES)), [VMEM] * 4
-    )(main, edge, below, above)
+        xmsg_kernel, "xmsg", (tiles(2 * SLOT), tiles(NE), tiles(A_TILES), tiles(A_TILES)), [VMEM] * 3
+    )(edge, below, above)
     left, right = from_sides("gx", to_right, to_left, 2)
     coef, block_1, block_2, my, em, ey, to_left, to_right = call(
         functools.partial(first_two_kernel, sizes),
@@ -680,9 +716,9 @@
             tiles(B_TILES),
             tiles(B_TILES),
         ),
-        [SMEM, SMEM] + [VMEM] * 6,
+        [VMEM] * 9,
         scratch(24, 64, 6 * HALF, 6 * HALF, 6 * TG, 6 * TG, 4 * HALF, 4 * HALF, 4 * TG, 4 * TG),
-    )(well_cells, well_rate, main, edge, my, ey, left, right)
+    )(wells, main, edge, my, ey, left_main, right_main, left, right)
     left, right = from_sides("gx", to_right, to_left, 2)
     keep, send = call(
         last_two_kernel,
@@ -692,11 +728,16 @@
         scratch(6 * HALF, 6 * HALF, 6 * TG, 6 * TG, 4 * HALF, 4 * HALF, 4 * TG, 2 * HALF),
     )(coef, block_1, block_2, my, em, ey, left, right)
     got = other_core(send)
-    basis, gram = call(gram_kernel, "gram", (f32(LEVELS * M, 1024), f32(8 * M, 128)), [VMEM] * 3)(
-        block_0, keep, got
-    )
-
-    plane = ("gy", "gz")
+    part = jax.ShapeDtypeStruct((LEVELS * M, 1024), jnp.bfloat16)
+    high, low, gram = call(
+        gram_kernel,
+        "gram",
+        (part, part, f32(8 * M, 128)),
+        [VMEM] * 3,
+        [pltpu.VMEM((LEVELS * M, 1024), jnp.float32)],
+    )(block_0, keep, got)
+
+    plane = ("gz", "gy")
     count = lax.axis_size(plane)
     gram = lax.all_to_all(gram.reshape(count, -1, 128), plane, 0, 0)
     gram = jnp.sum(gram, axis=0)
@@ -706,9 +747,9 @@
         final_kernel,
         "final",
         (f32(8 * M, 128), f32(8 * M, 128)),
-        [VMEM, VMEM],
+        [VMEM] * 3,
         [pltpu.VMEM((LEVELS * M, LEVELS * M), jnp.float32)],
-    )(gram, basis)
+    )(gram, high, low)
     return field.reshape(right_side.shape), resid.reshape(right_side.shape)
 
 

time: 144 us -> 135 us (0.938); the launches traced: 144 us -> 133 us
  waiting for transfers between devices: 28 us -> 15.7 us
  starting transfers between devices: 31.3 us -> 37.3 us
  local copies, waits for them, and re-layouts: 3.73 us -> 0.05 us
  Pallas kernels: 24.4 us -> 22.6 us
    ppermute x4 -> x5, waiting for transfers between devices: 13.2 us -> 3.85 us  [from_sides(): upper = lax.ppermute(down, axis, [(i + by, i) for i in range(count - by)])]
    ppermute x4 -> x5, starting transfers between devices: 10.5 us -> 15.7 us  [from_sides(): lower = lax.ppermute(up, axis, [(i, i + by) for i in range(count - by)])]
    unnamed x16 -> x6, local copies, waits for them, and re-layouts: 3.7 us -> 0.02 us
    ppermute x4 -> x5, waiting for transfers between devices: 12.3 us -> 9.38 us  [from_sides(): lower = lax.ppermute(up, axis, [(i, i + by) for i in range(count - by)])]
    ppermute x4 -> x5, starting transfers between devices: 5.17 us -> 6.46 us  [from_sides(): upper = lax.ppermute(down, axis, [(i + by, i) for i in range(count - by)])]
    pallas_call x3 -> x4, Pallas kernels: 15.9 us -> 14.9 us  [the longest x1 11.4 us: per_device(): call(final_kernel, 'final', (f32(8 * M, 128), f32(8 * M, 128)), [VMEM] *...]
  transfers between devices with their start and end apart: 10 -> 12, of which waited for: 9 -> 7; matrix products, arithmetic and copies ran while one was open for 0% -> 0% of each run, Pallas kernels for 0% -> 1%
where the time goes in v4:
time: 135 us; the launch traced here: 133 us
  blocking collectives  56.4 us (42%)
  starting transfers between devices  37.3 us (28%)
  Pallas kernels  22.6 us (17%)
  waiting for transfers between devices  15.7 us (12%)
    all_to_all x2, blocking collectives, spread(): lax.all_to_all(jnp.broadcast_to(values, (count, *values.shape)), axes, 0, 0)  34.4 us
    all_to_all x1, blocking collectives, per_device(): gram = lax.all_to_all(gram.reshape(count, -1, 128), plane, 0, 0)  22 us
    ppermute x5, starting transfers between devices, from_sides(): lower = lax.ppermute(up, axis, [(i, i + by) for i in range(count - by)])  15.7 us
    ppermute x2, starting transfers between devices, other_core(): return lax.ppermute(values, 'gx', [(i, i ^ 1) for i in range(count)])  15.1 us
    pallas_call x1, Pallas kernels, per_device(): call(final_kernel, 'final', (f32(8 * M, 128), f32(8 * M, 128)), [VMEM] *...  11.4 us
    ppermute x5, waiting for transfers between devices, from_sides(): lower = lax.ppermute(up, axis, [(i, i + by) for i in range(count - by)])  9.38 us
    ppermute x5, starting transfers between devices, from_sides(): upper = lax.ppermute(down, axis, [(i + by, i) for i in range(count - by)])  6.46 us
    pallas_call x1, Pallas kernels, per_device(): call(functools.partial(first_two_kernel, sizes), 'first_two', (tiles(4 *...  5.08 us
  transfers between devices with their start and end apart: 12, of which 7 were waited for; matrix products, arithmetic and copies ran while one was open for 0% of the time, Pallas kernels for 1%

profile of v4, /device:TPU:1, one launch (start us, length us, event | category | flops | bytes accessed | tf_op | source)
XLA Modules:
  0.0 133.0 jit_solution(14897696011182324934)
XLA Ops:
  0.6 1.1 pack.1
  1.7 8.8 %collective-permute-start = (f32[296,128]{1,0:T(8,128)S(1)}, f32[296,128]{1,0:T(8,128)S(1)}, u32[]{:S(2)}, u32[]{:S(2)}) collective-permute-start(f32[296,128]{1,0:T(8,128)S(1)} %get-tuple-element.29), channel_id=1, source_target_pairs={{0,32},{32,0},{64,96},{96,64},{128,160},{160,128},{192,224},{224,1... | collective-permute-start | bytes 454664 | tf_op jit(solution)/shard_map/ppermute | solution.py:660
  11.7 1.3 collective-permute-start.2
  13.0 4.0 %collective-permute-start.1 = (f32[40,128]{1,0:T(8,128)S(1)}, f32[40,128]{1,0:T(8,128)S(1)}, u32[]{:S(2)}, u32[]{:S(2)}) collective-permute-start(f32[40,128]{1,0:T(8,128)S(1)} %get-tuple-element.31), channel_id=1, source_target_pairs={{0,1},{1,2},{2,3},{4,5},{5,6},{6,7},{8,9},{9,10},{10,11},{12,13},{... | collective-permute-start | bytes 61448 | tf_op jit(solution)/shard_map/ppermute | solution.py:644
  17.9 1.3 collective-permute-start.3
  19.2 1.3 collective-permute-start.4
  20.5 1.3 collective-permute-start.6
  21.8 4.0 %collective-permute-start.5 = (f32[592,128]{1,0:T(8,128)S(1)}, f32[592,128]{1,0:T(8,128)S(1)}, u32[]{:S(2)}, u32[]{:S(2)}) collective-permute-start(f32[592,128]{1,0:T(8,128)S(1)} %get-tuple-element.30.main_ref), channel_id=1, source_target_pairs={{0,64},{32,96},{64,128},{96,160},{128,192},{160,224},{192,256},{22... | collective-permute-start | bytes 909320 | tf_op jit(solution)/shard_map/ppermute | solution.py:644
  25.9 1.9 %collective-permute-start.7 = (f32[512,128]{1,0:T(8,128)S(1)}, f32[512,128]{1,0:T(8,128)S(1)}, u32[]{:S(2)}, u32[]{:S(2)}) collective-permute-start(f32[512,128]{1,0:T(8,128)S(1)} %get-tuple-element.37), channel_id=1, source_target_pairs={{0,64},{32,96},{64,128},{96,160},{128,192},{160,224},{192,256},{22... | collective-permute-start | bytes 786440 | tf_op jit(solution)/shard_map/ppermute | solution.py:644
  27.9 1.3 collective-permute-start.8
  30.5 5.6 %collective-permute-done.7.left_ref = f32[512,128]{1,0:T(8,128)S(1)} collective-permute-done((f32[512,128]{1,0:T(8,128)S(1)}, f32[512,128]{1,0:T(8,128)S(1)}, u32[]{:S(2)}, u32[]{:S(2)}) %collective-permute-start.7) | collective-permute-done | bytes 262176 | tf_op jit(solution)/shard_map/ppermute | solution.py:644
  36.1 5.1 %first_two.1 = (f32[896,128]{1,0:T(8,128)S(1)}, f32[512,128]{1,0:T(8,128)S(1)}, f32[512,128]{1,0:T(8,128)S(1)}, f32[512,128]{1,0:T(8,128)S(1)}, f32[32,128]{1,0:...) custom-call(f32[128,128]{1,0:T(8,128)S(1)} %wells.1.wells_ref, ...), custom_call_target="tpu_custom_call" | custom-call | tf_op jit(solution)/shard_map/first_two/pallas_call | solution.py:706
  41.2 4.5 %collective-permute-start.9 = (f32[592,128]{1,0:T(8,128)S(1)}, f32[592,128]{1,0:T(8,128)S(1)}, u32[]{:S(2)}, u32[]{:S(2)}) collective-permute-start(f32[592,128]{1,0:T(8,128)S(1)} %get-tuple-element.45), channel_id=1, source_target_pairs={{0,64},{32,96},{64,128},{96,160},{128,192},{160,224},{192,256},{22... | collective-permute-start | bytes 909320 | tf_op jit(solution)/shard_map/ppermute | solution.py:644
  45.7 1.3 collective-permute-start.10
  47.0 2.4 %collective-permute-done.9.left_ref = f32[592,128]{1,0:T(8,128)S(1)} collective-permute-done((f32[592,128]{1,0:T(8,128)S(1)}, f32[592,128]{1,0:T(8,128)S(1)}, u32[]{:S(2)}, u32[]{:S(2)}) %collective-permute-start.9) | collective-permute-done | bytes 303136 | tf_op jit(solution)/shard_map/ppermute | solution.py:644
  49.4 3.8 %collective-permute-done.10.right_ref = f32[592,128]{1,0:T(8,128)S(1)} collective-permute-done((f32[592,128]{1,0:T(8,128)S(1)}, f32[592,128]{1,0:T(8,128)S(1)}, u32[]{:S(2)}, u32[]{:S(2)}) %collective-permute-start.10) | collective-permute-done | bytes 303136 | tf_op jit(solution)/shard_map/ppermute | solution.py:645
  53.3 2.4 %last_two.1 = (f32[1024,128]{1,0:T(8,128)S(1)}, f32[1024,128]{1,0:T(8,128)S(1)}) custom-call(f32[896,128]{1,0:T(8,128)S(1)} %get-tuple-element.39.coef_ref, f32[512,128]{1,0:T(8,128)S(1)} %get-tuple-element.40.block_1_ref, f32[512,128]{1,0:T(8,128)S(1)} %get-tuple-element.41.block_2_ref, f32[512,128]{1,0:T(8,128)S(1)} %get-tuple-element.42.my_2_ref, ...), custom_call_target="tpu_custom_call" | custom-call | tf_op jit(solution)/shard_map/last_two/pallas_call | solution.py:723
  55.6 6.3 %collective-permute-start.11 = (f32[1024,128]{1,0:T(8,128)S(1)}, f32[1024,128]{1,0:T(8,128)S(1)}, u32[]{:S(2)}, u32[]{:S(2)}) collective-permute-start(f32[1024,128]{1,0:T(8,128)S(1)} %get-tuple-element.48), channel_id=1, source_target_pairs={{0,32},{32,0},{64,96},{96,64},{128,160},{160,128},{192,224},{224,1... | collective-permute-start | bytes 1572872 | tf_op jit(solution)/shard_map/ppermute | solution.py:660
  62.0 1.5 %collective-permute-done.11.got_ref = f32[1024,128]{1,0:T(8,128)S(1)} collective-permute-done((f32[1024,128]{1,0:T(8,128)S(1)}, f32[1024,128]{1,0:T(8,128)S(1)}, u32[]{:S(2)}, u32[]{:S(2)}) %collective-permute-start.11) | collective-permute-done | bytes 524320 | tf_op jit(solution)/shard_map/ppermute | solution.py:660
  63.5 1.6 %gram.1 = (bf16[320,1024]{1,0:T(8,128)(2,1)S(1)}, bf16[320,1024]{1,0:T(8,128)(2,1)S(1)}, f32[512,128]{1,0:T(8,128)S(1)}) custom-call(f32[512,128]{1,0:T(8,128)S(1)} %bitcast.13, f32[1024,128]{1,0:T(8,128)S(1)} %get-tuple-element.47.keep_ref, f32[1024,128]{1,0:T(8,128)S(1)} %collective-permute-done.11.got_ref), custom_call_target="tpu_custom_call" | custom-call | tf_op jit(solution)/shard_map/gram/pallas_call | solution.py:732
  65.1 22.0 %all_to_all.15 = f32[32,16,128]{2,1,0:T(8,128)S(1)} all-to-all(f32[32,16,128]{2,1,0:T(8,128)S(1)} %bitcast.15), channel_id=1, replica_groups=mesh['gx'=16,'gy'=8,'gz'=4] {'gz','gy'}, dimensions={0} | all-to-all | bytes 524288 | tf_op jit(solution)/shard_map/all_to_all | solution.py:742
  87.1 19.8 %all_to_all.16 = f32[16,16,128]{2,1,0:T(8,128)S(1)} all-to-all(f32[16,16,128]{2,1,0:T(8,128)S(1)} %broadcast_in_dim.6), channel_id=1, replica_groups=mesh['gx'=16,'gy'=8,'gz'=4] {'gx'}, dimensions={0} | all-to-all | bytes 262144 | tf_op jit(solution)/shard_map/all_to_all | solution.py:651
  106.9 14.6 %all_to_all.17 = f32[32,16,128]{2,1,0:T(8,128)S(1)} all-to-all(f32[32,16,128]{2,1,0:T(8,128)S(1)} %broadcast_in_dim.7), channel_id=1, replica_groups=mesh['gx'=16,'gy'=8,'gz'=4] {'gz','gy'}, dimensions={0} | all-to-all | bytes 524288 | tf_op jit(solution)/shard_map/all_to_all | solution.py:651
  121.6 11.4 %final.1 = (f32[512,128]{1,0:T(8,128)}, f32[512,128]{1,0:T(8,128)}) custom-call(f32[512,128]{1,0:T(8,128)S(1)} %bitcast.14, bf16[320,1024]{1,0:T(8,128)(2,1)S(1)} %get-tuple-element.50.high_ref, bf16[320,1024]{1,0:T(8,128)(2,1)S(1)} %get-tuple-element.51.low_ref), custom_call_target="tpu_custom_call" | custom-call | tf_op jit(solution)/shard_map/final/pallas_call | solution.py:746
  (22 shorter events, 3.5 us)
Async XLA Ops:
  1.7 9.8 %collective-permute-start = (f32[296,128]{1,0:T(8,128)S(1)}, f32[296,128]{1,0:T(8,128)S(1)}, u32[]{:S(2)}, u32[]{:S(2)}) collective-permute-start(f32[296,128]{1,0:T(8,128)S(1)} %get-tuple-element.29), channel_id=1, source_target_pairs={{0,32},{32,0},{64,96},{96,64},{128,160},{160,128},{192,224},{224,1... | collective-permute-start | bytes 454664 | tf_op jit(solution)/shard_map/ppermute | solution.py:660
  11.7 5.3 %collective-permute-start.2 = (f32[40,128]{1,0:T(8,128)S(1)}, f32[40,128]{1,0:T(8,128)S(1)}, u32[]{:S(2)}, u32[]{:S(2)}) collective-permute-start(f32[40,128]{1,0:T(8,128)S(1)} %get-tuple-element.31), channel_id=1, source_target_pairs={{1,0},{2,1},{3,2},{5,4},{6,5},{7,6},{9,8},{10,9},{11,10},{13,12},{... | collective-permute-start | bytes 61448 | tf_op jit(solution)/shard_map/ppermute | solution.py:645
  13.0 4.9 %collective-permute-start.1 = (f32[40,128]{1,0:T(8,128)S(1)}, f32[40,128]{1,0:T(8,128)S(1)}, u32[]{:S(2)}, u32[]{:S(2)}) collective-permute-start(f32[40,128]{1,0:T(8,128)S(1)} %get-tuple-element.31), channel_id=1, source_target_pairs={{0,1},{1,2},{2,3},{4,5},{5,6},{6,7},{8,9},{9,10},{10,11},{12,13},{... | collective-permute-start | bytes 61448 | tf_op jit(solution)/shard_map/ppermute | solution.py:644
  17.9 7.9 %collective-permute-start.3 = (f32[320,128]{1,0:T(8,128)S(1)}, f32[320,128]{1,0:T(8,128)S(1)}, u32[]{:S(2)}, u32[]{:S(2)}) collective-permute-start(f32[320,128]{1,0:T(8,128)S(1)} %get-tuple-element.33), channel_id=1, source_target_pairs={{0,4},{4,8},{8,12},{12,16},{16,20},{20,24},{24,28},{1,5},{5,9},{9,... | collective-permute-start | bytes 491528 | tf_op jit(solution)/shard_map/ppermute | solution.py:644
  19.2 6.6 %collective-permute-start.4 = (f32[320,128]{1,0:T(8,128)S(1)}, f32[320,128]{1,0:T(8,128)S(1)}, u32[]{:S(2)}, u32[]{:S(2)}) collective-permute-start(f32[320,128]{1,0:T(8,128)S(1)} %get-tuple-element.34), channel_id=1, source_target_pairs={{4,0},{8,4},{12,8},{16,12},{20,16},{24,20},{28,24},{5,1},{9,5},{13... | collective-permute-start | bytes 491528 | tf_op jit(solution)/shard_map/ppermute | solution.py:645
  20.5 9.5 %collective-permute-start.6 = (f32[592,128]{1,0:T(8,128)S(1)}, f32[592,128]{1,0:T(8,128)S(1)}, u32[]{:S(2)}, u32[]{:S(2)}) collective-permute-start(f32[592,128]{1,0:T(8,128)S(1)} %get-tuple-element.30.main_ref), channel_id=1, source_target_pairs={{64,0},{96,32},{128,64},{160,96},{192,128},{224,160},{256,192},{28... | collective-permute-start | bytes 909320 | tf_op jit(solution)/shard_map/ppermute | solution.py:645
  21.8 8.7 %collective-permute-start.5 = (f32[592,128]{1,0:T(8,128)S(1)}, f32[592,128]{1,0:T(8,128)S(1)}, u32[]{:S(2)}, u32[]{:S(2)}) collective-permute-start(f32[592,128]{1,0:T(8,128)S(1)} %get-tuple-element.30.main_ref), channel_id=1, source_target_pairs={{0,64},{32,96},{64,128},{96,160},{128,192},{160,224},{192,256},{22... | collective-permute-start | bytes 909320 | tf_op jit(solution)/shard_map/ppermute | solution.py:644
  25.9 3.3 %copy-start.1 = (s32[32]{0:T(128)S(1)}, s32[32]{0:T(128)}, u32[]{:S(2)}) copy-start(s32[32]{0:T(128)} %cells_ref.1) | copy-start | bytes 388
  25.9 3.2 %copy-start.2 = (f32[32]{0:T(128)S(1)}, f32[32]{0:T(128)}, u32[]{:S(2)}) copy-start(f32[32]{0:T(128)} %rate_ref.1) | copy-start | bytes 388
  25.9 10.2 %collective-permute-start.7 = (f32[512,128]{1,0:T(8,128)S(1)}, f32[512,128]{1,0:T(8,128)S(1)}, u32[]{:S(2)}, u32[]{:S(2)}) collective-permute-start(f32[512,128]{1,0:T(8,128)S(1)} %get-tuple-element.37), channel_id=1, source_target_pairs={{0,64},{32,96},{64,128},{96,160},{128,192},{160,224},{192,256},{22... | collective-permute-start | bytes 786440 | tf_op jit(solution)/shard_map/ppermute | solution.py:644
  27.9 8.2 %collective-permute-start.8 = (f32[512,128]{1,0:T(8,128)S(1)}, f32[512,128]{1,0:T(8,128)S(1)}, u32[]{:S(2)}, u32[]{:S(2)}) collective-permute-start(f32[512,128]{1,0:T(8,128)S(1)} %get-tuple-element.38), channel_id=1, source_target_pairs={{64,0},{96,32},{128,64},{160,96},{192,128},{224,160},{256,192},{28... | collective-permute-start | bytes 786440 | tf_op jit(solution)/shard_map/ppermute | solution.py:645
  41.2 8.2 %collective-permute-start.9 = (f32[592,128]{1,0:T(8,128)S(1)}, f32[592,128]{1,0:T(8,128)S(1)}, u32[]{:S(2)}, u32[]{:S(2)}) collective-permute-start(f32[592,128]{1,0:T(8,128)S(1)} %get-tuple-element.45), channel_id=1, source_target_pairs={{0,64},{32,96},{64,128},{96,160},{128,192},{160,224},{192,256},{22... | collective-permute-start | bytes 909320 | tf_op jit(solution)/shard_map/ppermute | solution.py:644
  45.7 7.6 %collective-permute-start.10 = (f32[592,128]{1,0:T(8,128)S(1)}, f32[592,128]{1,0:T(8,128)S(1)}, u32[]{:S(2)}, u32[]{:S(2)}) collective-permute-start(f32[592,128]{1,0:T(8,128)S(1)} %get-tuple-element.46), channel_id=1, source_target_pairs={{64,0},{96,32},{128,64},{160,96},{192,128},{224,160},{256,192},{28... | collective-permute-start | bytes 909320 | tf_op jit(solution)/shard_map/ppermute | solution.py:645
  53.2 10.2 %copy-start = (f32[64,1,8,128]{3,2,1,0:T(8,128)S(1)}, f32[64,1,8,128]{3,2,1,0:T(8,128)}, u32[]{:S(2)}) copy-start(f32[64,1,8,128]{3,2,1,0:T(8,128)} %param.7) | copy-start | bytes 786436
  55.6 7.8 %collective-permute-start.11 = (f32[1024,128]{1,0:T(8,128)S(1)}, f32[1024,128]{1,0:T(8,128)S(1)}, u32[]{:S(2)}, u32[]{:S(2)}) collective-permute-start(f32[1024,128]{1,0:T(8,128)S(1)} %get-tuple-element.48), channel_id=1, source_target_pairs={{0,32},{32,0},{64,96},{96,64},{128,160},{160,128},{192,224},{224,1... | collective-permute-start | bytes 1572872 | tf_op jit(solution)/shard_map/ppermute | solution.py:660

commit v5 on v4

--- a/solution.py
+++ b/solution.py
@@ -242,7 +242,7 @@
                 put(coef_ref, (s * 7 + index) * 4 + part, value)
         return carry
 
-    lax.fori_loop(0, 4, plane, 0)
+    lax.fori_loop(0, 4, plane, 0, unroll=True)
 
 
 def step(source, target, coef_ref, first, count, coef_shift, out_shift, with_my=True, with_em=True, with_ey=True):
@@ -508,19 +508,17 @@
     def column(value, at):
         return jnp.broadcast_to(value[:, at : at + 1], (8, 128))
 
-    for i in range(M // 8):
-        columns = [[column(t, 8 * i + b) for b in range(8)] for t in tiles]
-        row = [jnp.broadcast_to(tiles[i][a : a + 1, :], (8, 128)) for a in range(8)]
-        small = [
-            [jnp.broadcast_to(columns[i][b][a : a + 1, :], (8, 128)) for b in range(8)]
-            for a in range(8)
-        ]
+    def block(_, tiles):
+        tiles = list(tiles)
+        columns = [column(tiles[0], b) for b in range(8)]
+        row = [jnp.broadcast_to(tiles[0][a : a + 1, :], (8, 128)) for a in range(8)]
+        small = [[jnp.broadcast_to(columns[b][a : a + 1, :], (8, 128)) for b in range(8)] for a in range(8)]
         for p in range(8):
             inverse = 1.0 / small[p][p]
             for a in range(p + 1, 8):
-                factor = small[a][p] * inverse
+                factor = small[p][a] * inverse
                 row[a] = row[a] - factor * row[p]
-                for b in range(p + 1, 8):
+                for b in range(a, 8):
                     small[a][b] = small[a][b] - factor * small[p][b]
             row[p] = row[p] * inverse
             for b in range(p + 1, 8):
@@ -528,17 +526,19 @@
         for p in range(7, 0, -1):
             for a in range(p):
                 row[a] = row[a] - small[a][p] * row[p]
-        for j in range(M // 8):
-            if j == i:
-                value = row[0]
-                for b in range(1, 8):
-                    value = jnp.where(rows == b, row[b], value)
-            else:
-                value = tiles[j]
-                for b in range(8):
-                    value = value - columns[j][b] * row[b]
+        for j in range(1, M // 8):
+            value = tiles[j]
+            for b in range(8):
+                value = value - column(tiles[j], b) * row[b]
             tiles[j] = value
-    return jnp.concatenate(tiles, axis=0)[:, M:]
+        value = row[0]
+        for b in range(1, 8):
+            value = jnp.where(rows == b, row[b], value)
+        tiles[0] = value
+        return tuple(roll_lane(t, -8) for t in tiles[1:] + tiles[:1])
+
+    tiles = lax.fori_loop(0, M // 8, block, tuple(tiles), unroll=1)
+    return jnp.concatenate(tiles, axis=0)[:, :M]
 
 
 def apply_levels(blocks):

time: 135 us -> 132 us (0.978)
  Pallas kernels: 22.6 us -> 19.8 us
    pallas_call x1, Pallas kernels: 11.4 us -> 9.47 us  [per_device(): call(final_kernel, 'final', (f32(8 * M, 128), f32(8 * M, 128)), [VMEM] *...]
where the time goes in v5:
time: 132 us; the launch traced here: 130 us
  blocking collectives  56.4 us (43%)
  starting transfers between devices  37.3 us (28%)
  Pallas kernels  19.8 us (15%)
  waiting for transfers between devices  15.7 us (12%)
    all_to_all x2, blocking collectives, spread(): lax.all_to_all(jnp.broadcast_to(values, (count, *values.shape)), axes, 0, 0)  34.4 us
    all_to_all x1, blocking collectives, per_device(): gram = lax.all_to_all(gram.reshape(count, -1, 128), plane, 0, 0)  22 us
    ppermute x5, starting transfers between devices, from_sides(): lower = lax.ppermute(up, axis, [(i, i + by) for i in range(count - by)])  15.7 us
    ppermute x2, starting transfers between devices, other_core(): return lax.ppermute(values, 'gx', [(i, i ^ 1) for i in range(count)])  15.1 us
    pallas_call x1, Pallas kernels, per_device(): call(final_kernel, 'final', (f32(8 * M, 128), f32(8 * M, 128)), [VMEM] *...  9.47 us
    ppermute x5, waiting for transfers between devices, from_sides(): lower = lax.ppermute(up, axis, [(i, i + by) for i in range(count - by)])  9.38 us
    ppermute x5, starting transfers between devices, from_sides(): upper = lax.ppermute(down, axis, [(i + by, i) for i in range(count - by)])  6.46 us
    pallas_call x1, Pallas kernels, per_device(): call(functools.partial(first_two_kernel, sizes), 'first_two', (tiles(4 *...  4.19 us
  transfers between devices with their start and end apart: 12, of which 7 were waited for; matrix products, arithmetic and copies ran while one was open for 0% of the time, Pallas kernels for 1%

profile of v5, /device:TPU:1, one launch (start us, length us, event | category | flops | bytes accessed | tf_op | source)
XLA Modules:
  0.0 130.2 jit_solution(10196398469442424112)
XLA Ops:
  0.6 1.1 pack.1
  1.7 8.8 %collective-permute-start = (f32[296,128]{1,0:T(8,128)S(1)}, f32[296,128]{1,0:T(8,128)S(1)}, u32[]{:S(2)}, u32[]{:S(2)}) collective-permute-start(f32[296,128]{1,0:T(8,128)S(1)} %get-tuple-element.29), channel_id=1, source_target_pairs={{0,32},{32,0},{64,96},{96,64},{128,160},{160,128},{192,224},{224,1... | collective-permute-start | bytes 454664 | tf_op jit(solution)/shard_map/ppermute | solution.py:660
  11.7 1.3 collective-permute-start.2
  13.0 4.0 %collective-permute-start.1 = (f32[40,128]{1,0:T(8,128)S(1)}, f32[40,128]{1,0:T(8,128)S(1)}, u32[]{:S(2)}, u32[]{:S(2)}) collective-permute-start(f32[40,128]{1,0:T(8,128)S(1)} %get-tuple-element.31), channel_id=1, source_target_pairs={{0,1},{1,2},{2,3},{4,5},{5,6},{6,7},{8,9},{9,10},{10,11},{12,13},{... | collective-permute-start | bytes 61448 | tf_op jit(solution)/shard_map/ppermute | solution.py:644
  17.9 1.3 collective-permute-start.3
  19.2 1.3 collective-permute-start.4
  20.5 1.3 collective-permute-start.6
  21.8 4.0 %collective-permute-start.5 = (f32[592,128]{1,0:T(8,128)S(1)}, f32[592,128]{1,0:T(8,128)S(1)}, u32[]{:S(2)}, u32[]{:S(2)}) collective-permute-start(f32[592,128]{1,0:T(8,128)S(1)} %get-tuple-element.30.main_ref), channel_id=1, source_target_pairs={{0,64},{32,96},{64,128},{96,160},{128,192},{160,224},{192,256},{22... | collective-permute-start | bytes 909320 | tf_op jit(solution)/shard_map/ppermute | solution.py:644
  25.9 1.9 %collective-permute-start.7 = (f32[512,128]{1,0:T(8,128)S(1)}, f32[512,128]{1,0:T(8,128)S(1)}, u32[]{:S(2)}, u32[]{:S(2)}) collective-permute-start(f32[512,128]{1,0:T(8,128)S(1)} %get-tuple-element.37), channel_id=1, source_target_pairs={{0,64},{32,96},{64,128},{96,160},{128,192},{160,224},{192,256},{22... | collective-permute-start | bytes 786440 | tf_op jit(solution)/shard_map/ppermute | solution.py:644
  27.9 1.3 collective-permute-start.8
  30.5 5.6 %collective-permute-done.7.left_ref = f32[512,128]{1,0:T(8,128)S(1)} collective-permute-done((f32[512,128]{1,0:T(8,128)S(1)}, f32[512,128]{1,0:T(8,128)S(1)}, u32[]{:S(2)}, u32[]{:S(2)}) %collective-permute-start.7) | collective-permute-done | bytes 262176 | tf_op jit(solution)/shard_map/ppermute | solution.py:644
  36.1 4.2 %first_two.1 = (f32[896,128]{1,0:T(8,128)S(1)}, f32[512,128]{1,0:T(8,128)S(1)}, f32[512,128]{1,0:T(8,128)S(1)}, f32[512,128]{1,0:T(8,128)S(1)}, f32[32,128]{1,0:...) custom-call(f32[128,128]{1,0:T(8,128)S(1)} %wells.1.wells_ref, ...), custom_call_target="tpu_custom_call" | custom-call | tf_op jit(solution)/shard_map/first_two/pallas_call | solution.py:706
  40.3 4.5 %collective-permute-start.9 = (f32[592,128]{1,0:T(8,128)S(1)}, f32[592,128]{1,0:T(8,128)S(1)}, u32[]{:S(2)}, u32[]{:S(2)}) collective-permute-start(f32[592,128]{1,0:T(8,128)S(1)} %get-tuple-element.45), channel_id=1, source_target_pairs={{0,64},{32,96},{64,128},{96,160},{128,192},{160,224},{192,256},{22... | collective-permute-start | bytes 909320 | tf_op jit(solution)/shard_map/ppermute | solution.py:644
  44.8 1.3 collective-permute-start.10
  46.1 2.4 %collective-permute-done.9.left_ref = f32[592,128]{1,0:T(8,128)S(1)} collective-permute-done((f32[592,128]{1,0:T(8,128)S(1)}, f32[592,128]{1,0:T(8,128)S(1)}, u32[]{:S(2)}, u32[]{:S(2)}) %collective-permute-start.9) | collective-permute-done | bytes 303136 | tf_op jit(solution)/shard_map/ppermute | solution.py:644
  48.5 3.8 %collective-permute-done.10.right_ref = f32[592,128]{1,0:T(8,128)S(1)} collective-permute-done((f32[592,128]{1,0:T(8,128)S(1)}, f32[592,128]{1,0:T(8,128)S(1)}, u32[]{:S(2)}, u32[]{:S(2)}) %collective-permute-start.10) | collective-permute-done | bytes 303136 | tf_op jit(solution)/shard_map/ppermute | solution.py:645
  52.4 2.4 %last_two.1 = (f32[1024,128]{1,0:T(8,128)S(1)}, f32[1024,128]{1,0:T(8,128)S(1)}) custom-call(f32[896,128]{1,0:T(8,128)S(1)} %get-tuple-element.39.coef_ref, f32[512,128]{1,0:T(8,128)S(1)} %get-tuple-element.40.block_1_ref, f32[512,128]{1,0:T(8,128)S(1)} %get-tuple-element.41.block_2_ref, f32[512,128]{1,0:T(8,128)S(1)} %get-tuple-element.42.my_2_ref, ...), custom_call_target="tpu_custom_call" | custom-call | tf_op jit(solution)/shard_map/last_two/pallas_call | solution.py:723
  54.7 6.3 %collective-permute-start.11 = (f32[1024,128]{1,0:T(8,128)S(1)}, f32[1024,128]{1,0:T(8,128)S(1)}, u32[]{:S(2)}, u32[]{:S(2)}) collective-permute-start(f32[1024,128]{1,0:T(8,128)S(1)} %get-tuple-element.48), channel_id=1, source_target_pairs={{0,32},{32,0},{64,96},{96,64},{128,160},{160,128},{192,224},{224,1... | collective-permute-start | bytes 1572872 | tf_op jit(solution)/shard_map/ppermute | solution.py:660
  61.1 1.5 %collective-permute-done.11.got_ref = f32[1024,128]{1,0:T(8,128)S(1)} collective-permute-done((f32[1024,128]{1,0:T(8,128)S(1)}, f32[1024,128]{1,0:T(8,128)S(1)}, u32[]{:S(2)}, u32[]{:S(2)}) %collective-permute-start.11) | collective-permute-done | bytes 524320 | tf_op jit(solution)/shard_map/ppermute | solution.py:660
  62.6 1.6 %gram.1 = (bf16[320,1024]{1,0:T(8,128)(2,1)S(1)}, bf16[320,1024]{1,0:T(8,128)(2,1)S(1)}, f32[512,128]{1,0:T(8,128)S(1)}) custom-call(f32[512,128]{1,0:T(8,128)S(1)} %bitcast.13, f32[1024,128]{1,0:T(8,128)S(1)} %get-tuple-element.47.keep_ref, f32[1024,128]{1,0:T(8,128)S(1)} %collective-permute-done.11.got_ref), custom_call_target="tpu_custom_call" | custom-call | tf_op jit(solution)/shard_map/gram/pallas_call | solution.py:732
  64.2 22.0 %all_to_all.15 = f32[32,16,128]{2,1,0:T(8,128)S(1)} all-to-all(f32[32,16,128]{2,1,0:T(8,128)S(1)} %bitcast.15), channel_id=1, replica_groups=mesh['gx'=16,'gy'=8,'gz'=4] {'gz','gy'}, dimensions={0} | all-to-all | bytes 524288 | tf_op jit(solution)/shard_map/all_to_all | solution.py:742
  86.2 19.8 %all_to_all.16 = f32[16,16,128]{2,1,0:T(8,128)S(1)} all-to-all(f32[16,16,128]{2,1,0:T(8,128)S(1)} %broadcast_in_dim.6), channel_id=1, replica_groups=mesh['gx'=16,'gy'=8,'gz'=4] {'gx'}, dimensions={0} | all-to-all | bytes 262144 | tf_op jit(solution)/shard_map/all_to_all | solution.py:651
  106.1 14.6 %all_to_all.17 = f32[32,16,128]{2,1,0:T(8,128)S(1)} all-to-all(f32[32,16,128]{2,1,0:T(8,128)S(1)} %broadcast_in_dim.7), channel_id=1, replica_groups=mesh['gx'=16,'gy'=8,'gz'=4] {'gz','gy'}, dimensions={0} | all-to-all | bytes 524288 | tf_op jit(solution)/shard_map/all_to_all | solution.py:651
  120.7 9.5 %final.1 = (f32[512,128]{1,0:T(8,128)}, f32[512,128]{1,0:T(8,128)}) custom-call(f32[512,128]{1,0:T(8,128)S(1)} %bitcast.14, bf16[320,1024]{1,0:T(8,128)(2,1)S(1)} %get-tuple-element.50.high_ref, bf16[320,1024]{1,0:T(8,128)(2,1)S(1)} %get-tuple-element.51.low_ref), custom_call_target="tpu_custom_call" | custom-call | tf_op jit(solution)/shard_map/final/pallas_call | solution.py:746
  (22 shorter events, 3.5 us)
Async XLA Ops:
  1.7 9.8 %collective-permute-start = (f32[296,128]{1,0:T(8,128)S(1)}, f32[296,128]{1,0:T(8,128)S(1)}, u32[]{:S(2)}, u32[]{:S(2)}) collective-permute-start(f32[296,128]{1,0:T(8,128)S(1)} %get-tuple-element.29), channel_id=1, source_target_pairs={{0,32},{32,0},{64,96},{96,64},{128,160},{160,128},{192,224},{224,1... | collective-permute-start | bytes 454664 | tf_op jit(solution)/shard_map/ppermute | solution.py:660
  11.7 5.3 %collective-permute-start.2 = (f32[40,128]{1,0:T(8,128)S(1)}, f32[40,128]{1,0:T(8,128)S(1)}, u32[]{:S(2)}, u32[]{:S(2)}) collective-permute-start(f32[40,128]{1,0:T(8,128)S(1)} %get-tuple-element.31), channel_id=1, source_target_pairs={{1,0},{2,1},{3,2},{5,4},{6,5},{7,6},{9,8},{10,9},{11,10},{13,12},{... | collective-permute-start | bytes 61448 | tf_op jit(solution)/shard_map/ppermute | solution.py:645
  13.0 4.9 %collective-permute-start.1 = (f32[40,128]{1,0:T(8,128)S(1)}, f32[40,128]{1,0:T(8,128)S(1)}, u32[]{:S(2)}, u32[]{:S(2)}) collective-permute-start(f32[40,128]{1,0:T(8,128)S(1)} %get-tuple-element.31), channel_id=1, source_target_pairs={{0,1},{1,2},{2,3},{4,5},{5,6},{6,7},{8,9},{9,10},{10,11},{12,13},{... | collective-permute-start | bytes 61448 | tf_op jit(solution)/shard_map/ppermute | solution.py:644
  17.9 7.9 %collective-permute-start.3 = (f32[320,128]{1,0:T(8,128)S(1)}, f32[320,128]{1,0:T(8,128)S(1)}, u32[]{:S(2)}, u32[]{:S(2)}) collective-permute-start(f32[320,128]{1,0:T(8,128)S(1)} %get-tuple-element.33), channel_id=1, source_target_pairs={{0,4},{4,8},{8,12},{12,16},{16,20},{20,24},{24,28},{1,5},{5,9},{9,... | collective-permute-start | bytes 491528 | tf_op jit(solution)/shard_map/ppermute | solution.py:644
  19.2 6.6 %collective-permute-start.4 = (f32[320,128]{1,0:T(8,128)S(1)}, f32[320,128]{1,0:T(8,128)S(1)}, u32[]{:S(2)}, u32[]{:S(2)}) collective-permute-start(f32[320,128]{1,0:T(8,128)S(1)} %get-tuple-element.34), channel_id=1, source_target_pairs={{4,0},{8,4},{12,8},{16,12},{20,16},{24,20},{28,24},{5,1},{9,5},{13... | collective-permute-start | bytes 491528 | tf_op jit(solution)/shard_map/ppermute | solution.py:645
  20.5 9.5 %collective-permute-start.6 = (f32[592,128]{1,0:T(8,128)S(1)}, f32[592,128]{1,0:T(8,128)S(1)}, u32[]{:S(2)}, u32[]{:S(2)}) collective-permute-start(f32[592,128]{1,0:T(8,128)S(1)} %get-tuple-element.30.main_ref), channel_id=1, source_target_pairs={{64,0},{96,32},{128,64},{160,96},{192,128},{224,160},{256,192},{28... | collective-permute-start | bytes 909320 | tf_op jit(solution)/shard_map/ppermute | solution.py:645
  21.8 8.7 %collective-permute-start.5 = (f32[592,128]{1,0:T(8,128)S(1)}, f32[592,128]{1,0:T(8,128)S(1)}, u32[]{:S(2)}, u32[]{:S(2)}) collective-permute-start(f32[592,128]{1,0:T(8,128)S(1)} %get-tuple-element.30.main_ref), channel_id=1, source_target_pairs={{0,64},{32,96},{64,128},{96,160},{128,192},{160,224},{192,256},{22... | collective-permute-start | bytes 909320 | tf_op jit(solution)/shard_map/ppermute | solution.py:644
  25.9 3.3 %copy-start.1 = (s32[32]{0:T(128)S(1)}, s32[32]{0:T(128)}, u32[]{:S(2)}) copy-start(s32[32]{0:T(128)} %cells_ref.1) | copy-start | bytes 388
  25.9 3.2 %copy-start.2 = (f32[32]{0:T(128)S(1)}, f32[32]{0:T(128)}, u32[]{:S(2)}) copy-start(f32[32]{0:T(128)} %rate_ref.1) | copy-start | bytes 388
  25.9 10.2 %collective-permute-start.7 = (f32[512,128]{1,0:T(8,128)S(1)}, f32[512,128]{1,0:T(8,128)S(1)}, u32[]{:S(2)}, u32[]{:S(2)}) collective-permute-start(f32[512,128]{1,0:T(8,128)S(1)} %get-tuple-element.37), channel_id=1, source_target_pairs={{0,64},{32,96},{64,128},{96,160},{128,192},{160,224},{192,256},{22... | collective-permute-start | bytes 786440 | tf_op jit(solution)/shard_map/ppermute | solution.py:644
  27.9 8.2 %collective-permute-start.8 = (f32[512,128]{1,0:T(8,128)S(1)}, f32[512,128]{1,0:T(8,128)S(1)}, u32[]{:S(2)}, u32[]{:S(2)}) collective-permute-start(f32[512,128]{1,0:T(8,128)S(1)} %get-tuple-element.38), channel_id=1, source_target_pairs={{64,0},{96,32},{128,64},{160,96},{192,128},{224,160},{256,192},{28... | collective-permute-start | bytes 786440 | tf_op jit(solution)/shard_map/ppermute | solution.py:645
  40.3 8.2 %collective-permute-start.9 = (f32[592,128]{1,0:T(8,128)S(1)}, f32[592,128]{1,0:T(8,128)S(1)}, u32[]{:S(2)}, u32[]{:S(2)}) collective-permute-start(f32[592,128]{1,0:T(8,128)S(1)} %get-tuple-element.45), channel_id=1, source_target_pairs={{0,64},{32,96},{64,128},{96,160},{128,192},{160,224},{192,256},{22... | collective-permute-start | bytes 909320 | tf_op jit(solution)/shard_map/ppermute | solution.py:644
  44.8 7.6 %collective-permute-start.10 = (f32[592,128]{1,0:T(8,128)S(1)}, f32[592,128]{1,0:T(8,128)S(1)}, u32[]{:S(2)}, u32[]{:S(2)}) collective-permute-start(f32[592,128]{1,0:T(8,128)S(1)} %get-tuple-element.46), channel_id=1, source_target_pairs={{64,0},{96,32},{128,64},{160,96},{192,128},{224,160},{256,192},{28... | collective-permute-start | bytes 909320 | tf_op jit(solution)/shard_map/ppermute | solution.py:645
  52.4 10.2 %copy-start = (f32[64,1,8,128]{3,2,1,0:T(8,128)S(1)}, f32[64,1,8,128]{3,2,1,0:T(8,128)}, u32[]{:S(2)}) copy-start(f32[64,1,8,128]{3,2,1,0:T(8,128)} %param.7) | copy-start | bytes 786436
  54.7 7.8 %collective-permute-start.11 = (f32[1024,128]{1,0:T(8,128)S(1)}, f32[1024,128]{1,0:T(8,128)S(1)}, u32[]{:S(2)}, u32[]{:S(2)}) collective-permute-start(f32[1024,128]{1,0:T(8,128)S(1)} %get-tuple-element.48), channel_id=1, source_target_pairs={{0,32},{32,0},{64,96},{96,64},{128,160},{160,128},{192,224},{224,1... | collective-permute-start | bytes 1572872 | tf_op jit(solution)/shard_map/ppermute | solution.py:660

commit v6 on v5

--- a/solution.py
+++ b/solution.py
@@ -324,7 +324,8 @@
     left_ref,
     right_ref,
     coef_ref,
-    block_1_ref,
+    keep_ref,
+    send_ref,
     block_2_ref,
     my_2_ref,
     em_2_ref,
@@ -387,7 +388,6 @@
                     put(given_ref, ((plane - 1) * 4 + e) * 4 + part, value)
     plane_coefficients(sizes, wells_ref, conduct_ref, given_ref, coef_ref)
     step((main_0, my_0, em_0, ey_0), (main_1, my_1, em_1, ey_1), coef_ref, 1, 4, -1, -1)
-    copy_tiles(main_1, HALF, block_1_ref, 0, 2 * HALF)
     step((main_1, my_1, em_1, ey_1), (block_2_ref, my_2_ref, em_2_ref, ey_2_ref), coef_ref, 1, 2, 0, -1)
     for p, (adjacent, second) in enumerate(((to_left_ref, to_right_ref), (to_right_ref, to_left_ref))):
         for i in range(HALF):
@@ -401,17 +401,26 @@
                 value = jnp.where(at_row, roll_row(tile(my_2_ref, HALF * p + 4 * i + k), 2 * k), value)
             put(adjacent, B_MY + i, value)
         copy_tiles(em_2_ref, TG * p, adjacent, B_EDGE, TG)
+    by_plane(((main_1, HALF), (block_2_ref, 0)), keep_ref, send_ref)
+
+
+def by_plane(levels, keep_ref, send_ref):
+    mine, other = core() * HALF, (1 - core()) * HALF
+    for level, (ref, base) in enumerate(levels):
+        for i in range(HALF):
+            put(keep_ref, HALF * level + i, tile(ref, base + mine + i))
+            put(send_ref, HALF * level + i, tile(ref, base + other + i))
 
 
 def last_two_kernel(
     coef_ref,
-    block_1_ref,
     block_2_ref,
     my_2_ref,
     em_2_ref,
     ey_2_ref,
     left_ref,
     right_ref,
+    _,
     keep_ref,
     send_ref,
     main_2,
@@ -440,11 +449,7 @@
         step(source, target, coef_ref, plane, 1, -1, -1, False, False, False)
     step(source, target, coef_ref, 2, 2, -1, -1, True, True, False)
     step((main_3, my_3, em_3, None), (main_4, None, None, None), coef_ref, 1, 2, 0, -1, False, False, False)
-    mine, other = core() * HALF, (1 - core()) * HALF
-    for level, (ref, base) in enumerate(((block_1_ref, 0), (block_2_ref, 0), (main_3, HALF), (main_4, 0))):
-        for i in range(HALF):
-            put(keep_ref, HALF * level + i, tile(ref, base + mine + i))
-            put(send_ref, HALF * level + i, tile(ref, base + other + i))
+    by_plane(((main_3, HALF), (main_4, 0)), keep_ref, send_ref)
 
 
 PAIRS = (
@@ -479,24 +484,43 @@
     return lax.dot_general(first, second, (((1,), (0,)), ((), ())), precision=HI, preferred_element_type=jnp.float32)
 
 
-def gram_kernel(block_0, keep_ref, got_ref, high_ref, low_ref, gram_ref, basis_ref):
+def fill_levels(keep_ref, got_ref, basis_ref, base):
     mine, other = core() * HALF, (1 - core()) * HALF
     for y in range(8):
         lanes = slice(128 * y, 128 * (y + 1))
-        basis_ref[0:M, lanes] = block_0[pl.ds(y, M, stride=8), :]
-        for level in range(1, LEVELS):
-            at = pl.ds(8 * HALF * (level - 1) + y, HALF, stride=8)
-            basis_ref[pl.ds(pl.multiple_of(M * level + mine, 8), HALF), lanes] = keep_ref[at, :]
-            basis_ref[pl.ds(pl.multiple_of(M * level + other, 8), HALF), lanes] = got_ref[at, :]
+        for level in range(2):
+            at = pl.ds(8 * HALF * level + y, HALF, stride=8)
+            rows = base + M * level
+            basis_ref[pl.ds(pl.multiple_of(rows + mine, 8), HALF), lanes] = keep_ref[at, :]
+            basis_ref[pl.ds(pl.multiple_of(rows + other, 8), HALF), lanes] = got_ref[at, :]
+
+
+def early_gram_kernel(block_0, keep_ref, got_ref, high_ref, low_ref, full_ref, basis_ref):
+    for y in range(8):
+        basis_ref[0:M, 128 * y : 128 * (y + 1)] = block_0[pl.ds(y, M, stride=8), :]
+    fill_levels(keep_ref, got_ref, basis_ref, M)
     parts = two_parts(basis_ref[...])
     high_ref[...], low_ref[...] = parts
-    full = three_products(parts, parts, ((1,), (1,)))
+    full_ref[...] = three_products(parts, parts, ((1,), (1,)))
+
+
+def gram_kernel(keep_ref, got_ref, early_high, early_low, early_full, high_ref, low_ref, gram_ref, basis_ref):
+    fill_levels(keep_ref, got_ref, basis_ref, 0)
+    parts = two_parts(basis_ref[...])
+    high_ref[...], low_ref[...] = parts
+    among = three_products(parts, parts, ((1,), (1,)))
+    across = three_products((early_high[...], early_low[...]), parts, ((1,), (1,)))
     for index, pair in enumerate(PAIRS):
         for half, at in enumerate(pair):
             if at is None:
                 value = jnp.zeros((M, M), jnp.float32)
             else:
-                value = full[M * at[0] : M * at[0] + M, M * at[1] : M * at[1] + M]
+                first, second = (slice(M * k, M * k + M) for k in at)
+                if at[1] < 3:
+                    value = early_full[first, second]
+                else:
+                    source, shift = (among, 3 * M) if at[0] >= 3 else (across, 0)
+                    value = source[first.start - shift : first.stop - shift, second.start - 3 * M : second.stop - 3 * M]
             gram_ref[M * index : M * (index + 1), M * half : M * (half + 1)] = value
 
 
@@ -552,7 +576,7 @@
     return list(blocks) + [jnp.zeros((M, M), jnp.float32)] * (count - len(blocks))
 
 
-def final_kernel(gram_ref, high_ref, low_ref, field_ref, resid_ref, full_ref):
+def final_kernel(gram_ref, early_high, early_low, high_ref, low_ref, field_ref, resid_ref, full_ref):
     for index, pair in enumerate(PAIRS):
         for half, at in enumerate(pair):
             if at is None:
@@ -613,7 +637,9 @@
     field = pad_levels(field, 5)
     resid = [h - omega * s for h, s in zip(pad_levels(half, 5), second)]
     coefs = jnp.concatenate([jnp.concatenate(field, axis=0), jnp.concatenate(resid, axis=0)], axis=1)
-    result = three_products(two_parts(coefs.T), (high_ref[...], low_ref[...]), ((1,), (0,)))
+    coefs = coefs.T
+    result = three_products(two_parts(coefs[:, 0 : 3 * M]), (early_high[...], early_low[...]), ((1,), (0,)))
+    result = result + three_products(two_parts(coefs[:, 3 * M :]), (high_ref[...], low_ref[...]), ((1,), (0,)))
     for y in range(8):
         field_ref[pl.ds(y, M, stride=8), :] = result[0:M, 128 * y : 128 * (y + 1)]
         resid_ref[pl.ds(y, M, stride=8), :] = result[M:, 128 * y : 128 * (y + 1)]
@@ -703,12 +729,13 @@
         xmsg_kernel, "xmsg", (tiles(2 * SLOT), tiles(NE), tiles(A_TILES), tiles(A_TILES)), [VMEM] * 3
     )(edge, below, above)
     left, right = from_sides("gx", to_right, to_left, 2)
-    coef, block_1, block_2, my, em, ey, to_left, to_right = call(
+    coef, keep, send, block_2, my, em, ey, to_left, to_right = call(
         functools.partial(first_two_kernel, sizes),
         "first_two",
         (
             tiles(4 * 28),
-            tiles(M),
+            tiles(2 * HALF),
+            tiles(2 * HALF),
             tiles(M),
             tiles(M),
             tiles(2 * TG),
@@ -720,22 +747,33 @@
         scratch(24, 64, 6 * HALF, 6 * HALF, 6 * TG, 6 * TG, 4 * HALF, 4 * HALF, 4 * TG, 4 * TG),
     )(wells, main, edge, my, ey, left_main, right_main, left, right)
     left, right = from_sides("gx", to_right, to_left, 2)
+    got = other_core(send)
+
+    def rows(levels):
+        return jax.ShapeDtypeStruct((levels * M, 1024), jnp.bfloat16)
+
+    early_high, early_low, early_full = call(
+        early_gram_kernel,
+        "early_gram",
+        (rows(3), rows(3), f32(3 * M, 3 * M)),
+        [VMEM] * 3,
+        [pltpu.VMEM((3 * M, 1024), jnp.float32)],
+    )(block_0, keep, got)
     keep, send = call(
         last_two_kernel,
         "last_two",
-        (tiles(4 * HALF), tiles(4 * HALF)),
-        [VMEM] * 8,
+        (tiles(2 * HALF), tiles(2 * HALF)),
+        [VMEM] * 7 + [pl.BlockSpec(memory_space=pl.ANY)],
         scratch(6 * HALF, 6 * HALF, 6 * TG, 6 * TG, 4 * HALF, 4 * HALF, 4 * TG, 2 * HALF),
-    )(coef, block_1, block_2, my, em, ey, left, right)
+    )(coef, block_2, my, em, ey, left, right, early_full)
     got = other_core(send)
-    part = jax.ShapeDtypeStruct((LEVELS * M, 1024), jnp.bfloat16)
     high, low, gram = call(
         gram_kernel,
         "gram",
-        (part, part, f32(8 * M, 128)),
-        [VMEM] * 3,
-        [pltpu.VMEM((LEVELS * M, 1024), jnp.float32)],
-    )(block_0, keep, got)
+        (rows(2), rows(2), f32(8 * M, 128)),
+        [VMEM] * 5,
+        [pltpu.VMEM((2 * M, 1024), jnp.float32)],
+    )(keep, got, early_high, early_low, early_full)
 
     plane = ("gz", "gy")
     count = lax.axis_size(plane)
@@ -747,9 +785,9 @@
         final_kernel,
         "final",
         (f32(8 * M, 128), f32(8 * M, 128)),
-        [VMEM] * 3,
+        [VMEM] * 5,
         [pltpu.VMEM((LEVELS * M, LEVELS * M), jnp.float32)],
-    )(gram, high, low)
+    )(gram, early_high, early_low, high, low)
     return field.reshape(right_side.shape), resid.reshape(right_side.shape)
 
 

time: 132 us -> 131 us (level)
  waiting for transfers between devices: 15.7 us -> 10.3 us
  starting transfers between devices: 37.3 us -> 41.6 us
    ppermute x2 -> x3, starting transfers between devices: 15.1 us -> 19.4 us  [other_core(): return lax.ppermute(values, 'gx', [(i, i ^ 1) for i in range(count)])]
    ppermute x5, waiting for transfers between devices: 3.85 us -> 0.01 us  [from_sides(): upper = lax.ppermute(down, axis, [(i + by, i) for i in range(count - by)])]
    ppermute x5, waiting for transfers between devices: 9.38 us -> 6.97 us  [from_sides(): lower = lax.ppermute(up, axis, [(i, i + by) for i in range(count - by)])]
    ppermute x2 -> x3, waiting for transfers between devices: 2.51 us -> 3.27 us  [other_core(): return lax.ppermute(values, 'gx', [(i, i ^ 1) for i in range(count)])]
    pallas_call x2 -> x3, Pallas kernels: 3.98 us -> 4.07 us  [the longest x1 2.34 us: per_device(): call(last_two_kernel, 'last_two', (tiles(2 * HALF), tiles(2 * HALF)), [VM...]
  transfers between devices with their start and end apart: 12 -> 13, of which waited for: 7 -> 6; matrix products, arithmetic and copies ran while one was open for 0% -> 0% of each run, Pallas kernels for 1% -> 1%
where the time goes in v6:
time: 131 us; the launch traced here: 129 us
  blocking collectives  56.4 us (43%)
  starting transfers between devices  41.6 us (32%)
  Pallas kernels  20 us (15%)
  waiting for transfers between devices  10.3 us (8%)
    all_to_all x2, blocking collectives, spread(): lax.all_to_all(jnp.broadcast_to(values, (count, *values.shape)), axes, 0, 0)  34.4 us
    all_to_all x1, blocking collectives, per_device(): gram = lax.all_to_all(gram.reshape(count, -1, 128), plane, 0, 0)  22 us
    ppermute x3, starting transfers between devices, other_core(): return lax.ppermute(values, 'gx', [(i, i ^ 1) for i in range(count)])  19.4 us
    ppermute x5, starting transfers between devices, from_sides(): lower = lax.ppermute(up, axis, [(i, i + by) for i in range(count - by)])  15.7 us
    pallas_call x1, Pallas kernels, per_device(): call(final_kernel, 'final', (f32(8 * M, 128), f32(8 * M, 128)), [VMEM] *...  9.53 us
    ppermute x5, waiting for transfers between devices, from_sides(): lower = lax.ppermute(up, axis, [(i, i + by) for i in range(count - by)])  6.97 us
    ppermute x5, starting transfers between devices, from_sides(): upper = lax.ppermute(down, axis, [(i + by, i) for i in range(count - by)])  6.46 us
    pallas_call x1, Pallas kernels, per_device(): call(functools.partial(first_two_kernel, sizes), 'first_two', (tiles(4 *...  4.2 us
  transfers between devices with their start and end apart: 13, of which 6 were waited for; matrix products, arithmetic and copies ran while one was open for 0% of the time, Pallas kernels for 1%

profile of v6, /device:TPU:1, one launch (start us, length us, event | category | flops | bytes accessed | tf_op | source)
XLA Modules:
  0.0 129.2 jit_solution(14906455419611140566)
XLA Ops:
  0.6 1.1 pack.1
  1.7 8.8 %collective-permute-start = (f32[296,128]{1,0:T(8,128)S(1)}, f32[296,128]{1,0:T(8,128)S(1)}, u32[]{:S(2)}, u32[]{:S(2)}) collective-permute-start(f32[296,128]{1,0:T(8,128)S(1)} %get-tuple-element.33), channel_id=1, source_target_pairs={{0,32},{32,0},{64,96},{96,64},{128,160},{160,128},{192,224},{224,1... | collective-permute-start | bytes 454664 | tf_op jit(solution)/shard_map/ppermute | solution.py:686
  10.5 1.0 collective-permute-done.got_ref
  11.7 1.3 %collective-permute-start.2 = (f32[40,128]{1,0:T(8,128)S(1)}, f32[40,128]{1,0:T(8,128)S(1)}, u32[]{:S(2)}, u32[]{:S(2)}) collective-permute-start(f32[40,128]{1,0:T(8,128)S(1)} %get-tuple-element.35), channel_id=1, source_target_pairs={{1,0},{2,1},{3,2},{5,4},{6,5},{7,6},{9,8},{10,9},{11,10},{13,12},{... | collective-permute-start | bytes 61448 | tf_op jit(solution)/shard_map/ppermute | solution.py:671
  13.0 4.0 %collective-permute-start.1 = (f32[40,128]{1,0:T(8,128)S(1)}, f32[40,128]{1,0:T(8,128)S(1)}, u32[]{:S(2)}, u32[]{:S(2)}) collective-permute-start(f32[40,128]{1,0:T(8,128)S(1)} %get-tuple-element.35), channel_id=1, source_target_pairs={{0,1},{1,2},{2,3},{4,5},{5,6},{6,7},{8,9},{9,10},{10,11},{12,13},{... | collective-permute-start | bytes 61448 | tf_op jit(solution)/shard_map/ppermute | solution.py:670
  17.9 1.3 %collective-permute-start.3 = (f32[320,128]{1,0:T(8,128)S(1)}, f32[320,128]{1,0:T(8,128)S(1)}, u32[]{:S(2)}, u32[]{:S(2)}) collective-permute-start(f32[320,128]{1,0:T(8,128)S(1)} %get-tuple-element.37), channel_id=1, source_target_pairs={{0,4},{4,8},{8,12},{12,16},{16,20},{20,24},{24,28},{1,5},{5,9},{9,... | collective-permute-start | bytes 491528 | tf_op jit(solution)/shard_map/ppermute | solution.py:670
  19.2 1.3 %collective-permute-start.4 = (f32[320,128]{1,0:T(8,128)S(1)}, f32[320,128]{1,0:T(8,128)S(1)}, u32[]{:S(2)}, u32[]{:S(2)}) collective-permute-start(f32[320,128]{1,0:T(8,128)S(1)} %get-tuple-element.38), channel_id=1, source_target_pairs={{4,0},{8,4},{12,8},{16,12},{20,16},{24,20},{28,24},{5,1},{9,5},{13... | collective-permute-start | bytes 491528 | tf_op jit(solution)/shard_map/ppermute | solution.py:671
  20.5 1.3 %collective-permute-start.6 = (f32[592,128]{1,0:T(8,128)S(1)}, f32[592,128]{1,0:T(8,128)S(1)}, u32[]{:S(2)}, u32[]{:S(2)}) collective-permute-start(f32[592,128]{1,0:T(8,128)S(1)} %get-tuple-element.34.main_ref), channel_id=1, source_target_pairs={{64,0},{96,32},{128,64},{160,96},{192,128},{224,160},{256,192},{28... | collective-permute-start | bytes 909320 | tf_op jit(solution)/shard_map/ppermute | solution.py:671
  21.8 4.0 %collective-permute-start.5 = (f32[592,128]{1,0:T(8,128)S(1)}, f32[592,128]{1,0:T(8,128)S(1)}, u32[]{:S(2)}, u32[]{:S(2)}) collective-permute-start(f32[592,128]{1,0:T(8,128)S(1)} %get-tuple-element.34.main_ref), channel_id=1, source_target_pairs={{0,64},{32,96},{64,128},{96,160},{128,192},{160,224},{192,256},{22... | collective-permute-start | bytes 909320 | tf_op jit(solution)/shard_map/ppermute | solution.py:670
  25.9 1.9 %collective-permute-start.7 = (f32[512,128]{1,0:T(8,128)S(1)}, f32[512,128]{1,0:T(8,128)S(1)}, u32[]{:S(2)}, u32[]{:S(2)}) collective-permute-start(f32[512,128]{1,0:T(8,128)S(1)} %get-tuple-element.41), channel_id=1, source_target_pairs={{0,64},{32,96},{64,128},{96,160},{128,192},{160,224},{192,256},{22... | collective-permute-start | bytes 786440 | tf_op jit(solution)/shard_map/ppermute | solution.py:670
  27.9 1.3 %collective-permute-start.8 = (f32[512,128]{1,0:T(8,128)S(1)}, f32[512,128]{1,0:T(8,128)S(1)}, u32[]{:S(2)}, u32[]{:S(2)}) collective-permute-start(f32[512,128]{1,0:T(8,128)S(1)} %get-tuple-element.42), channel_id=1, source_target_pairs={{64,0},{96,32},{128,64},{160,96},{192,128},{224,160},{256,192},{28... | collective-permute-start | bytes 786440 | tf_op jit(solution)/shard_map/ppermute | solution.py:671
  30.5 5.6 %collective-permute-done.7.left_ref = f32[512,128]{1,0:T(8,128)S(1)} collective-permute-done((f32[512,128]{1,0:T(8,128)S(1)}, f32[512,128]{1,0:T(8,128)S(1)}, u32[]{:S(2)}, u32[]{:S(2)}) %collective-permute-start.7) | collective-permute-done | bytes 262176 | tf_op jit(solution)/shard_map/ppermute | solution.py:670
  36.1 4.2 %first_two.1 = (f32[896,128]{1,0:T(8,128)S(1)}, f32[512,128]{1,0:T(8,128)S(1)}, f32[512,128]{1,0:T(8,128)S(1)}, f32[512,128]{1,0:T(8,128)S(1)}, f32[512,128]{1,0...) custom-call(f32[128,128]{1,0:T(8,128)S(1)} %wells.1.wells_ref, ...), custom_call_target="tpu_custom_call" | custom-call | tf_op jit(solution)/shard_map/first_two/pallas_call | solution.py:732
  40.3 4.5 %collective-permute-start.9 = (f32[592,128]{1,0:T(8,128)S(1)}, f32[592,128]{1,0:T(8,128)S(1)}, u32[]{:S(2)}, u32[]{:S(2)}) collective-permute-start(f32[592,128]{1,0:T(8,128)S(1)} %get-tuple-element.48), channel_id=1, source_target_pairs={{0,64},{32,96},{64,128},{96,160},{128,192},{160,224},{192,256},{22... | collective-permute-start | bytes 909320 | tf_op jit(solution)/shard_map/ppermute | solution.py:670
  44.8 1.3 %collective-permute-start.10 = (f32[592,128]{1,0:T(8,128)S(1)}, f32[592,128]{1,0:T(8,128)S(1)}, u32[]{:S(2)}, u32[]{:S(2)}) collective-permute-start(f32[592,128]{1,0:T(8,128)S(1)} %get-tuple-element.49), channel_id=1, source_target_pairs={{64,0},{96,32},{128,64},{160,96},{192,128},{224,160},{256,192},{28... | collective-permute-start | bytes 909320 | tf_op jit(solution)/shard_map/ppermute | solution.py:671
  46.1 5.2 %collective-permute-start.11 = (f32[512,128]{1,0:T(8,128)S(1)}, f32[512,128]{1,0:T(8,128)S(1)}, u32[]{:S(2)}, u32[]{:S(2)}) collective-permute-start(f32[512,128]{1,0:T(8,128)S(1)} %get-tuple-element.51), channel_id=1, source_target_pairs={{0,32},{32,0},{64,96},{96,64},{128,160},{160,128},{192,224},{224,1... | collective-permute-start | bytes 786440 | tf_op jit(solution)/shard_map/ppermute | solution.py:686
  51.3 1.1 collective-permute-done.11.got_ref
  53.3 2.3 %last_two.1 = (f32[512,128]{1,0:T(8,128)S(1)}, f32[512,128]{1,0:T(8,128)S(1)}) custom-call(f32[896,128]{1,0:T(8,128)S(1)} %get-tuple-element.43.coef_ref, f32[512,128]{1,0:T(8,128)S(1)} %get-tuple-element.44.block_2_ref, f32[512,128]{1,0:T(8,128)S(1)} %get-tuple-element.45.my_2_ref, f32[32,128]{1,0:T(8,128)S(1)} %get-tuple-element.46.em_2_ref, ...), custom_call_target="tpu_custom_call" | custom-call | tf_op jit(solution)/shard_map/last_two/pallas_call | solution.py:762
  55.6 5.4 %collective-permute-start.12 = (f32[512,128]{1,0:T(8,128)S(1)}, f32[512,128]{1,0:T(8,128)S(1)}, u32[]{:S(2)}, u32[]{:S(2)}) collective-permute-start(f32[512,128]{1,0:T(8,128)S(1)} %get-tuple-element.54), channel_id=1, source_target_pairs={{0,32},{32,0},{64,96},{96,64},{128,160},{160,128},{192,224},{224,1... | collective-permute-start | bytes 786440 | tf_op jit(solution)/shard_map/ppermute | solution.py:686
  61.0 1.1 collective-permute-done.12.got_ref
  63.1 22.0 %all_to_all.15 = f32[32,16,128]{2,1,0:T(8,128)S(1)} all-to-all(f32[32,16,128]{2,1,0:T(8,128)S(1)} %bitcast.15), channel_id=1, replica_groups=mesh['gx'=16,'gy'=8,'gz'=4] {'gz','gy'}, dimensions={0} | all-to-all | bytes 524288 | tf_op jit(solution)/shard_map/all_to_all | solution.py:780
  85.1 19.8 %all_to_all.16 = f32[16,16,128]{2,1,0:T(8,128)S(1)} all-to-all(f32[16,16,128]{2,1,0:T(8,128)S(1)} %broadcast_in_dim.6), channel_id=1, replica_groups=mesh['gx'=16,'gy'=8,'gz'=4] {'gx'}, dimensions={0} | all-to-all | bytes 262144 | tf_op jit(solution)/shard_map/all_to_all | solution.py:677
  105.0 14.6 %all_to_all.17 = f32[32,16,128]{2,1,0:T(8,128)S(1)} all-to-all(f32[32,16,128]{2,1,0:T(8,128)S(1)} %broadcast_in_dim.7), channel_id=1, replica_groups=mesh['gx'=16,'gy'=8,'gz'=4] {'gz','gy'}, dimensions={0} | all-to-all | bytes 524288 | tf_op jit(solution)/shard_map/all_to_all | solution.py:677
  119.6 9.5 %final.1 = (f32[512,128]{1,0:T(8,128)}, f32[512,128]{1,0:T(8,128)}) custom-call(f32[512,128]{1,0:T(8,128)S(1)} %bitcast.14, bf16[192,1024]{1,0:T(8,128)(2,1)S(1)} %get-tuple-element.55.early_high, bf16[192,1024]{1,0:T(8,128)(2,1)S(1)} %get-tuple-element.56.early_low, bf16[128,1024]{1,0:T(8,128)(2,1)S(1)} %get-tuple-element.58.high_ref, ...), custom_call_target="tpu_custom_call" | custom-call | tf_op jit(solution)/shard_map/final/pallas_call | solution.py:784
  (25 shorter events, 4.3 us)
Async XLA Ops:
  1.7 9.8 %collective-permute-start = (f32[296,128]{1,0:T(8,128)S(1)}, f32[296,128]{1,0:T(8,128)S(1)}, u32[]{:S(2)}, u32[]{:S(2)}) collective-permute-start(f32[296,128]{1,0:T(8,128)S(1)} %get-tuple-element.33), channel_id=1, source_target_pairs={{0,32},{32,0},{64,96},{96,64},{128,160},{160,128},{192,224},{224,1... | collective-permute-start | bytes 454664 | tf_op jit(solution)/shard_map/ppermute | solution.py:686
  11.7 5.3 %collective-permute-start.2 = (f32[40,128]{1,0:T(8,128)S(1)}, f32[40,128]{1,0:T(8,128)S(1)}, u32[]{:S(2)}, u32[]{:S(2)}) collective-permute-start(f32[40,128]{1,0:T(8,128)S(1)} %get-tuple-element.35), channel_id=1, source_target_pairs={{1,0},{2,1},{3,2},{5,4},{6,5},{7,6},{9,8},{10,9},{11,10},{13,12},{... | collective-permute-start | bytes 61448 | tf_op jit(solution)/shard_map/ppermute | solution.py:671
  13.0 4.9 %collective-permute-start.1 = (f32[40,128]{1,0:T(8,128)S(1)}, f32[40,128]{1,0:T(8,128)S(1)}, u32[]{:S(2)}, u32[]{:S(2)}) collective-permute-start(f32[40,128]{1,0:T(8,128)S(1)} %get-tuple-element.35), channel_id=1, source_target_pairs={{0,1},{1,2},{2,3},{4,5},{5,6},{6,7},{8,9},{9,10},{10,11},{12,13},{... | collective-permute-start | bytes 61448 | tf_op jit(solution)/shard_map/ppermute | solution.py:670
  17.9 7.9 %collective-permute-start.3 = (f32[320,128]{1,0:T(8,128)S(1)}, f32[320,128]{1,0:T(8,128)S(1)}, u32[]{:S(2)}, u32[]{:S(2)}) collective-permute-start(f32[320,128]{1,0:T(8,128)S(1)} %get-tuple-element.37), channel_id=1, source_target_pairs={{0,4},{4,8},{8,12},{12,16},{16,20},{20,24},{24,28},{1,5},{5,9},{9,... | collective-permute-start | bytes 491528 | tf_op jit(solution)/shard_map/ppermute | solution.py:670
  19.2 6.6 %collective-permute-start.4 = (f32[320,128]{1,0:T(8,128)S(1)}, f32[320,128]{1,0:T(8,128)S(1)}, u32[]{:S(2)}, u32[]{:S(2)}) collective-permute-start(f32[320,128]{1,0:T(8,128)S(1)} %get-tuple-element.38), channel_id=1, source_target_pairs={{4,0},{8,4},{12,8},{16,12},{20,16},{24,20},{28,24},{5,1},{9,5},{13... | collective-permute-start | bytes 491528 | tf_op jit(solution)/shard_map/ppermute | solution.py:671
  20.5 9.5 %collective-permute-start.6 = (f32[592,128]{1,0:T(8,128)S(1)}, f32[592,128]{1,0:T(8,128)S(1)}, u32[]{:S(2)}, u32[]{:S(2)}) collective-permute-start(f32[592,128]{1,0:T(8,128)S(1)} %get-tuple-element.34.main_ref), channel_id=1, source_target_pairs={{64,0},{96,32},{128,64},{160,96},{192,128},{224,160},{256,192},{28... | collective-permute-start | bytes 909320 | tf_op jit(solution)/shard_map/ppermute | solution.py:671
  21.8 8.7 %collective-permute-start.5 = (f32[592,128]{1,0:T(8,128)S(1)}, f32[592,128]{1,0:T(8,128)S(1)}, u32[]{:S(2)}, u32[]{:S(2)}) collective-permute-start(f32[592,128]{1,0:T(8,128)S(1)} %get-tuple-element.34.main_ref), channel_id=1, source_target_pairs={{0,64},{32,96},{64,128},{96,160},{128,192},{160,224},{192,256},{22... | collective-permute-start | bytes 909320 | tf_op jit(solution)/shard_map/ppermute | solution.py:670
  25.9 3.3 %copy-start.1 = (s32[32]{0:T(128)S(1)}, s32[32]{0:T(128)}, u32[]{:S(2)}) copy-start(s32[32]{0:T(128)} %cells_ref.1) | copy-start | bytes 388
  25.9 3.2 %copy-start.2 = (f32[32]{0:T(128)S(1)}, f32[32]{0:T(128)}, u32[]{:S(2)}) copy-start(f32[32]{0:T(128)} %rate_ref.1) | copy-start | bytes 388
  25.9 10.2 %collective-permute-start.7 = (f32[512,128]{1,0:T(8,128)S(1)}, f32[512,128]{1,0:T(8,128)S(1)}, u32[]{:S(2)}, u32[]{:S(2)}) collective-permute-start(f32[512,128]{1,0:T(8,128)S(1)} %get-tuple-element.41), channel_id=1, source_target_pairs={{0,64},{32,96},{64,128},{96,160},{128,192},{160,224},{192,256},{22... | collective-permute-start | bytes 786440 | tf_op jit(solution)/shard_map/ppermute | solution.py:670
  27.9 8.2 %collective-permute-start.8 = (f32[512,128]{1,0:T(8,128)S(1)}, f32[512,128]{1,0:T(8,128)S(1)}, u32[]{:S(2)}, u32[]{:S(2)}) collective-permute-start(f32[512,128]{1,0:T(8,128)S(1)} %get-tuple-element.42), channel_id=1, source_target_pairs={{64,0},{96,32},{128,64},{160,96},{192,128},{224,160},{256,192},{28... | collective-permute-start | bytes 786440 | tf_op jit(solution)/shard_map/ppermute | solution.py:671
  36.1 16.3 %copy-start = (f32[64,1,8,128]{3,2,1,0:T(8,128)S(1)}, f32[64,1,8,128]{3,2,1,0:T(8,128)}, u32[]{:S(2)}) copy-start(f32[64,1,8,128]{3,2,1,0:T(8,128)} %param.7) | copy-start | bytes 786436
  40.3 12.9 %collective-permute-start.9 = (f32[592,128]{1,0:T(8,128)S(1)}, f32[592,128]{1,0:T(8,128)S(1)}, u32[]{:S(2)}, u32[]{:S(2)}) collective-permute-start(f32[592,128]{1,0:T(8,128)S(1)} %get-tuple-element.48), channel_id=1, source_target_pairs={{0,64},{32,96},{64,128},{96,160},{128,192},{160,224},{192,256},{22... | collective-permute-start | bytes 909320 | tf_op jit(solution)/shard_map/ppermute | solution.py:670
  44.8 8.4 %collective-permute-start.10 = (f32[592,128]{1,0:T(8,128)S(1)}, f32[592,128]{1,0:T(8,128)S(1)}, u32[]{:S(2)}, u32[]{:S(2)}) collective-permute-start(f32[592,128]{1,0:T(8,128)S(1)} %get-tuple-element.49), channel_id=1, source_target_pairs={{64,0},{96,32},{128,64},{160,96},{192,128},{224,160},{256,192},{28... | collective-permute-start | bytes 909320 | tf_op jit(solution)/shard_map/ppermute | solution.py:671
  46.1 6.3 %collective-permute-start.11 = (f32[512,128]{1,0:T(8,128)S(1)}, f32[512,128]{1,0:T(8,128)S(1)}, u32[]{:S(2)}, u32[]{:S(2)}) collective-permute-start(f32[512,128]{1,0:T(8,128)S(1)} %get-tuple-element.51), channel_id=1, source_target_pairs={{0,32},{32,0},{64,96},{96,64},{128,160},{160,128},{192,224},{224,1... | collective-permute-start | bytes 786440 | tf_op jit(solution)/shard_map/ppermute | solution.py:686
  55.6 6.6 %collective-permute-start.12 = (f32[512,128]{1,0:T(8,128)S(1)}, f32[512,128]{1,0:T(8,128)S(1)}, u32[]{:S(2)}, u32[]{:S(2)}) collective-permute-start(f32[512,128]{1,0:T(8,128)S(1)} %get-tuple-element.54), channel_id=1, source_target_pairs={{0,32},{32,0},{64,96},{96,64},{128,160},{160,128},{192,224},{224,1... | collective-permute-start | bytes 786440 | tf_op jit(solution)/shard_map/ppermute | solution.py:686

commit v7 on v6

--- a/solution.py
+++ b/solution.py
@@ -91,7 +91,10 @@
         put(send_ref, HALF + e, tile(keep_ref, HALF + e))
 
 
-def zmsg_kernel(keep_ref, got_ref, main_ref, zmsg_ref):
+EARLY_TILES = SLOT + HALF + 1
+
+
+def zmsg_kernel(keep_ref, got_ref, main_ref, zmsg_ref, to_left_ref, to_right_ref):
     lane = iota_lane()
     mine, other = core() * SLOT, (1 - core()) * SLOT
     for i in range(SLOT):
@@ -108,6 +111,12 @@
         for t in range(TG):
             put(zmsg_ref, TG * p + t, packed([SLOT * p + GROUPS * t + q for q in range(GROUPS)]))
     put(zmsg_ref, NE - 1, packed([SLOT * p + HALF + e for p in range(2) for e in range(NEXTRA)]))
+    for p, (adjacent, second) in enumerate(((to_left_ref, to_right_ref), (to_right_ref, to_left_ref))):
+        for i in range(SLOT):
+            value = tile(main_ref, SLOT * p + i)
+            put(adjacent, i, value)
+            if i < HALF or i == SLOT - 1:
+                put(second, SLOT + min(i, HALF), value)
 
 
 YPAIRS = (2 * SLOT + NE + 1) // 2
@@ -133,7 +142,8 @@
         put(down_ref, g, jnp.where(lower, first, second))
 
 
-A_SECOND = SLOT
+A_EXTRA = HALF // 4 * 3
+A_SECOND = A_EXTRA + NEXTRA
 A_EDGE = A_SECOND + HALF // 2 + 1
 A_TILES = A_EDGE + 2 * NE
 B_MY = HALF
@@ -154,14 +164,26 @@
             if index < 2 * SLOT:
                 put(my_ref, index, pair[half])
                 p, i = divmod(index, SLOT)
-                put((to_left_ref, to_right_ref)[p], i, pair[half])
+                if i >= HALF:
+                    put((to_left_ref, to_right_ref)[p], A_EXTRA + i - HALF, pair[half])
                 if i == SLOT - 1:
                     put((to_right_ref, to_left_ref)[p], A_SECOND + HALF // 2, pair[half])
             elif index < 2 * SLOT + NE:
                 put(ey_ref, index - 2 * SLOT, pair[half])
                 for ref in (to_left_ref, to_right_ref):
                     put(ref, A_EDGE + NE + index - 2 * SLOT, pair[half])
-    for p, second in enumerate((to_right_ref, to_left_ref)):
+    free = (row == 3) | (row == 4)
+    for p, (adjacent, second) in enumerate(((to_left_ref, to_right_ref), (to_right_ref, to_left_ref))):
+        for i in range(HALF // 4):
+            first = SLOT * p + 4 * i
+            fourth = tile(my_ref, first + 3)
+            moved = (
+                roll_row(fourth, 3),
+                jnp.where(row < 4, roll_row(fourth, 1), roll_row(fourth, -1)),
+                roll_row(fourth, -3),
+            )
+            for k in range(3):
+                put(adjacent, 3 * i + k, jnp.where(free, moved[k], tile(my_ref, first + k)))
         for i in range(HALF // 2):
             value = jnp.where(
                 keep_2,
@@ -352,9 +374,16 @@
     extras = {2: (main_ref, HALF, my_ref, HALF, edge_ref, NE - 1, ey_ref, NE - 1, 0)}
     extras[3] = (main_ref, SLOT + HALF, my_ref, SLOT + HALF, edge_ref, NE - 1, ey_ref, NE - 1, NEXTRA)
     for whole, ref, adjacent, second, p in ((left_main_ref, left_ref, 1, 0, 1), (right_main_ref, right_ref, 4, 5, 0)):
-        copy_tiles(whole, SLOT * p, main_0, HALF * adjacent, HALF)
-        copy_tiles(whole, SLOT * (1 - p), main_0, HALF * second, HALF)
-        copy_tiles(ref, 0, my_0, HALF * adjacent, HALF)
+        copy_tiles(whole, 0, main_0, HALF * adjacent, HALF)
+        copy_tiles(whole, SLOT, main_0, HALF * second, HALF)
+        for i in range(HALF // 4):
+            three = [tile(ref, 3 * i + k) for k in range(3)]
+            for k in range(3):
+                put(my_0, HALF * adjacent + 4 * i + k, three[k])
+            fourth = jnp.where(row < 6, roll_row(three[1], 1), roll_row(three[2], 3))
+            fourth = jnp.where(row < 4, roll_row(three[1], -1), fourth)
+            fourth = jnp.where(row < 2, roll_row(three[0], -3), fourth)
+            put(my_0, HALF * adjacent + 4 * i + 3, fourth)
         for i in range(HALF // 2):
             value = tile(ref, A_SECOND + i)
             put(my_0, HALF * second + 2 * i, value)
@@ -363,10 +392,10 @@
             copy_tiles(ref, A_EDGE + TG * at, em_0, TG * plane, TG)
             copy_tiles(ref, A_EDGE + NE + TG * at, ey_0, TG * plane, TG)
         em_at, ey_at = A_EDGE + NE - 1, A_EDGE + 2 * NE - 1
-        extras[adjacent] = (whole, SLOT * p + HALF, ref, HALF, ref, em_at, ref, ey_at, NEXTRA * p)
+        extras[adjacent] = (whole, HALF, ref, A_EXTRA, ref, em_at, ref, ey_at, NEXTRA * p)
         for part, value in enumerate(
             (
-                tile(whole, SLOT * (1 - p) + SLOT - 1),
+                tile(whole, SLOT + HALF),
                 tile(ref, A_SECOND + HALF // 2),
                 roll_lane(tile(ref, em_at), -8 * (NEXTRA * (1 - p) + 4)),
                 roll_lane(tile(ref, ey_at), -8 * (NEXTRA * (1 - p) + 4)),
@@ -718,8 +747,10 @@
     )
     got = other_core(send)
     wells = call(functools.partial(wells_kernel, sizes), "wells", tiles(16), [SMEM, SMEM])(well_cells, well_rate)
-    main, zmsg = call(zmsg_kernel, "zmsg", (tiles(2 * SLOT), tiles(NE)), [VMEM] * 2)(keep, got)
-    left_main, right_main = from_sides("gx", main, main, 2)
+    main, zmsg, to_left, to_right = call(
+        zmsg_kernel, "zmsg", (tiles(2 * SLOT), tiles(NE), tiles(EARLY_TILES), tiles(EARLY_TILES)), [VMEM] * 2
+    )(keep, got)
+    left_main, right_main = from_sides("gx", to_right, to_left, 2)
     low, high = from_sides("gz", zmsg, zmsg)
     up, down, edge = call(ymsg_kernel, "ymsg", (tiles(YPAIRS), tiles(YPAIRS), tiles(NE)), [VMEM] * 3)(
         main, low, high

time: 131 us -> 131 us (level)
  waiting for transfers between devices: 10.3 us -> 12.1 us
    ppermute x5, waiting for transfers between devices: 0.01 us -> 6.73 us  [from_sides(): upper = lax.ppermute(down, axis, [(i + by, i) for i in range(count - by)])]
    ppermute x5, waiting for transfers between devices: 6.97 us -> 2.11 us  [from_sides(): lower = lax.ppermute(up, axis, [(i, i + by) for i in range(count - by)])]
    ppermute x5, starting transfers between devices: 15.7 us -> 13.1 us  [from_sides(): lower = lax.ppermute(up, axis, [(i, i + by) for i in range(count - by)])]
    ppermute x3, starting transfers between devices: 19.4 us -> 20.7 us  [other_core(): return lax.ppermute(values, 'gx', [(i, i ^ 1) for i in range(count)])]
  transfers between devices with their start and end apart: 13 -> 13, of which waited for: 6 -> 9; matrix products, arithmetic and copies ran while one was open for 0% -> 0% of each run, Pallas kernels for 1% -> 1%
where the time goes in v7:
time: 131 us; the launch traced here: 129 us
  blocking collectives  56.2 us (43%)
  starting transfers between devices  40.3 us (31%)
  Pallas kernels  20 us (15%)
  waiting for transfers between devices  12.1 us (9%)
    all_to_all x2, blocking collectives, spread(): lax.all_to_all(jnp.broadcast_to(values, (count, *values.shape)), axes, 0, 0)  33.9 us
    all_to_all x1, blocking collectives, per_device(): gram = lax.all_to_all(gram.reshape(count, -1, 128), plane, 0, 0)  22.2 us
    ppermute x3, starting transfers between devices, other_core(): return lax.ppermute(values, 'gx', [(i, i ^ 1) for i in range(count)])  20.7 us
    ppermute x5, starting transfers between devices, from_sides(): lower = lax.ppermute(up, axis, [(i, i + by) for i in range(count - by)])  13.1 us
    pallas_call x1, Pallas kernels, per_device(): call(final_kernel, 'final', (f32(8 * M, 128), f32(8 * M, 128)), [VMEM] *...  9.53 us
    ppermute x5, waiting for transfers between devices, from_sides(): upper = lax.ppermute(down, axis, [(i + by, i) for i in range(count - by)])  6.73 us
    ppermute x5, starting transfers between devices, from_sides(): upper = lax.ppermute(down, axis, [(i + by, i) for i in range(count - by)])  6.46 us
    pallas_call x1, Pallas kernels, per_device(): call(functools.partial(first_two_kernel, sizes), 'first_two', (tiles(4 *...  4.18 us
  transfers between devices with their start and end apart: 13, of which 9 were waited for; matrix products, arithmetic and copies ran while one was open for 0% of the time, Pallas kernels for 1%

profile of v7, /device:TPU:1, one launch (start us, length us, event | category | flops | bytes accessed | tf_op | source)
XLA Modules:
  0.0 129.5 jit_solution(1481995806523681836)
XLA Ops:
  1.7 8.8 %collective-permute-start = (f32[296,128]{1,0:T(8,128)S(1)}, f32[296,128]{1,0:T(8,128)S(1)}, u32[]{:S(2)}, u32[]{:S(2)}) collective-permute-start(f32[296,128]{1,0:T(8,128)S(1)} %get-tuple-element.35), channel_id=1, source_target_pairs={{0,32},{32,0},{64,96},{96,64},{128,160},{160,128},{192,224},{224,1... | collective-permute-start | bytes 454664 | tf_op jit(solution)/shard_map/ppermute | solution.py:715
  11.7 1.3 collective-permute-start.2
  13.0 4.0 %collective-permute-start.1 = (f32[40,128]{1,0:T(8,128)S(1)}, f32[40,128]{1,0:T(8,128)S(1)}, u32[]{:S(2)}, u32[]{:S(2)}) collective-permute-start(f32[40,128]{1,0:T(8,128)S(1)} %get-tuple-element.37), channel_id=1, source_target_pairs={{0,1},{1,2},{2,3},{4,5},{5,6},{6,7},{8,9},{9,10},{10,11},{12,13},{... | collective-permute-start | bytes 61448 | tf_op jit(solution)/shard_map/ppermute | solution.py:699
  17.9 1.3 %collective-permute-start.3 = (f32[320,128]{1,0:T(8,128)S(1)}, f32[320,128]{1,0:T(8,128)S(1)}, u32[]{:S(2)}, u32[]{:S(2)}) collective-permute-start(f32[320,128]{1,0:T(8,128)S(1)} %get-tuple-element.39), channel_id=1, source_target_pairs={{0,4},{4,8},{8,12},{12,16},{16,20},{20,24},{24,28},{1,5},{5,9},{9,... | collective-permute-start | bytes 491528 | tf_op jit(solution)/shard_map/ppermute | solution.py:699
  19.2 1.3 collective-permute-start.4
  20.5 1.3 %collective-permute-start.5 = (f32[560,128]{1,0:T(8,128)S(1)}, f32[560,128]{1,0:T(8,128)S(1)}, u32[]{:S(2)}, u32[]{:S(2)}) collective-permute-start(f32[560,128]{1,0:T(8,128)S(1)} %get-tuple-element.43), channel_id=1, source_target_pairs={{0,64},{32,96},{64,128},{96,160},{128,192},{160,224},{192,256},{22... | collective-permute-start | bytes 860168 | tf_op jit(solution)/shard_map/ppermute | solution.py:699
  21.8 1.3 collective-permute-start.6
  23.1 2.1 %collective-permute-done.4.above_ref = f32[320,128]{1,0:T(8,128)S(1)} collective-permute-done((f32[320,128]{1,0:T(8,128)S(1)}, f32[320,128]{1,0:T(8,128)S(1)}, u32[]{:S(2)}, u32[]{:S(2)}) %collective-permute-start.4) | collective-permute-done | bytes 163872 | tf_op jit(solution)/shard_map/ppermute | solution.py:700
  25.4 1.9 %collective-permute-start.7 = (f32[448,128]{1,0:T(8,128)S(1)}, f32[448,128]{1,0:T(8,128)S(1)}, u32[]{:S(2)}, u32[]{:S(2)}) collective-permute-start(f32[448,128]{1,0:T(8,128)S(1)} %get-tuple-element.45), channel_id=1, source_target_pairs={{0,64},{32,96},{64,128},{96,160},{128,192},{160,224},{192,256},{22... | collective-permute-start | bytes 688136 | tf_op jit(solution)/shard_map/ppermute | solution.py:699
  27.3 1.3 collective-permute-start.8
  30.4 1.2 collective-permute-done.7.left_ref
  31.6 3.5 %collective-permute-done.8.right_ref = f32[448,128]{1,0:T(8,128)S(1)} collective-permute-done((f32[448,128]{1,0:T(8,128)S(1)}, f32[448,128]{1,0:T(8,128)S(1)}, u32[]{:S(2)}, u32[]{:S(2)}) %collective-permute-start.8) | collective-permute-done | bytes 229408 | tf_op jit(solution)/shard_map/ppermute | solution.py:700
  35.1 4.2 %first_two.1 = (f32[896,128]{1,0:T(8,128)S(1)}, f32[512,128]{1,0:T(8,128)S(1)}, f32[512,128]{1,0:T(8,128)S(1)}, f32[512,128]{1,0:T(8,128)S(1)}, f32[512,128]{1,0...) custom-call(f32[128,128]{1,0:T(8,128)S(1)} %wells.1.wells_ref, ...), custom_call_target="tpu_custom_call" | custom-call | tf_op jit(solution)/shard_map/first_two/pallas_call | solution.py:763
  39.3 4.6 %collective-permute-start.9 = (f32[592,128]{1,0:T(8,128)S(1)}, f32[592,128]{1,0:T(8,128)S(1)}, u32[]{:S(2)}, u32[]{:S(2)}) collective-permute-start(f32[592,128]{1,0:T(8,128)S(1)} %get-tuple-element.52), channel_id=1, source_target_pairs={{0,64},{32,96},{64,128},{96,160},{128,192},{160,224},{192,256},{22... | collective-permute-start | bytes 909320 | tf_op jit(solution)/shard_map/ppermute | solution.py:699
  43.9 1.3 collective-permute-start.10
  45.2 5.4 %collective-permute-start.11 = (f32[512,128]{1,0:T(8,128)S(1)}, f32[512,128]{1,0:T(8,128)S(1)}, u32[]{:S(2)}, u32[]{:S(2)}) collective-permute-start(f32[512,128]{1,0:T(8,128)S(1)} %get-tuple-element.55), channel_id=1, source_target_pairs={{0,32},{32,0},{64,96},{96,64},{128,160},{160,128},{192,224},{224,1... | collective-permute-start | bytes 786440 | tf_op jit(solution)/shard_map/ppermute | solution.py:715
  50.6 1.1 collective-permute-done.11.got_ref
  52.7 2.3 %last_two.1 = (f32[512,128]{1,0:T(8,128)S(1)}, f32[512,128]{1,0:T(8,128)S(1)}) custom-call(f32[896,128]{1,0:T(8,128)S(1)} %get-tuple-element.47.coef_ref, f32[512,128]{1,0:T(8,128)S(1)} %get-tuple-element.48.block_2_ref, f32[512,128]{1,0:T(8,128)S(1)} %get-tuple-element.49.my_2_ref, f32[32,128]{1,0:T(8,128)S(1)} %get-tuple-element.50.em_2_ref, ...), custom_call_target="tpu_custom_call" | custom-call | tf_op jit(solution)/shard_map/last_two/pallas_call | solution.py:793
  55.0 6.5 %collective-permute-start.12 = (f32[512,128]{1,0:T(8,128)S(1)}, f32[512,128]{1,0:T(8,128)S(1)}, u32[]{:S(2)}, u32[]{:S(2)}) collective-permute-start(f32[512,128]{1,0:T(8,128)S(1)} %get-tuple-element.58), channel_id=1, source_target_pairs={{0,32},{32,0},{64,96},{96,64},{128,160},{160,128},{192,224},{224,1... | collective-permute-start | bytes 786440 | tf_op jit(solution)/shard_map/ppermute | solution.py:715
  61.6 1.1 collective-permute-done.12.got_ref
  63.7 22.2 %all_to_all.15 = f32[32,16,128]{2,1,0:T(8,128)S(1)} all-to-all(f32[32,16,128]{2,1,0:T(8,128)S(1)} %bitcast.15), channel_id=1, replica_groups=mesh['gx'=16,'gy'=8,'gz'=4] {'gz','gy'}, dimensions={0} | all-to-all | bytes 524288 | tf_op jit(solution)/shard_map/all_to_all | solution.py:811
  86.0 19.3 %all_to_all.16 = f32[16,16,128]{2,1,0:T(8,128)S(1)} all-to-all(f32[16,16,128]{2,1,0:T(8,128)S(1)} %broadcast_in_dim.6), channel_id=1, replica_groups=mesh['gx'=16,'gy'=8,'gz'=4] {'gx'}, dimensions={0} | all-to-all | bytes 262144 | tf_op jit(solution)/shard_map/all_to_all | solution.py:706
  105.3 14.6 %all_to_all.17 = f32[32,16,128]{2,1,0:T(8,128)S(1)} all-to-all(f32[32,16,128]{2,1,0:T(8,128)S(1)} %broadcast_in_dim.7), channel_id=1, replica_groups=mesh['gx'=16,'gy'=8,'gz'=4] {'gz','gy'}, dimensions={0} | all-to-all | bytes 524288 | tf_op jit(solution)/shard_map/all_to_all | solution.py:706
  120.0 9.5 %final.1 = (f32[512,128]{1,0:T(8,128)}, f32[512,128]{1,0:T(8,128)}) custom-call(f32[512,128]{1,0:T(8,128)S(1)} %bitcast.14, bf16[192,1024]{1,0:T(8,128)(2,1)S(1)} %get-tuple-element.59.early_high, bf16[192,1024]{1,0:T(8,128)(2,1)S(1)} %get-tuple-element.60.early_low, bf16[128,1024]{1,0:T(8,128)(2,1)S(1)} %get-tuple-element.62.high_ref, ...), custom_call_target="tpu_custom_call" | custom-call | tf_op jit(solution)/shard_map/final/pallas_call | solution.py:815
  (25 shorter events, 7.0 us)
Async XLA Ops:
  1.7 9.8 %collective-permute-start = (f32[296,128]{1,0:T(8,128)S(1)}, f32[296,128]{1,0:T(8,128)S(1)}, u32[]{:S(2)}, u32[]{:S(2)}) collective-permute-start(f32[296,128]{1,0:T(8,128)S(1)} %get-tuple-element.35), channel_id=1, source_target_pairs={{0,32},{32,0},{64,96},{96,64},{128,160},{160,128},{192,224},{224,1... | collective-permute-start | bytes 454664 | tf_op jit(solution)/shard_map/ppermute | solution.py:715
  11.7 5.3 %collective-permute-start.2 = (f32[40,128]{1,0:T(8,128)S(1)}, f32[40,128]{1,0:T(8,128)S(1)}, u32[]{:S(2)}, u32[]{:S(2)}) collective-permute-start(f32[40,128]{1,0:T(8,128)S(1)} %get-tuple-element.37), channel_id=1, source_target_pairs={{1,0},{2,1},{3,2},{5,4},{6,5},{7,6},{9,8},{10,9},{11,10},{13,12},{... | collective-permute-start | bytes 61448 | tf_op jit(solution)/shard_map/ppermute | solution.py:700
  13.0 4.9 %collective-permute-start.1 = (f32[40,128]{1,0:T(8,128)S(1)}, f32[40,128]{1,0:T(8,128)S(1)}, u32[]{:S(2)}, u32[]{:S(2)}) collective-permute-start(f32[40,128]{1,0:T(8,128)S(1)} %get-tuple-element.37), channel_id=1, source_target_pairs={{0,1},{1,2},{2,3},{4,5},{5,6},{6,7},{8,9},{9,10},{10,11},{12,13},{... | collective-permute-start | bytes 61448 | tf_op jit(solution)/shard_map/ppermute | solution.py:699
  17.9 5.2 %collective-permute-start.3 = (f32[320,128]{1,0:T(8,128)S(1)}, f32[320,128]{1,0:T(8,128)S(1)}, u32[]{:S(2)}, u32[]{:S(2)}) collective-permute-start(f32[320,128]{1,0:T(8,128)S(1)} %get-tuple-element.39), channel_id=1, source_target_pairs={{0,4},{4,8},{8,12},{12,16},{16,20},{20,24},{24,28},{1,5},{5,9},{9,... | collective-permute-start | bytes 491528 | tf_op jit(solution)/shard_map/ppermute | solution.py:699
  19.2 6.1 %collective-permute-start.4 = (f32[320,128]{1,0:T(8,128)S(1)}, f32[320,128]{1,0:T(8,128)S(1)}, u32[]{:S(2)}, u32[]{:S(2)}) collective-permute-start(f32[320,128]{1,0:T(8,128)S(1)} %get-tuple-element.40), channel_id=1, source_target_pairs={{4,0},{8,4},{12,8},{16,12},{20,16},{24,20},{28,24},{5,1},{9,5},{13... | collective-permute-start | bytes 491528 | tf_op jit(solution)/shard_map/ppermute | solution.py:700
  20.5 8.9 %collective-permute-start.5 = (f32[560,128]{1,0:T(8,128)S(1)}, f32[560,128]{1,0:T(8,128)S(1)}, u32[]{:S(2)}, u32[]{:S(2)}) collective-permute-start(f32[560,128]{1,0:T(8,128)S(1)} %get-tuple-element.43), channel_id=1, source_target_pairs={{0,64},{32,96},{64,128},{96,160},{128,192},{160,224},{192,256},{22... | collective-permute-start | bytes 860168 | tf_op jit(solution)/shard_map/ppermute | solution.py:699
  21.8 8.6 %collective-permute-start.6 = (f32[560,128]{1,0:T(8,128)S(1)}, f32[560,128]{1,0:T(8,128)S(1)}, u32[]{:S(2)}, u32[]{:S(2)}) collective-permute-start(f32[560,128]{1,0:T(8,128)S(1)} %get-tuple-element.44), channel_id=1, source_target_pairs={{64,0},{96,32},{128,64},{160,96},{192,128},{224,160},{256,192},{28... | collective-permute-start | bytes 860168 | tf_op jit(solution)/shard_map/ppermute | solution.py:700
  25.4 3.2 %copy-start.1 = (s32[32]{0:T(128)S(1)}, s32[32]{0:T(128)}, u32[]{:S(2)}) copy-start(s32[32]{0:T(128)} %cells_ref.1) | copy-start | bytes 388
  25.4 3.2 %copy-start.2 = (f32[32]{0:T(128)S(1)}, f32[32]{0:T(128)}, u32[]{:S(2)}) copy-start(f32[32]{0:T(128)} %rate_ref.1) | copy-start | bytes 388
  25.4 6.3 %collective-permute-start.7 = (f32[448,128]{1,0:T(8,128)S(1)}, f32[448,128]{1,0:T(8,128)S(1)}, u32[]{:S(2)}, u32[]{:S(2)}) collective-permute-start(f32[448,128]{1,0:T(8,128)S(1)} %get-tuple-element.45), channel_id=1, source_target_pairs={{0,64},{32,96},{64,128},{96,160},{128,192},{160,224},{192,256},{22... | collective-permute-start | bytes 688136 | tf_op jit(solution)/shard_map/ppermute | solution.py:699
  27.3 7.9 %collective-permute-start.8 = (f32[448,128]{1,0:T(8,128)S(1)}, f32[448,128]{1,0:T(8,128)S(1)}, u32[]{:S(2)}, u32[]{:S(2)}) collective-permute-start(f32[448,128]{1,0:T(8,128)S(1)} %get-tuple-element.46), channel_id=1, source_target_pairs={{64,0},{96,32},{128,64},{160,96},{192,128},{224,160},{256,192},{28... | collective-permute-start | bytes 688136 | tf_op jit(solution)/shard_map/ppermute | solution.py:700
  35.1 16.7 %copy-start = (f32[64,1,8,128]{3,2,1,0:T(8,128)S(1)}, f32[64,1,8,128]{3,2,1,0:T(8,128)}, u32[]{:S(2)}) copy-start(f32[64,1,8,128]{3,2,1,0:T(8,128)} %param.7) | copy-start | bytes 786436
  39.3 13.3 %collective-permute-start.9 = (f32[592,128]{1,0:T(8,128)S(1)}, f32[592,128]{1,0:T(8,128)S(1)}, u32[]{:S(2)}, u32[]{:S(2)}) collective-permute-start(f32[592,128]{1,0:T(8,128)S(1)} %get-tuple-element.52), channel_id=1, source_target_pairs={{0,64},{32,96},{64,128},{96,160},{128,192},{160,224},{192,256},{22... | collective-permute-start | bytes 909320 | tf_op jit(solution)/shard_map/ppermute | solution.py:699
  43.9 8.8 %collective-permute-start.10 = (f32[592,128]{1,0:T(8,128)S(1)}, f32[592,128]{1,0:T(8,128)S(1)}, u32[]{:S(2)}, u32[]{:S(2)}) collective-permute-start(f32[592,128]{1,0:T(8,128)S(1)} %get-tuple-element.53), channel_id=1, source_target_pairs={{64,0},{96,32},{128,64},{160,96},{192,128},{224,160},{256,192},{28... | collective-permute-start | bytes 909320 | tf_op jit(solution)/shard_map/ppermute | solution.py:700
  45.2 6.5 %collective-permute-start.11 = (f32[512,128]{1,0:T(8,128)S(1)}, f32[512,128]{1,0:T(8,128)S(1)}, u32[]{:S(2)}, u32[]{:S(2)}) collective-permute-start(f32[512,128]{1,0:T(8,128)S(1)} %get-tuple-element.55), channel_id=1, source_target_pairs={{0,32},{32,0},{64,96},{96,64},{128,160},{160,128},{192,224},{224,1... | collective-permute-start | bytes 786440 | tf_op jit(solution)/shard_map/ppermute | solution.py:715
  55.0 7.7 %collective-permute-start.12 = (f32[512,128]{1,0:T(8,128)S(1)}, f32[512,128]{1,0:T(8,128)S(1)}, u32[]{:S(2)}, u32[]{:S(2)}) collective-permute-start(f32[512,128]{1,0:T(8,128)S(1)} %get-tuple-element.58), channel_id=1, source_target_pairs={{0,32},{32,0},{64,96},{96,64},{128,160},{160,128},{192,224},{224,1... | collective-permute-start | bytes 786440 | tf_op jit(solution)/shard_map/ppermute | solution.py:715

commit v8 on v7

--- a/solution.py
+++ b/solution.py
@@ -341,8 +341,8 @@
     edge_ref,
     my_ref,
     ey_ref,
+    right_main_ref,
     left_main_ref,
-    right_main_ref,
     left_ref,
     right_ref,
     coef_ref,
@@ -776,7 +776,7 @@
         ),
         [VMEM] * 9,
         scratch(24, 64, 6 * HALF, 6 * HALF, 6 * TG, 6 * TG, 4 * HALF, 4 * HALF, 4 * TG, 4 * TG),
-    )(wells, main, edge, my, ey, left_main, right_main, left, right)
+    )(wells, main, edge, my, ey, right_main, left_main, left, right)
     left, right = from_sides("gx", to_right, to_left, 2)
     got = other_core(send)
 

time: 131 us -> 130 us (level)
  waiting for transfers between devices: 12.1 us -> 9.2 us
  starting transfers between devices: 40.3 us -> 42 us
    ppermute x5, waiting for transfers between devices: 6.73 us -> 0.01 us  [from_sides(): upper = lax.ppermute(down, axis, [(i + by, i) for i in range(count - by)])]
    ppermute x5, waiting for transfers between devices: 2.11 us -> 5.92 us  [from_sides(): lower = lax.ppermute(up, axis, [(i, i + by) for i in range(count - by)])]
    ppermute x5, starting transfers between devices: 13.1 us -> 16.2 us  [from_sides(): lower = lax.ppermute(up, axis, [(i, i + by) for i in range(count - by)])]
    ppermute x3, starting transfers between devices: 20.7 us -> 19.3 us  [other_core(): return lax.ppermute(values, 'gx', [(i, i ^ 1) for i in range(count)])]
  transfers between devices with their start and end apart: 13 -> 13, of which waited for: 9 -> 6; matrix products, arithmetic and copies ran while one was open for 0% -> 0% of each run, Pallas kernels for 1% -> 1%
where the time goes in v8:
time: 130 us; the launch traced here: 129 us
  blocking collectives  56.4 us (43%)
  starting transfers between devices  42 us (32%)
  Pallas kernels  20 us (15%)
  waiting for transfers between devices  9.2 us (7%)
    all_to_all x2, blocking collectives, spread(): lax.all_to_all(jnp.broadcast_to(values, (count, *values.shape)), axes, 0, 0)  34.2 us
    all_to_all x1, blocking collectives, per_device(): gram = lax.all_to_all(gram.reshape(count, -1, 128), plane, 0, 0)  22.2 us
    ppermute x3, starting transfers between devices, other_core(): return lax.ppermute(values, 'gx', [(i, i ^ 1) for i in range(count)])  19.3 us
    ppermute x5, starting transfers between devices, from_sides(): lower = lax.ppermute(up, axis, [(i, i + by) for i in range(count - by)])  16.2 us
    pallas_call x1, Pallas kernels, per_device(): call(final_kernel, 'final', (f32(8 * M, 128), f32(8 * M, 128)), [VMEM] *...  9.53 us
    ppermute x5, starting transfers between devices, from_sides(): upper = lax.ppermute(down, axis, [(i + by, i) for i in range(count - by)])  6.46 us
    ppermute x5, waiting for transfers between devices, from_sides(): lower = lax.ppermute(up, axis, [(i, i + by) for i in range(count - by)])  5.92 us
    pallas_call x1, Pallas kernels, per_device(): call(functools.partial(first_two_kernel, sizes), 'first_two', (tiles(4 *...  4.18 us
  transfers between devices with their start and end apart: 13, of which 6 were waited for; matrix products, arithmetic and copies ran while one was open for 0% of the time, Pallas kernels for 1%

profile of v8, /device:TPU:1, one launch (start us, length us, event | category | flops | bytes accessed | tf_op | source)
XLA Modules:
  0.0 128.5 jit_solution(18078018765814677034)
XLA Ops:
  0.6 1.1 pack.1
  1.7 8.8 %collective-permute-start = (f32[296,128]{1,0:T(8,128)S(1)}, f32[296,128]{1,0:T(8,128)S(1)}, u32[]{:S(2)}, u32[]{:S(2)}) collective-permute-start(f32[296,128]{1,0:T(8,128)S(1)} %get-tuple-element.35), channel_id=1, source_target_pairs={{0,32},{32,0},{64,96},{96,64},{128,160},{160,128},{192,224},{224,1... | collective-permute-start | bytes 454664 | tf_op jit(solution)/shard_map/ppermute | solution.py:715
  10.5 1.0 collective-permute-done.got_ref
  11.7 1.3 %collective-permute-start.2 = (f32[40,128]{1,0:T(8,128)S(1)}, f32[40,128]{1,0:T(8,128)S(1)}, u32[]{:S(2)}, u32[]{:S(2)}) collective-permute-start(f32[40,128]{1,0:T(8,128)S(1)} %get-tuple-element.37), channel_id=1, source_target_pairs={{1,0},{2,1},{3,2},{5,4},{6,5},{7,6},{9,8},{10,9},{11,10},{13,12},{... | collective-permute-start | bytes 61448 | tf_op jit(solution)/shard_map/ppermute | solution.py:700
  13.0 4.0 %collective-permute-start.1 = (f32[40,128]{1,0:T(8,128)S(1)}, f32[40,128]{1,0:T(8,128)S(1)}, u32[]{:S(2)}, u32[]{:S(2)}) collective-permute-start(f32[40,128]{1,0:T(8,128)S(1)} %get-tuple-element.37), channel_id=1, source_target_pairs={{0,1},{1,2},{2,3},{4,5},{5,6},{6,7},{8,9},{9,10},{10,11},{12,13},{... | collective-permute-start | bytes 61448 | tf_op jit(solution)/shard_map/ppermute | solution.py:699
  17.9 1.3 %collective-permute-start.3 = (f32[320,128]{1,0:T(8,128)S(1)}, f32[320,128]{1,0:T(8,128)S(1)}, u32[]{:S(2)}, u32[]{:S(2)}) collective-permute-start(f32[320,128]{1,0:T(8,128)S(1)} %get-tuple-element.39), channel_id=1, source_target_pairs={{0,4},{4,8},{8,12},{12,16},{16,20},{20,24},{24,28},{1,5},{5,9},{9,... | collective-permute-start | bytes 491528 | tf_op jit(solution)/shard_map/ppermute | solution.py:699
  19.2 1.3 %collective-permute-start.4 = (f32[320,128]{1,0:T(8,128)S(1)}, f32[320,128]{1,0:T(8,128)S(1)}, u32[]{:S(2)}, u32[]{:S(2)}) collective-permute-start(f32[320,128]{1,0:T(8,128)S(1)} %get-tuple-element.40), channel_id=1, source_target_pairs={{4,0},{8,4},{12,8},{16,12},{20,16},{24,20},{28,24},{5,1},{9,5},{13... | collective-permute-start | bytes 491528 | tf_op jit(solution)/shard_map/ppermute | solution.py:700
  20.5 1.3 %collective-permute-start.5 = (f32[560,128]{1,0:T(8,128)S(1)}, f32[560,128]{1,0:T(8,128)S(1)}, u32[]{:S(2)}, u32[]{:S(2)}) collective-permute-start(f32[560,128]{1,0:T(8,128)S(1)} %get-tuple-element.43), channel_id=1, source_target_pairs={{64,0},{96,32},{128,64},{160,96},{192,128},{224,160},{256,192},{28... | collective-permute-start | bytes 860168 | tf_op jit(solution)/shard_map/ppermute | solution.py:700
  21.8 4.0 %collective-permute-start.6 = (f32[560,128]{1,0:T(8,128)S(1)}, f32[560,128]{1,0:T(8,128)S(1)}, u32[]{:S(2)}, u32[]{:S(2)}) collective-permute-start(f32[560,128]{1,0:T(8,128)S(1)} %get-tuple-element.44), channel_id=1, source_target_pairs={{0,64},{32,96},{64,128},{96,160},{128,192},{160,224},{192,256},{22... | collective-permute-start | bytes 860168 | tf_op jit(solution)/shard_map/ppermute | solution.py:699
  25.9 1.9 %collective-permute-start.7 = (f32[448,128]{1,0:T(8,128)S(1)}, f32[448,128]{1,0:T(8,128)S(1)}, u32[]{:S(2)}, u32[]{:S(2)}) collective-permute-start(f32[448,128]{1,0:T(8,128)S(1)} %get-tuple-element.45), channel_id=1, source_target_pairs={{0,64},{32,96},{64,128},{96,160},{128,192},{160,224},{192,256},{22... | collective-permute-start | bytes 688136 | tf_op jit(solution)/shard_map/ppermute | solution.py:699
  27.9 1.3 %collective-permute-start.8 = (f32[448,128]{1,0:T(8,128)S(1)}, f32[448,128]{1,0:T(8,128)S(1)}, u32[]{:S(2)}, u32[]{:S(2)}) collective-permute-start(f32[448,128]{1,0:T(8,128)S(1)} %get-tuple-element.46), channel_id=1, source_target_pairs={{64,0},{96,32},{128,64},{160,96},{192,128},{224,160},{256,192},{28... | collective-permute-start | bytes 688136 | tf_op jit(solution)/shard_map/ppermute | solution.py:700
  30.1 4.9 %collective-permute-done.7.left_ref = f32[448,128]{1,0:T(8,128)S(1)} collective-permute-done((f32[448,128]{1,0:T(8,128)S(1)}, f32[448,128]{1,0:T(8,128)S(1)}, u32[]{:S(2)}, u32[]{:S(2)}) %collective-permute-start.7) | collective-permute-done | bytes 229408 | tf_op jit(solution)/shard_map/ppermute | solution.py:699
  35.1 4.2 %first_two.1 = (f32[896,128]{1,0:T(8,128)S(1)}, f32[512,128]{1,0:T(8,128)S(1)}, f32[512,128]{1,0:T(8,128)S(1)}, f32[512,128]{1,0:T(8,128)S(1)}, f32[512,128]{1,0...) custom-call(f32[128,128]{1,0:T(8,128)S(1)} %wells.1.wells_ref, ...), custom_call_target="tpu_custom_call" | custom-call | tf_op jit(solution)/shard_map/first_two/pallas_call | solution.py:763
  39.2 5.0 %collective-permute-start.9 = (f32[592,128]{1,0:T(8,128)S(1)}, f32[592,128]{1,0:T(8,128)S(1)}, u32[]{:S(2)}, u32[]{:S(2)}) collective-permute-start(f32[592,128]{1,0:T(8,128)S(1)} %get-tuple-element.52), channel_id=1, source_target_pairs={{0,64},{32,96},{64,128},{96,160},{128,192},{160,224},{192,256},{22... | collective-permute-start | bytes 909320 | tf_op jit(solution)/shard_map/ppermute | solution.py:699
  44.2 1.3 %collective-permute-start.10 = (f32[592,128]{1,0:T(8,128)S(1)}, f32[592,128]{1,0:T(8,128)S(1)}, u32[]{:S(2)}, u32[]{:S(2)}) collective-permute-start(f32[592,128]{1,0:T(8,128)S(1)} %get-tuple-element.53), channel_id=1, source_target_pairs={{64,0},{96,32},{128,64},{160,96},{192,128},{224,160},{256,192},{28... | collective-permute-start | bytes 909320 | tf_op jit(solution)/shard_map/ppermute | solution.py:700
  45.5 5.1 %collective-permute-start.11 = (f32[512,128]{1,0:T(8,128)S(1)}, f32[512,128]{1,0:T(8,128)S(1)}, u32[]{:S(2)}, u32[]{:S(2)}) collective-permute-start(f32[512,128]{1,0:T(8,128)S(1)} %get-tuple-element.55), channel_id=1, source_target_pairs={{0,32},{32,0},{64,96},{96,64},{128,160},{160,128},{192,224},{224,1... | collective-permute-start | bytes 786440 | tf_op jit(solution)/shard_map/ppermute | solution.py:715
  50.6 1.1 collective-permute-done.11.got_ref
  52.6 2.3 %last_two.1 = (f32[512,128]{1,0:T(8,128)S(1)}, f32[512,128]{1,0:T(8,128)S(1)}) custom-call(f32[896,128]{1,0:T(8,128)S(1)} %get-tuple-element.47.coef_ref, f32[512,128]{1,0:T(8,128)S(1)} %get-tuple-element.48.block_2_ref, f32[512,128]{1,0:T(8,128)S(1)} %get-tuple-element.49.my_2_ref, f32[32,128]{1,0:T(8,128)S(1)} %get-tuple-element.50.em_2_ref, ...), custom_call_target="tpu_custom_call" | custom-call | tf_op jit(solution)/shard_map/last_two/pallas_call | solution.py:793
  55.0 5.4 %collective-permute-start.12 = (f32[512,128]{1,0:T(8,128)S(1)}, f32[512,128]{1,0:T(8,128)S(1)}, u32[]{:S(2)}, u32[]{:S(2)}) collective-permute-start(f32[512,128]{1,0:T(8,128)S(1)} %get-tuple-element.58), channel_id=1, source_target_pairs={{0,32},{32,0},{64,96},{96,64},{128,160},{160,128},{192,224},{224,1... | collective-permute-start | bytes 786440 | tf_op jit(solution)/shard_map/ppermute | solution.py:715
  60.4 1.1 collective-permute-done.12.got_ref
  62.5 22.2 %all_to_all.15 = f32[32,16,128]{2,1,0:T(8,128)S(1)} all-to-all(f32[32,16,128]{2,1,0:T(8,128)S(1)} %bitcast.15), channel_id=1, replica_groups=mesh['gx'=16,'gy'=8,'gz'=4] {'gz','gy'}, dimensions={0} | all-to-all | bytes 524288 | tf_op jit(solution)/shard_map/all_to_all | solution.py:811
  84.8 19.5 %all_to_all.16 = f32[16,16,128]{2,1,0:T(8,128)S(1)} all-to-all(f32[16,16,128]{2,1,0:T(8,128)S(1)} %broadcast_in_dim.6), channel_id=1, replica_groups=mesh['gx'=16,'gy'=8,'gz'=4] {'gx'}, dimensions={0} | all-to-all | bytes 262144 | tf_op jit(solution)/shard_map/all_to_all | solution.py:706
  104.3 14.6 %all_to_all.17 = f32[32,16,128]{2,1,0:T(8,128)S(1)} all-to-all(f32[32,16,128]{2,1,0:T(8,128)S(1)} %broadcast_in_dim.7), channel_id=1, replica_groups=mesh['gx'=16,'gy'=8,'gz'=4] {'gz','gy'}, dimensions={0} | all-to-all | bytes 524288 | tf_op jit(solution)/shard_map/all_to_all | solution.py:706
  119.0 9.5 %final.1 = (f32[512,128]{1,0:T(8,128)}, f32[512,128]{1,0:T(8,128)}) custom-call(f32[512,128]{1,0:T(8,128)S(1)} %bitcast.14, bf16[192,1024]{1,0:T(8,128)(2,1)S(1)} %get-tuple-element.59.early_high, bf16[192,1024]{1,0:T(8,128)(2,1)S(1)} %get-tuple-element.60.early_low, bf16[128,1024]{1,0:T(8,128)(2,1)S(1)} %get-tuple-element.62.high_ref, ...), custom_call_target="tpu_custom_call" | custom-call | tf_op jit(solution)/shard_map/final/pallas_call | solution.py:815
  (25 shorter events, 3.9 us)
Async XLA Ops:
  1.7 9.8 %collective-permute-start = (f32[296,128]{1,0:T(8,128)S(1)}, f32[296,128]{1,0:T(8,128)S(1)}, u32[]{:S(2)}, u32[]{:S(2)}) collective-permute-start(f32[296,128]{1,0:T(8,128)S(1)} %get-tuple-element.35), channel_id=1, source_target_pairs={{0,32},{32,0},{64,96},{96,64},{128,160},{160,128},{192,224},{224,1... | collective-permute-start | bytes 454664 | tf_op jit(solution)/shard_map/ppermute | solution.py:715
  11.7 5.3 %collective-permute-start.2 = (f32[40,128]{1,0:T(8,128)S(1)}, f32[40,128]{1,0:T(8,128)S(1)}, u32[]{:S(2)}, u32[]{:S(2)}) collective-permute-start(f32[40,128]{1,0:T(8,128)S(1)} %get-tuple-element.37), channel_id=1, source_target_pairs={{1,0},{2,1},{3,2},{5,4},{6,5},{7,6},{9,8},{10,9},{11,10},{13,12},{... | collective-permute-start | bytes 61448 | tf_op jit(solution)/shard_map/ppermute | solution.py:700
  13.0 4.9 %collective-permute-start.1 = (f32[40,128]{1,0:T(8,128)S(1)}, f32[40,128]{1,0:T(8,128)S(1)}, u32[]{:S(2)}, u32[]{:S(2)}) collective-permute-start(f32[40,128]{1,0:T(8,128)S(1)} %get-tuple-element.37), channel_id=1, source_target_pairs={{0,1},{1,2},{2,3},{4,5},{5,6},{6,7},{8,9},{9,10},{10,11},{12,13},{... | collective-permute-start | bytes 61448 | tf_op jit(solution)/shard_map/ppermute | solution.py:699
  17.9 7.9 %collective-permute-start.3 = (f32[320,128]{1,0:T(8,128)S(1)}, f32[320,128]{1,0:T(8,128)S(1)}, u32[]{:S(2)}, u32[]{:S(2)}) collective-permute-start(f32[320,128]{1,0:T(8,128)S(1)} %get-tuple-element.39), channel_id=1, source_target_pairs={{0,4},{4,8},{8,12},{12,16},{16,20},{20,24},{24,28},{1,5},{5,9},{9,... | collective-permute-start | bytes 491528 | tf_op jit(solution)/shard_map/ppermute | solution.py:699
  19.2 6.6 %collective-permute-start.4 = (f32[320,128]{1,0:T(8,128)S(1)}, f32[320,128]{1,0:T(8,128)S(1)}, u32[]{:S(2)}, u32[]{:S(2)}) collective-permute-start(f32[320,128]{1,0:T(8,128)S(1)} %get-tuple-element.40), channel_id=1, source_target_pairs={{4,0},{8,4},{12,8},{16,12},{20,16},{24,20},{28,24},{5,1},{9,5},{13... | collective-permute-start | bytes 491528 | tf_op jit(solution)/shard_map/ppermute | solution.py:700
  20.5 9.5 %collective-permute-start.5 = (f32[560,128]{1,0:T(8,128)S(1)}, f32[560,128]{1,0:T(8,128)S(1)}, u32[]{:S(2)}, u32[]{:S(2)}) collective-permute-start(f32[560,128]{1,0:T(8,128)S(1)} %get-tuple-element.43), channel_id=1, source_target_pairs={{64,0},{96,32},{128,64},{160,96},{192,128},{224,160},{256,192},{28... | collective-permute-start | bytes 860168 | tf_op jit(solution)/shard_map/ppermute | solution.py:700
  21.8 8.3 %collective-permute-start.6 = (f32[560,128]{1,0:T(8,128)S(1)}, f32[560,128]{1,0:T(8,128)S(1)}, u32[]{:S(2)}, u32[]{:S(2)}) collective-permute-start(f32[560,128]{1,0:T(8,128)S(1)} %get-tuple-element.44), channel_id=1, source_target_pairs={{0,64},{32,96},{64,128},{96,160},{128,192},{160,224},{192,256},{22... | collective-permute-start | bytes 860168 | tf_op jit(solution)/shard_map/ppermute | solution.py:699
  25.9 3.3 %copy-start.1 = (s32[32]{0:T(128)S(1)}, s32[32]{0:T(128)}, u32[]{:S(2)}) copy-start(s32[32]{0:T(128)} %cells_ref.1) | copy-start | bytes 388
  25.9 3.2 %copy-start.2 = (f32[32]{0:T(128)S(1)}, f32[32]{0:T(128)}, u32[]{:S(2)}) copy-start(f32[32]{0:T(128)} %rate_ref.1) | copy-start | bytes 388
  25.9 9.1 %collective-permute-start.7 = (f32[448,128]{1,0:T(8,128)S(1)}, f32[448,128]{1,0:T(8,128)S(1)}, u32[]{:S(2)}, u32[]{:S(2)}) collective-permute-start(f32[448,128]{1,0:T(8,128)S(1)} %get-tuple-element.45), channel_id=1, source_target_pairs={{0,64},{32,96},{64,128},{96,160},{128,192},{160,224},{192,256},{22... | collective-permute-start | bytes 688136 | tf_op jit(solution)/shard_map/ppermute | solution.py:699
  27.9 7.2 %collective-permute-start.8 = (f32[448,128]{1,0:T(8,128)S(1)}, f32[448,128]{1,0:T(8,128)S(1)}, u32[]{:S(2)}, u32[]{:S(2)}) collective-permute-start(f32[448,128]{1,0:T(8,128)S(1)} %get-tuple-element.46), channel_id=1, source_target_pairs={{64,0},{96,32},{128,64},{160,96},{192,128},{224,160},{256,192},{28... | collective-permute-start | bytes 688136 | tf_op jit(solution)/shard_map/ppermute | solution.py:700
  35.1 16.7 %copy-start = (f32[64,1,8,128]{3,2,1,0:T(8,128)S(1)}, f32[64,1,8,128]{3,2,1,0:T(8,128)}, u32[]{:S(2)}) copy-start(f32[64,1,8,128]{3,2,1,0:T(8,128)} %param.7) | copy-start | bytes 786436
  39.2 13.3 %collective-permute-start.9 = (f32[592,128]{1,0:T(8,128)S(1)}, f32[592,128]{1,0:T(8,128)S(1)}, u32[]{:S(2)}, u32[]{:S(2)}) collective-permute-start(f32[592,128]{1,0:T(8,128)S(1)} %get-tuple-element.52), channel_id=1, source_target_pairs={{0,64},{32,96},{64,128},{96,160},{128,192},{160,224},{192,256},{22... | collective-permute-start | bytes 909320 | tf_op jit(solution)/shard_map/ppermute | solution.py:699
  44.2 8.4 %collective-permute-start.10 = (f32[592,128]{1,0:T(8,128)S(1)}, f32[592,128]{1,0:T(8,128)S(1)}, u32[]{:S(2)}, u32[]{:S(2)}) collective-permute-start(f32[592,128]{1,0:T(8,128)S(1)} %get-tuple-element.53), channel_id=1, source_target_pairs={{64,0},{96,32},{128,64},{160,96},{192,128},{224,160},{256,192},{28... | collective-permute-start | bytes 909320 | tf_op jit(solution)/shard_map/ppermute | solution.py:700
  45.5 6.2 %collective-permute-start.11 = (f32[512,128]{1,0:T(8,128)S(1)}, f32[512,128]{1,0:T(8,128)S(1)}, u32[]{:S(2)}, u32[]{:S(2)}) collective-permute-start(f32[512,128]{1,0:T(8,128)S(1)} %get-tuple-element.55), channel_id=1, source_target_pairs={{0,32},{32,0},{64,96},{96,64},{128,160},{160,128},{192,224},{224,1... | collective-permute-start | bytes 786440 | tf_op jit(solution)/shard_map/ppermute | solution.py:715
  55.0 6.6 %collective-permute-start.12 = (f32[512,128]{1,0:T(8,128)S(1)}, f32[512,128]{1,0:T(8,128)S(1)}, u32[]{:S(2)}, u32[]{:S(2)}) collective-permute-start(f32[512,128]{1,0:T(8,128)S(1)} %get-tuple-element.58), channel_id=1, source_target_pairs={{0,32},{32,0},{64,96},{96,64},{128,160},{160,128},{192,224},{224,1... | collective-permute-start | bytes 786440 | tf_op jit(solution)/shard_map/ppermute | solution.py:715

commit v9 on v8

--- a/solution.py
+++ b/solution.py
@@ -343,8 +343,8 @@
     ey_ref,
     right_main_ref,
     left_main_ref,
+    right_ref,
     left_ref,
-    right_ref,
     coef_ref,
     keep_ref,
     send_ref,
@@ -776,7 +776,7 @@
         ),
         [VMEM] * 9,
         scratch(24, 64, 6 * HALF, 6 * HALF, 6 * TG, 6 * TG, 4 * HALF, 4 * HALF, 4 * TG, 4 * TG),
-    )(wells, main, edge, my, ey, right_main, left_main, left, right)
+    )(wells, main, edge, my, ey, right_main, left_main, right, left)
     left, right = from_sides("gx", to_right, to_left, 2)
     got = other_core(send)
 

time: 130 us -> 131 us (level)
  blocking collectives: 56.4 us -> 58.4 us
  waiting for transfers between devices: 9.2 us -> 7.25 us
    ppermute x5, waiting for transfers between devices: 5.92 us -> 1.79 us  [from_sides(): lower = lax.ppermute(up, axis, [(i, i + by) for i in range(count - by)])]
    all_to_all x2, blocking collectives: 34.2 us -> 37.6 us  [spread(): lax.all_to_all(jnp.broadcast_to(values, (count, *values.shape)), axes, 0, 0)]
    ppermute x5, waiting for transfers between devices: 0.01 us -> 2.19 us  [from_sides(): upper = lax.ppermute(down, axis, [(i + by, i) for i in range(count - by)])]
    all_to_all x1, blocking collectives: 22.2 us -> 20.8 us  [per_device(): gram = lax.all_to_all(gram.reshape(count, -1, 128), plane, 0, 0)]
where the time goes in v9:
time: 131 us; the launch traced here: 129 us
  blocking collectives  58.4 us (45%)
  starting transfers between devices  42.8 us (33%)
  Pallas kernels  20 us (15%)
  waiting for transfers between devices  7.25 us (6%)
    all_to_all x2, blocking collectives, spread(): lax.all_to_all(jnp.broadcast_to(values, (count, *values.shape)), axes, 0, 0)  37.6 us
    all_to_all x1, blocking collectives, per_device(): gram = lax.all_to_all(gram.reshape(count, -1, 128), plane, 0, 0)  20.8 us
    ppermute x3, starting transfers between devices, other_core(): return lax.ppermute(values, 'gx', [(i, i ^ 1) for i in range(count)])  19 us
    ppermute x5, starting transfers between devices, from_sides(): lower = lax.ppermute(up, axis, [(i, i + by) for i in range(count - by)])  17.4 us
    pallas_call x1, Pallas kernels, per_device(): call(final_kernel, 'final', (f32(8 * M, 128), f32(8 * M, 128)), [VMEM] *...  9.53 us
    ppermute x5, starting transfers between devices, from_sides(): upper = lax.ppermute(down, axis, [(i + by, i) for i in range(count - by)])  6.46 us
    pallas_call x1, Pallas kernels, per_device(): call(functools.partial(first_two_kernel, sizes), 'first_two', (tiles(4 *...  4.18 us
    ppermute x3, waiting for transfers between devices, other_core(): return lax.ppermute(values, 'gx', [(i, i ^ 1) for i in range(count)])  3.27 us
  transfers between devices with their start and end apart: 13, of which 6 were waited for; matrix products, arithmetic and copies ran while one was open for 0% of the time, Pallas kernels for 1%

profile of v9, /device:TPU:1, one launch (start us, length us, event | category | flops | bytes accessed | tf_op | source)
XLA Modules:
  0.0 129.5 jit_solution(3346271984247936543)
XLA Ops:
  0.6 1.1 pack.1
  1.7 8.8 %collective-permute-start = (f32[296,128]{1,0:T(8,128)S(1)}, f32[296,128]{1,0:T(8,128)S(1)}, u32[]{:S(2)}, u32[]{:S(2)}) collective-permute-start(f32[296,128]{1,0:T(8,128)S(1)} %get-tuple-element.35), channel_id=1, source_target_pairs={{0,32},{32,0},{64,96},{96,64},{128,160},{160,128},{192,224},{224,1... | collective-permute-start | bytes 454664 | tf_op jit(solution)/shard_map/ppermute | solution.py:715
  10.5 1.0 collective-permute-done.got_ref
  11.7 1.3 collective-permute-start.2
  13.0 4.0 %collective-permute-start.1 = (f32[40,128]{1,0:T(8,128)S(1)}, f32[40,128]{1,0:T(8,128)S(1)}, u32[]{:S(2)}, u32[]{:S(2)}) collective-permute-start(f32[40,128]{1,0:T(8,128)S(1)} %get-tuple-element.37), channel_id=1, source_target_pairs={{0,1},{1,2},{2,3},{4,5},{5,6},{6,7},{8,9},{9,10},{10,11},{12,13},{... | collective-permute-start | bytes 61448 | tf_op jit(solution)/shard_map/ppermute | solution.py:699
  17.9 1.3 %collective-permute-start.3 = (f32[320,128]{1,0:T(8,128)S(1)}, f32[320,128]{1,0:T(8,128)S(1)}, u32[]{:S(2)}, u32[]{:S(2)}) collective-permute-start(f32[320,128]{1,0:T(8,128)S(1)} %get-tuple-element.39), channel_id=1, source_target_pairs={{0,4},{4,8},{8,12},{12,16},{16,20},{20,24},{24,28},{1,5},{5,9},{9,... | collective-permute-start | bytes 491528 | tf_op jit(solution)/shard_map/ppermute | solution.py:699
  19.2 1.3 collective-permute-start.4
  20.5 1.3 collective-permute-start.5
  21.8 4.0 %collective-permute-start.6 = (f32[560,128]{1,0:T(8,128)S(1)}, f32[560,128]{1,0:T(8,128)S(1)}, u32[]{:S(2)}, u32[]{:S(2)}) collective-permute-start(f32[560,128]{1,0:T(8,128)S(1)} %get-tuple-element.44), channel_id=1, source_target_pairs={{0,64},{32,96},{64,128},{96,160},{128,192},{160,224},{192,256},{22... | collective-permute-start | bytes 860168 | tf_op jit(solution)/shard_map/ppermute | solution.py:699
  25.9 1.3 collective-permute-start.7
  27.2 4.0 %collective-permute-start.8 = (f32[448,128]{1,0:T(8,128)S(1)}, f32[448,128]{1,0:T(8,128)S(1)}, u32[]{:S(2)}, u32[]{:S(2)}) collective-permute-start(f32[448,128]{1,0:T(8,128)S(1)} %get-tuple-element.46), channel_id=1, source_target_pairs={{0,64},{32,96},{64,128},{96,160},{128,192},{160,224},{192,256},{22... | collective-permute-start | bytes 688136 | tf_op jit(solution)/shard_map/ppermute | solution.py:699
  32.1 2.2 %collective-permute-done.7.right_ref = f32[448,128]{1,0:T(8,128)S(1)} collective-permute-done((f32[448,128]{1,0:T(8,128)S(1)}, f32[448,128]{1,0:T(8,128)S(1)}, u32[]{:S(2)}, u32[]{:S(2)}) %collective-permute-start.7) | collective-permute-done | bytes 229408 | tf_op jit(solution)/shard_map/ppermute | solution.py:700
  35.2 4.2 %first_two.1 = (f32[896,128]{1,0:T(8,128)S(1)}, f32[512,128]{1,0:T(8,128)S(1)}, f32[512,128]{1,0:T(8,128)S(1)}, f32[512,128]{1,0:T(8,128)S(1)}, f32[512,128]{1,0...) custom-call(f32[128,128]{1,0:T(8,128)S(1)} %wells.1.wells_ref, ...), custom_call_target="tpu_custom_call" | custom-call | tf_op jit(solution)/shard_map/first_two/pallas_call | solution.py:763
  39.4 4.1 %collective-permute-start.9 = (f32[592,128]{1,0:T(8,128)S(1)}, f32[592,128]{1,0:T(8,128)S(1)}, u32[]{:S(2)}, u32[]{:S(2)}) collective-permute-start(f32[592,128]{1,0:T(8,128)S(1)} %get-tuple-element.52), channel_id=1, source_target_pairs={{0,64},{32,96},{64,128},{96,160},{128,192},{160,224},{192,256},{22... | collective-permute-start | bytes 909320 | tf_op jit(solution)/shard_map/ppermute | solution.py:699
  43.5 1.3 collective-permute-start.10
  44.8 4.8 %collective-permute-start.11 = (f32[512,128]{1,0:T(8,128)S(1)}, f32[512,128]{1,0:T(8,128)S(1)}, u32[]{:S(2)}, u32[]{:S(2)}) collective-permute-start(f32[512,128]{1,0:T(8,128)S(1)} %get-tuple-element.55), channel_id=1, source_target_pairs={{0,32},{32,0},{64,96},{96,64},{128,160},{160,128},{192,224},{224,1... | collective-permute-start | bytes 786440 | tf_op jit(solution)/shard_map/ppermute | solution.py:715
  49.6 1.1 collective-permute-done.11.got_ref
  51.5 2.3 %last_two.1 = (f32[512,128]{1,0:T(8,128)S(1)}, f32[512,128]{1,0:T(8,128)S(1)}) custom-call(f32[896,128]{1,0:T(8,128)S(1)} %get-tuple-element.47.coef_ref, f32[512,128]{1,0:T(8,128)S(1)} %get-tuple-element.48.block_2_ref, f32[512,128]{1,0:T(8,128)S(1)} %get-tuple-element.49.my_2_ref, f32[32,128]{1,0:T(8,128)S(1)} %get-tuple-element.50.em_2_ref, ...), custom_call_target="tpu_custom_call" | custom-call | tf_op jit(solution)/shard_map/last_two/pallas_call | solution.py:793
  53.9 5.4 %collective-permute-start.12 = (f32[512,128]{1,0:T(8,128)S(1)}, f32[512,128]{1,0:T(8,128)S(1)}, u32[]{:S(2)}, u32[]{:S(2)}) collective-permute-start(f32[512,128]{1,0:T(8,128)S(1)} %get-tuple-element.58), channel_id=1, source_target_pairs={{0,32},{32,0},{64,96},{96,64},{128,160},{160,128},{192,224},{224,1... | collective-permute-start | bytes 786440 | tf_op jit(solution)/shard_map/ppermute | solution.py:715
  59.3 1.1 collective-permute-done.12.got_ref
  61.4 20.8 %all_to_all.15 = f32[32,16,128]{2,1,0:T(8,128)S(1)} all-to-all(f32[32,16,128]{2,1,0:T(8,128)S(1)} %bitcast.15), channel_id=1, replica_groups=mesh['gx'=16,'gy'=8,'gz'=4] {'gz','gy'}, dimensions={0} | all-to-all | bytes 524288 | tf_op jit(solution)/shard_map/all_to_all | solution.py:811
  82.3 23.0 %all_to_all.16 = f32[16,16,128]{2,1,0:T(8,128)S(1)} all-to-all(f32[16,16,128]{2,1,0:T(8,128)S(1)} %broadcast_in_dim.6), channel_id=1, replica_groups=mesh['gx'=16,'gy'=8,'gz'=4] {'gx'}, dimensions={0} | all-to-all | bytes 262144 | tf_op jit(solution)/shard_map/all_to_all | solution.py:706
  105.3 14.6 %all_to_all.17 = f32[32,16,128]{2,1,0:T(8,128)S(1)} all-to-all(f32[32,16,128]{2,1,0:T(8,128)S(1)} %broadcast_in_dim.7), channel_id=1, replica_groups=mesh['gx'=16,'gy'=8,'gz'=4] {'gz','gy'}, dimensions={0} | all-to-all | bytes 524288 | tf_op jit(solution)/shard_map/all_to_all | solution.py:706
  120.0 9.5 %final.1 = (f32[512,128]{1,0:T(8,128)}, f32[512,128]{1,0:T(8,128)}) custom-call(f32[512,128]{1,0:T(8,128)S(1)} %bitcast.14, bf16[192,1024]{1,0:T(8,128)(2,1)S(1)} %get-tuple-element.59.early_high, bf16[192,1024]{1,0:T(8,128)(2,1)S(1)} %get-tuple-element.60.early_low, bf16[128,1024]{1,0:T(8,128)(2,1)S(1)} %get-tuple-element.62.high_ref, ...), custom_call_target="tpu_custom_call" | custom-call | tf_op jit(solution)/shard_map/final/pallas_call | solution.py:815
  (25 shorter events, 4.7 us)
Async XLA Ops:
  1.7 9.8 %collective-permute-start = (f32[296,128]{1,0:T(8,128)S(1)}, f32[296,128]{1,0:T(8,128)S(1)}, u32[]{:S(2)}, u32[]{:S(2)}) collective-permute-start(f32[296,128]{1,0:T(8,128)S(1)} %get-tuple-element.35), channel_id=1, source_target_pairs={{0,32},{32,0},{64,96},{96,64},{128,160},{160,128},{192,224},{224,1... | collective-permute-start | bytes 454664 | tf_op jit(solution)/shard_map/ppermute | solution.py:715
  11.7 5.3 %collective-permute-start.2 = (f32[40,128]{1,0:T(8,128)S(1)}, f32[40,128]{1,0:T(8,128)S(1)}, u32[]{:S(2)}, u32[]{:S(2)}) collective-permute-start(f32[40,128]{1,0:T(8,128)S(1)} %get-tuple-element.37), channel_id=1, source_target_pairs={{1,0},{2,1},{3,2},{5,4},{6,5},{7,6},{9,8},{10,9},{11,10},{13,12},{... | collective-permute-start | bytes 61448 | tf_op jit(solution)/shard_map/ppermute | solution.py:700
  13.0 4.9 %collective-permute-start.1 = (f32[40,128]{1,0:T(8,128)S(1)}, f32[40,128]{1,0:T(8,128)S(1)}, u32[]{:S(2)}, u32[]{:S(2)}) collective-permute-start(f32[40,128]{1,0:T(8,128)S(1)} %get-tuple-element.37), channel_id=1, source_target_pairs={{0,1},{1,2},{2,3},{4,5},{5,6},{6,7},{8,9},{9,10},{10,11},{12,13},{... | collective-permute-start | bytes 61448 | tf_op jit(solution)/shard_map/ppermute | solution.py:699
  17.9 7.9 %collective-permute-start.3 = (f32[320,128]{1,0:T(8,128)S(1)}, f32[320,128]{1,0:T(8,128)S(1)}, u32[]{:S(2)}, u32[]{:S(2)}) collective-permute-start(f32[320,128]{1,0:T(8,128)S(1)} %get-tuple-element.39), channel_id=1, source_target_pairs={{0,4},{4,8},{8,12},{12,16},{16,20},{20,24},{24,28},{1,5},{5,9},{9,... | collective-permute-start | bytes 491528 | tf_op jit(solution)/shard_map/ppermute | solution.py:699
  19.2 6.6 %collective-permute-start.4 = (f32[320,128]{1,0:T(8,128)S(1)}, f32[320,128]{1,0:T(8,128)S(1)}, u32[]{:S(2)}, u32[]{:S(2)}) collective-permute-start(f32[320,128]{1,0:T(8,128)S(1)} %get-tuple-element.40), channel_id=1, source_target_pairs={{4,0},{8,4},{12,8},{16,12},{20,16},{24,20},{28,24},{5,1},{9,5},{13... | collective-permute-start | bytes 491528 | tf_op jit(solution)/shard_map/ppermute | solution.py:700
  20.5 11.6 %collective-permute-start.5 = (f32[560,128]{1,0:T(8,128)S(1)}, f32[560,128]{1,0:T(8,128)S(1)}, u32[]{:S(2)}, u32[]{:S(2)}) collective-permute-start(f32[560,128]{1,0:T(8,128)S(1)} %get-tuple-element.43), channel_id=1, source_target_pairs={{64,0},{96,32},{128,64},{160,96},{192,128},{224,160},{256,192},{28... | collective-permute-start | bytes 860168 | tf_op jit(solution)/shard_map/ppermute | solution.py:700
  21.8 10.3 %collective-permute-start.6 = (f32[560,128]{1,0:T(8,128)S(1)}, f32[560,128]{1,0:T(8,128)S(1)}, u32[]{:S(2)}, u32[]{:S(2)}) collective-permute-start(f32[560,128]{1,0:T(8,128)S(1)} %get-tuple-element.44), channel_id=1, source_target_pairs={{0,64},{32,96},{64,128},{96,160},{128,192},{160,224},{192,256},{22... | collective-permute-start | bytes 860168 | tf_op jit(solution)/shard_map/ppermute | solution.py:699
  25.9 5.3 %copy-start.1 = (s32[32]{0:T(128)S(1)}, s32[32]{0:T(128)}, u32[]{:S(2)}) copy-start(s32[32]{0:T(128)} %cells_ref.1) | copy-start | bytes 388
  25.9 5.3 %copy-start.2 = (f32[32]{0:T(128)S(1)}, f32[32]{0:T(128)}, u32[]{:S(2)}) copy-start(f32[32]{0:T(128)} %rate_ref.1) | copy-start | bytes 388
  25.9 8.3 %collective-permute-start.7 = (f32[448,128]{1,0:T(8,128)S(1)}, f32[448,128]{1,0:T(8,128)S(1)}, u32[]{:S(2)}, u32[]{:S(2)}) collective-permute-start(f32[448,128]{1,0:T(8,128)S(1)} %get-tuple-element.45), channel_id=1, source_target_pairs={{64,0},{96,32},{128,64},{160,96},{192,128},{224,160},{256,192},{28... | collective-permute-start | bytes 688136 | tf_op jit(solution)/shard_map/ppermute | solution.py:700
  27.2 7.9 %collective-permute-start.8 = (f32[448,128]{1,0:T(8,128)S(1)}, f32[448,128]{1,0:T(8,128)S(1)}, u32[]{:S(2)}, u32[]{:S(2)}) collective-permute-start(f32[448,128]{1,0:T(8,128)S(1)} %get-tuple-element.46), channel_id=1, source_target_pairs={{0,64},{32,96},{64,128},{96,160},{128,192},{160,224},{192,256},{22... | collective-permute-start | bytes 688136 | tf_op jit(solution)/shard_map/ppermute | solution.py:699
  35.2 15.5 %copy-start = (f32[64,1,8,128]{3,2,1,0:T(8,128)S(1)}, f32[64,1,8,128]{3,2,1,0:T(8,128)}, u32[]{:S(2)}) copy-start(f32[64,1,8,128]{3,2,1,0:T(8,128)} %param.7) | copy-start | bytes 786436
  39.4 12.1 %collective-permute-start.9 = (f32[592,128]{1,0:T(8,128)S(1)}, f32[592,128]{1,0:T(8,128)S(1)}, u32[]{:S(2)}, u32[]{:S(2)}) collective-permute-start(f32[592,128]{1,0:T(8,128)S(1)} %get-tuple-element.52), channel_id=1, source_target_pairs={{0,64},{32,96},{64,128},{96,160},{128,192},{160,224},{192,256},{22... | collective-permute-start | bytes 909320 | tf_op jit(solution)/shard_map/ppermute | solution.py:699
  43.5 8.0 %collective-permute-start.10 = (f32[592,128]{1,0:T(8,128)S(1)}, f32[592,128]{1,0:T(8,128)S(1)}, u32[]{:S(2)}, u32[]{:S(2)}) collective-permute-start(f32[592,128]{1,0:T(8,128)S(1)} %get-tuple-element.53), channel_id=1, source_target_pairs={{64,0},{96,32},{128,64},{160,96},{192,128},{224,160},{256,192},{28... | collective-permute-start | bytes 909320 | tf_op jit(solution)/shard_map/ppermute | solution.py:700
  44.8 5.9 %collective-permute-start.11 = (f32[512,128]{1,0:T(8,128)S(1)}, f32[512,128]{1,0:T(8,128)S(1)}, u32[]{:S(2)}, u32[]{:S(2)}) collective-permute-start(f32[512,128]{1,0:T(8,128)S(1)} %get-tuple-element.55), channel_id=1, source_target_pairs={{0,32},{32,0},{64,96},{96,64},{128,160},{160,128},{192,224},{224,1... | collective-permute-start | bytes 786440 | tf_op jit(solution)/shard_map/ppermute | solution.py:715
  53.9 6.6 %collective-permute-start.12 = (f32[512,128]{1,0:T(8,128)S(1)}, f32[512,128]{1,0:T(8,128)S(1)}, u32[]{:S(2)}, u32[]{:S(2)}) collective-permute-start(f32[512,128]{1,0:T(8,128)S(1)} %get-tuple-element.58), channel_id=1, source_target_pairs={{0,32},{32,0},{64,96},{96,64},{128,160},{160,128},{192,224},{224,1... | collective-permute-start | bytes 786440 | tf_op jit(solution)/shard_map/ppermute | solution.py:715
